TPU v7x, 128 devices: a whole 4x4x4 slice. The times are simulated.
128 devices in a mesh: frames: 32 (over z, y, core), points: 4 (over x).
Axes of the slice: x: 4, y: 4, z: 4, core: 2. Of those that a mesh axis runs over, the one named last changes fastest.
Arguments:
- obs_count: int32 [512], P(('frames', 'points')), may hold values from 128 to 2048, as said below
- obs_point: int32 [1048576], P(('frames', 'points')), may hold values from 0 to 1023
- obs_frame: int32 [1048576], P(('frames', 'points')), may hold values from 0 to 255
- jac_cam: float32 [2, 6, 1048576], P(None, None, ('frames', 'points')), may hold values from -4 to 4
- jac_point: float32 [2, 24, 1048576], P(None, None, ('frames', 'points')), may hold values from -1.25 to 1.25
- residual: float32 [2, 1048576], P(None, ('frames', 'points')), may hold values from -38 to 38
- point_inv: float32 [24, 24, 131072], P(None, None, ('frames', 'points')), may hold values from -1 to 2
- band: float32 [127, 6, 6, 8192], P(None, None, None, 'frames'), may hold values from -1 to 8, as said below
- edge_weight: float32 [8192], P('frames'), may hold values from 0.5 to 5
- precond: float32 [6, 6, 8192], P(None, None, 'frames'), may hold values from -1 to 1, as said below
Outputs:
- camera_step: float32 [6, 8192], P(None, 'frames')
- point_step: float32 [24, 131072], P(None, ('frames', 'points'))
Inputs may be any that keep to these rules, and one draw needn't show every extreme that they name: `obs_count`: multiples of 128; in one frame block, chosen anew for each draw, every device of that block uses all 2048 slots toward one same owner block; other counts vary. `band`: a symmetric positive definite matrix over all frames: the block at offset k of frame f is the transpose of the block at offset 127 - 1 - k of frame f + k - 63. `precond`: each frame's block is symmetric positive definite.
All inputs are finite; a program needn't handle non-finite values.
Results may differ from a plain program's by a relative error of at most 0.0001.
Values sent between devices are 32-bit elements; how exact they have to be, the bound alone decides.
No kernel may reach another device: no remote copies, remote signals or barrier semaphores. Data moves between devices by JAX's collectives and lax.ppermute only.
A program may use at most 128 MiB of HBM per device.

v0:
```python
import jax
import jax.numpy as jnp
from jax import lax
from jax.sharding import PartitionSpec as P

ITERS = 2


HIGHEST = lax.Precision.HIGHEST


def extended(block, sides, width):
    for axis, dim in sides:
        count = lax.axis_size(axis)
        forward = [(i, i + 1) for i in range(count - 1)]
        backward = [(target, source) for source, target in forward]
        low = lax.ppermute(
            lax.slice_in_dim(block, block.shape[dim] - width, None, axis=dim), axis, forward
        )
        high = lax.ppermute(lax.slice_in_dim(block, 0, width, axis=dim), axis, backward)
        block = jnp.concatenate([low, block, high], axis=dim)
    return block


def passed_along(value, axis, steps):
    count = lax.axis_size(axis)
    leading, last = (max(0, -steps), min(count, count - steps))
    return lax.ppermute(value, axis, [(source, source + steps) for source in range(leading, last)])


def precondition(precond, vector_in):
    return jnp.einsum("ijf,jf->if", precond, vector_in, precision=HIGHEST)


def project_points(jac_point, pairs, used_slot):
    return jnp.einsum("aqo,ao->qo", jac_point, pairs, precision=HIGHEST) * used_slot


def collect(values_in, point_ids, pt_rows):
    return jax.ops.segment_sum(values_in.T, point_ids, num_segments=pt_rows).T


def invert_points(point_inv, gradient):
    return jnp.einsum("ijp,jp->ip", point_inv, gradient, precision=HIGHEST)


def apply_operator(field_in, band, edge_here, edge_prev):
    reach_back = band.shape[0] // 2
    frames_here = field_in.shape[1]
    padded = extended(field_in, (("frames", 1),), reach_back)
    window_idx = jnp.arange(frames_here)[None, :] + jnp.arange(band.shape[0])[:, None]
    window = padded[:, window_idx]
    banded = jnp.einsum("kijf,jkf->if", band, window, precision=HIGHEST)
    before = padded[:, reach_back - 1 : reach_back - 1 + frames_here]
    after_frame = padded[:, reach_back + 1 : reach_back + 1 + frames_here]
    return banded + edge_prev * (field_in - before) + edge_here * (field_in - after_frame)


def precond_inner(remainder, scaled):
    return lax.psum(jnp.sum(remainder * scaled), "frames")


def local(
    obs_count,
    obs_point,
    obs_frame,
    jac_cam,
    jac_point,
    residual,
    point_inv,
    band,
    edge_weight,
    precond,
):
    groups = lax.axis_size("points")
    slot_count = obs_point.shape[0]
    slot_width = slot_count // groups
    pt_rows = point_inv.shape[2]
    frames_here = band.shape[3]
    coeffs = jac_point.shape[1]
    slot_order = jnp.arange(slot_count, dtype=jnp.int32)
    limits = jnp.repeat(obs_count, slot_width, total_repeat_length=slot_count)
    used_slot = (slot_order % slot_width < limits).astype(jnp.float32)
    grad_terms = project_points(jac_point, residual, used_slot)
    slot_ids = obs_point.astype(jnp.float32).reshape(1, groups, slot_width)
    got_terms, got_ids = (
        lax.all_to_all(
            grad_terms.reshape(coeffs, groups, slot_width),
            "points",
            split_axis=1,
            concat_axis=1,
            tiled=True,
        ),
        lax.all_to_all(slot_ids, "points", split_axis=1, concat_axis=1, tiled=True),
    )
    arrived = got_ids.reshape(-1).astype(jnp.int32)
    point_grad = collect(got_terms.reshape(coeffs, -1), arrived, pt_rows)
    point_solved = invert_points(point_inv, point_grad)
    outgoing = jnp.take(point_solved, arrived, axis=1).reshape(coeffs, groups, slot_width)
    seen_values = lax.all_to_all(
        outgoing, "points", split_axis=1, concat_axis=1, tiled=True
    ).reshape(coeffs, slot_count)
    remain = residual - jnp.einsum("aqo,qo->ao", jac_point, seen_values, precision=HIGHEST)
    cam_terms = jnp.einsum("aco,ao->co", jac_cam, remain, precision=HIGHEST) * used_slot
    local_rhs = jax.ops.segment_sum(cam_terms.T, obs_frame, num_segments=frames_here).T
    rhs = lax.psum(local_rhs, "points")
    index_here = lax.axis_index("frames") * frames_here + jnp.arange(frames_here, dtype=jnp.int32)
    last_frame = frames_here * lax.axis_size("frames") - 1
    edge_here = edge_weight * (index_here < last_frame).astype(jnp.float32)
    carried = passed_along(edge_here[-1:], "frames", 1)
    edge_prev = jnp.concatenate([carried, edge_here[:-1]])
    camera_step = jnp.zeros_like(rhs)
    remainder = rhs
    scaled = precondition(precond, remainder)
    direction = scaled
    inner_now = precond_inner(remainder, scaled)
    for step_index in range(ITERS):
        image_now = apply_operator(direction, band, edge_here, edge_prev)
        step_size = inner_now / lax.psum(jnp.sum(direction * image_now), "frames")
        camera_step = camera_step + step_size * direction
        remainder = remainder - step_size * image_now
        if step_index + 1 < ITERS:
            scaled = precondition(precond, remainder)
            inner_next = precond_inner(remainder, scaled)
            direction = scaled + inner_next / inner_now * direction
            inner_now = inner_next
    frame_values = jnp.take(camera_step, obs_frame, axis=1)
    shifted_res = residual - jnp.einsum("aco,co->ao", jac_cam, frame_values, precision=HIGHEST)
    new_terms = project_points(jac_point, shifted_res, used_slot)
    got_update = lax.all_to_all(
        new_terms.reshape(coeffs, groups, slot_width),
        "points",
        split_axis=1,
        concat_axis=1,
        tiled=True,
    )
    update_grad = collect(got_update.reshape(coeffs, -1), arrived, pt_rows)
    point_step = invert_points(point_inv, update_grad)
    return (camera_step, point_step)


def solution(mesh):
    placed = (
        P(("frames", "points")),
        P(("frames", "points")),
        P(("frames", "points")),
        P(None, None, ("frames", "points")),
        P(None, None, ("frames", "points")),
        P(None, ("frames", "points")),
        P(None, None, ("frames", "points")),
        P(None, None, None, "frames"),
        P("frames"),
        P(None, None, "frames"),
    )
    return jax.shard_map(
        local,
        mesh=mesh,
        in_specs=placed,
        out_specs=(P(None, "frames"), P(None, ("frames", "points"))),
        check_vma=False,
    )
```

profile of v0, /device:TPU:1, one launch (start us, length us, event | category | flops | bytes accessed | tf_op | source)
XLA Modules:
  0.0 665.2 jit_solution(18102906167156909086)
XLA Ops:
  2.2 4.8 all-to-all-start
  10.1 3.3 fusion.13
  14.4 7.3 %copy.116 = f32[24,24,1024]{0,1,2:T(8,128)} copy(f32[24,24,1024]{2,1,0:T(8,128)S(1)} %copy-done.1) | data formatting | bytes 4718592 | tf_op args[6]
  21.7 4.2 all-to-all-start.1
  26.1 10.7 %all-to-all-done.1 = f32[24,4,2048]{2,0,1:T(8,128)S(1)} async-done(((f32[24,4,2048]{2,0,1:T(8,128)}), f32[24,4,2048]{2,0,1:T(8,128)S(1)}, u32[]{:S(2)}, u32[]{:S(2)}) %all-to-all-start.1) | async-done | bytes 786464 | tf_op jit(solution)/shard_map/all_to_all | solution.py:87
  36.9 2.6 copy.99
  39.5 44.4 %scatter_custom_fusion = f32[1024,24]{1,0:T(8,128)S(1)} fusion(s32[8192]{0:T(1024)S(1)} %bitcast.139, f32[8192,24]{1,0:T(8,128)} %copy.99, f32[]{:T(128)} %constant.148.clone.1), kind=kCustom, calls=%fused_computation.27 | custom fusion | flops 196608 | bytes 98816 | tf_op jit(solution)/shard_map/scatter-add | solution.py:40
  84.0 14.3 %fusion.36 = f32[1024,1,24]{2,1,0:T(1,128)S(1)} fusion(f32[24,1024,1]{0,2,1:T(1,128)S(1)} %bitcast.133, f32[24,24,1024]{0,1,2:T(8,128)} %copy.116), kind=kOutput, calls=%fused_computation.84 | convolution fusion | flops 7077888 | bytes 2555904 | tf_op jit(solution)/shard_map/ijp,jp->ip/dot_general | solution.py:44
  98.3 27.7 %gather_fusion = f32[8192,24]{1,0:T(8,128)} fusion(f32[24,1024]{0,1:T(8,128)S(1)} %bitcast.120, s32[8192]{0:T(1024)S(1)} %broadcast_clamp_fusion), kind=kCustom, calls=%fused_computation | custom fusion | bytes 1605632 | tf_op jit(solution)/shard_map/jit(_take)/gather | solution.py:99
  126.0 2.9 copy.100
  129.9 3.5 all-to-all-start.2
  134.0 5.6 collective-permute-start.2
  139.7 3.4 all-to-all-done.2
  144.1 2.6 copy.130
  146.7 48.6 %scatter_custom_fusion.1 = f32[256,6]{1,0:T(8,128)S(1)} fusion(s32[8192]{0:T(1024)S(1)} %copy-done.6, f32[8192,6]{1,0:T(8,128)} %copy.130, f32[8192]{0:T(1024)S(1)} %fusion.13, f32[]{:T(128)} %constant.148.clone.1), kind=kCustom, calls=%fused_computation.9 | custom fusion | flops 98304 | bytes 235524 | tf_op jit(solution)/shard_map/scatter-add | solution.py:105
  195.4 7.0 %psum.35 = f32[6,256]{1,0:T(8,128)S(1)} all-reduce(f32[6,256]{1,0:T(8,128)S(1)} %bitcast.144), channel_id=1, replica_groups=mesh['frames'=32,'points'=4] {'points'}, use_global_device_ids=true, to_apply=%region_2.3 | all-reduce | flops 1536 | bytes 12288 | tf_op jit(solution)/shard_map/psum | solution.py:106
  202.5 8.6 %collective-permute-start = (f32[6,63]{1,0:T(8,128)S(1)}, f32[6,63]{1,0:T(8,128)S(1)}, u32[]{:S(2)}, u32[]{:S(2)}) collective-permute-start(f32[6,63]{1,0:T(8,128)S(1)} %get-tuple-element.31), channel_id=1, source_target_pairs={{0,4},{4,8},{8,12},{12,16},{16,20},{20,24},{24,28},{28,32},{32,36}... | collective-permute-start | bytes 4544 | tf_op jit(solution)/shard_map/ppermute | solution.py:17
  216.2 60.2 %gather_fusion.1 = f32[32512,6]{1,0:T(8,128)} fusion(f32[6,382]{0,1:T(8,128)S(1)} %copy.103, s32[32768]{0:T(1024)S(1)} %pad_clamp_fusion), kind=kCustom, calls=%fused_computation.1 | custom fusion | bytes 1690624 | tf_op jit(solution)/shard_map/gather | solution.py:52
  276.4 10.0 %copy.181 = f32[256,6,127]{0,2,1:T(8,128)S(1)} copy(f32[256,6,127]{1,0,2:T(8,128)} %bitcast.122) | data formatting | bytes 1560576
  286.5 2.8 multiply_reduce_fusion.1
  289.9 63.1 %all-reduce = (f32[]{:T(128)}, f32[]{:T(128)}) all-reduce(f32[]{:T(128)} %get-tuple-element.25, f32[]{:T(128)} %get-tuple-element.24), channel_id=1, replica_groups=mesh['frames'=32,'points'=4] {'frames'}, use_global_device_ids=true, to_apply=%region_4.5 | all-reduce | flops 2 | bytes 16 | tf_op jit(solution)/shard_map/psum | solution.py:60
  355.0 66.1 %psum.38 = f32[]{:T(128)} all-reduce(f32[]{:T(128)} %fusion.30), channel_id=1, replica_groups=mesh['frames'=32,'points'=4] {'frames'}, use_global_device_ids=true, to_apply=%region_8.9 | all-reduce | flops 1 | bytes 8 | tf_op jit(solution)/shard_map/psum | solution.py:60
  429.5 60.2 %gather_fusion.2 = f32[32512,6]{1,0:T(8,128)} fusion(f32[6,382]{0,1:T(8,128)S(1)} %copy.104, s32[32768]{0:T(1024)S(1)} %pad_clamp_fusion), kind=kCustom, calls=%fused_computation.2 | custom fusion | bytes 1690624 | tf_op jit(solution)/shard_map/gather | solution.py:52
  489.7 10.0 %copy.183 = f32[256,6,127]{0,2,1:T(8,128)S(1)} copy(f32[256,6,127]{1,0,2:T(8,128)} %bitcast.121) | data formatting | bytes 1560576
  499.8 2.8 multiply_reduce_fusion
  503.2 61.3 %psum.39 = f32[]{:T(128)} all-reduce(f32[]{:T(128)} %fusion.20), channel_id=1, replica_groups=mesh['frames'=32,'points'=4] {'frames'}, use_global_device_ids=true, to_apply=%region_10.11 | all-reduce | flops 1 | bytes 8 | tf_op jit(solution)/shard_map/psum | solution.py:119
  566.0 27.7 %gather_fusion.3 = f32[8192,6]{1,0:T(8,128)} fusion(f32[6,256]{0,1:T(8,128)S(1)} %copy.105, s32[8192]{0:T(1024)S(1)} %fusion.15), kind=kCustom, calls=%fused_computation.3 | custom fusion | bytes 425984 | tf_op jit(solution)/shard_map/jit(_take)/gather | solution.py:127
  593.7 7.5 %broadcast_select_fusion = f32[8192,6]{1,0:T(8,128)} fusion(f32[8192,6]{1,0:T(8,128)} %gather_fusion.3, pred[8192]{0:T(1024)(128)(4,1)S(1)} %compare_and_fusion), kind=kLoop, calls=%fused_computation.12 | loop fusion | flops 49152 | bytes 401408 | tf_op jit(solution)/shard_map/jit(_take)/select_n | solution.py:127
  601.2 2.8 copy.184
  604.6 12.3 %all_to_all.20 = f32[24,4,2048]{2,0,1:T(8,128)S(1)} all-to-all(f32[24,4,2048]{2,0,1:T(8,128)S(1)} %bitcast.130), channel_id=1, replica_groups=mesh['frames'=32,'points'=4] {'points'}, dimensions={1} | all-to-all | bytes 1572864 | tf_op jit(solution)/shard_map/all_to_all | solution.py:130
  616.9 2.6 copy.108
  619.6 44.4 %scatter_custom_fusion.2 = f32[1024,24]{1,0:T(8,128)S(1)} fusion(s32[8192]{0:T(1024)S(1)} %bitcast.140, f32[8192,24]{1,0:T(8,128)} %copy.108, f32[]{:T(128)} %constant.148.clone.1), kind=kCustom, calls=%fused_computation.25 | custom fusion | flops 196608 | bytes 98816 | tf_op jit(solution)/shard_map/scatter-add | solution.py:40
  (74 shorter events, 24.8 us)
Async XLA Ops:
  0.6 13.8 %copy-start.1 = (f32[24,24,1024]{2,1,0:T(8,128)S(1)}, f32[24,24,1024]{2,1,0:T(8,128)}, u32[]{:S(2)}) copy-start(f32[24,24,1024]{2,1,0:T(8,128)} %param.18) | copy-start | bytes 7077892
  2.2 19.6 %all-to-all-start = ((f32[1,4,2048]{2,0,1:T(1,128)}), f32[1,4,2048]{2,0,1:T(1,128)S(1)}, u32[]{:S(2)}, u32[]{:S(2)}) async-start(f32[1,4,2048]{2,0,1:T(1,128)} %bitcast.20), calls=%async_computation | async-start | bytes 65536 | tf_op jit(solution)/shard_map/all_to_all | solution.py:94
  21.7 15.1 %all-to-all-start.1 = ((f32[24,4,2048]{2,0,1:T(8,128)}), f32[24,4,2048]{2,0,1:T(8,128)S(1)}, u32[]{:S(2)}, u32[]{:S(2)}) async-start(f32[24,4,2048]{2,0,1:T(8,128)} %bitcast.118), calls=%async_computation.1 | async-start | bytes 1572864 | tf_op jit(solution)/shard_map/all_to_all | solution.py:87
  126.0 7.4 %copy-start.8 = (f32[256]{0:T(256)S(1)}, f32[256]{0:T(256)}, u32[]{:S(2)}) copy-start(f32[256]{0:T(256)} %param.20) | copy-start | bytes 3076
  126.0 17.2 %copy-start = (f32[2,24,8192]{2,1,0:T(8,128)S(1)}, f32[2,24,8192]{2,1,0:T(8,128)}, u32[]{:S(2)}) copy-start(f32[2,24,8192]{2,1,0:T(8,128)} %param.16) | copy-start | bytes 4718596
  128.9 14.6 %copy-start.4 = (f32[2,8192]{1,0:T(2,128)S(1)}, f32[2,8192]{1,0:T(2,128)}, u32[]{:S(2)}) copy-start(f32[2,8192]{1,0:T(2,128)} %param.17) | copy-start | bytes 196612
  128.9 14.6 %copy-start.3 = (f32[2,6,8192]{2,0,1:T(2,128)S(1)}, f32[2,6,8192]{2,0,1:T(2,128)}, u32[]{:S(2)}) copy-start(f32[2,6,8192]{2,0,1:T(2,128)} %param.15) | copy-start | bytes 1179652
  129.9 13.2 %all-to-all-start.2 = ((f32[24,4,2048]{2,0,1:T(8,128)}), f32[24,4,2048]{2,0,1:T(8,128)S(1)}, u32[]{:S(2)}, u32[]{:S(2)}) async-start(f32[24,4,2048]{2,0,1:T(8,128)} %broadcast_select_fusion.1), calls=%async_computation.2 | async-start | bytes 1572864 | tf_op jit(solution)/shard_map/all_to_all | solution.py:100
  134.0 79.0 %collective-permute-start.2 = (f32[1]{0:T(128)}, f32[1]{0:T(128)}, u32[]{:S(2)}, u32[]{:S(2)}) collective-permute-start(f32[1]{0:T(128)} %slice.52), channel_id=1, source_target_pairs={{0,4},{4,8},{8,12},{12,16},{16,20},{20,24},{24,28},{28,32},{32,36}... | collective-permute-start | bytes 20 | tf_op jit(solution)/shard_map/ppermute | solution.py:28
  143.1 3.6 copy-start.6
  144.1 58.3 %copy-start.5 = (f32[6,6,256]{2,1,0:T(8,128)S(1)}, f32[6,6,256]{2,1,0:T(8,128)}, u32[]{:S(2)}) copy-start(f32[6,6,256]{2,1,0:T(8,128)} %param.21) | copy-start | bytes 110596
  202.5 11.3 %collective-permute-start = (f32[6,63]{1,0:T(8,128)S(1)}, f32[6,63]{1,0:T(8,128)S(1)}, u32[]{:S(2)}, u32[]{:S(2)}) collective-permute-start(f32[6,63]{1,0:T(8,128)S(1)} %get-tuple-element.31), channel_id=1, source_target_pairs={{0,4},{4,8},{8,12},{12,16},{16,20},{20,24},{24,28},{28,32},{32,36}... | collective-permute-start | bytes 4544 | tf_op jit(solution)/shard_map/ppermute | solution.py:17
  211.1 4.9 collective-permute-start.1
  422.5 4.3 collective-permute-start.3
  424.4 4.9 collective-permute-start.4
  565.9 35.3 %copy-start.7 = (f32[6,256]{1,0:T(8,128)}, f32[6,256]{1,0:T(8,128)S(1)}, u32[]{:S(2)}) copy-start(f32[6,256]{1,0:T(8,128)S(1)} %multiply_add_fusion) | copy-start | bytes 18436
  616.9 47.3 %copy-start.2 = (f32[24,24,1024]{2,1,0:T(8,128)S(1)}, f32[24,24,1024]{2,1,0:T(8,128)}, u32[]{:S(2)}) copy-start(f32[24,24,1024]{2,1,0:T(8,128)} %param.18) | copy-start | bytes 7077892
where the time goes:
time: 668 us; the launch traced here: 665 us
  local copies, waits for them, and re-layouts  221 us (33%)
  blocking collectives  210 us (31%)
  other arithmetic  163 us (24%)
  starting transfers between devices  33.1 us (5%)
  waiting for transfers between devices  18.9 us (3%)
  matrix products  14.3 us (2%)
    psum x2, blocking collectives, precond_inner(): return lax.psum(jnp.sum(remainder * scaled), 'frames')  129 us
    gather x2, local copies, waits for them, and re-layouts, apply_operator(): window = padded[:, window_idx]  120 us
    scatter-add x2, other arithmetic, collect(): return jax.ops.segment_sum(values_in.T, point_ids, num_segments=pt_rows).T  88.9 us
    psum x1, blocking collectives, local(): step_size = inner_now / lax.psum(jnp.sum(direction * image_now), 'frames')  61.3 us
    scatter-add x1, other arithmetic, local(): jax.ops.segment_sum(cam_terms.T, obs_frame, num_segments=frames_here)  48.6 us
    gather x2, local copies, waits for them, and re-layouts, local(): jnp.take(point_solved, arrived, axis=1).reshape(coeffs, groups, slot_width)  30.6 us
    unnamed x23, local copies, waits for them, and re-layouts  30.5 us
    gather x1, local copies, waits for them, and re-layouts, local(): frame_values = jnp.take(camera_step, obs_frame, axis=1)  27.7 us
  transfers between devices with their start and end apart: 8, of which 4 were waited for; matrix products, arithmetic and copies ran while one was open for 10% of the time, Pallas kernels for 0%

commit v1 on v0

v1 whole, which is shorter than its diff:
```python
import functools

import jax
import jax.numpy as jnp
from jax import lax
from jax.experimental import pallas as pl
from jax.experimental.pallas import tpu as pltpu
from jax.sharding import PartitionSpec as P

F32 = jnp.float32
BF16 = jnp.bfloat16
CP = 6
Q = 24
BANDW = 127
REACH = 63
FR = 256
PT = 1024
CAP = 2048
GROUPS = 4
LO = 256
HI = PT // LO


def halves(x):
    lead = x.astype(BF16).astype(F32)
    return jnp.concatenate([lead, x - lead], axis=0).astype(BF16)


def one_hot(row, rows):
    n = row.shape[1]
    index = lax.broadcasted_iota(jnp.int32, (rows, 128), 0).astype(F32).astype(BF16)
    row = row.astype(BF16)
    cols = []
    for c in range(n // 128):
        here = jnp.broadcast_to(row[:, c * 128 : (c + 1) * 128], (rows, 128))
        cols.append(jnp.where(index == here, jnp.ones_like(index), jnp.zeros_like(index)))
    return jnp.concatenate(cols, axis=1)


def split_ids(ids):
    hi = lax.shift_right_logical(ids, 8)
    lo = lax.bitwise_and(ids, LO - 1)
    return hi.astype(F32), lo.astype(F32)


def used_row(count):
    lane = lax.broadcasted_iota(jnp.int32, (1, CAP), 1)
    return (lane < count).astype(F32)


def scatter_points(terms, ids):
    n = terms.shape[0]
    hi, lo = split_ids(ids)
    parts = halves(terms)
    table = one_hot(lo, LO)
    rows = []
    for h in range(HI):
        mask = jnp.broadcast_to((hi == h).astype(F32), (2 * n, CAP)).astype(BF16)
        rows.append(parts * mask)
    sums = lax.dot_general(
        jnp.concatenate(rows, axis=0), table, (((1,), (1,)), ((), ())), preferred_element_type=F32
    )
    out = []
    for h in range(HI):
        block = sums[h * 2 * n : (h + 1) * 2 * n]
        out.append(block[:n] + block[n:])
    return jnp.concatenate(out, axis=1)


def gather_points(values, ids):
    n = values.shape[0]
    hi, lo = split_ids(ids)
    parts = halves(values)
    table = one_hot(lo, LO)
    stacked = jnp.concatenate([parts[:, h * LO : (h + 1) * LO] for h in range(HI)], axis=0)
    got = lax.dot_general(stacked, table, (((1,), (0,)), ((), ())), preferred_element_type=F32)
    total = None
    for h in range(HI):
        block = got[h * 2 * n : (h + 1) * 2 * n]
        term = (block[:n] + block[n:]) * (hi == h).astype(F32)
        total = term if total is None else total + term
    return total


def grad_kernel(me_ref, count_ref, ids_ref, res_ref, jp_ref, *outs):
    k = pl.program_id(0)
    b = lax.rem(me_ref[0] + GROUPS - 1 - k, GROUPS)
    used = used_row(count_ref[b])
    res = res_ref[...] * used
    terms = jp_ref[0] * res[0:1] + jp_ref[1] * res[1:2]
    sums = scatter_points(terms, ids_ref[...])
    for j in range(GROUPS):

        @pl.when(k == j)
        def _():
            outs[j][...] = sums


def solve_kernel(a_ref, b_ref, c_ref, d_ref, inv_ref, out_ref):
    grad = a_ref[...] + b_ref[...] + c_ref[...] + d_ref[...]
    out_ref[...] = jnp.sum(inv_ref[...] * grad[None], axis=1)


def rhs_kernel(me_ref, count_ref, pid_ref, fid_ref, res_ref, jp_ref, jc_ref, *rest):
    solved, out_ref, chosen = rest[:GROUPS], rest[GROUPS], rest[GROUPS + 1]
    k = pl.program_id(0)
    b = lax.rem(me_ref[0] + GROUPS - k, GROUPS)
    for j in range(GROUPS):

        @pl.when(k == j)
        def _():
            chosen[...] = solved[j][...]

    used = used_row(count_ref[b])
    seen = gather_points(chosen[...], pid_ref[...])
    remain = [
        (res_ref[a : a + 1, :] - jnp.sum(jp_ref[a] * seen, axis=0, keepdims=True)) * used
        for a in range(2)
    ]
    cam = jc_ref[0] * remain[0] + jc_ref[1] * remain[1]
    cam = jnp.concatenate([cam, jnp.zeros((2, CAP), F32)], axis=0)
    table = one_hot(fid_ref[...].astype(F32), FR)
    sums = lax.dot_general(
        halves(cam), table, (((1,), (1,)), ((), ())), preferred_element_type=F32
    )
    sums = sums[0:CP] + sums[8 : 8 + CP]

    @pl.when(k == 0)
    def _():
        out_ref[...] = sums

    @pl.when(k > 0)
    def _():
        out_ref[...] += sums


def apply_precond(pre_ref, vec):
    return jnp.sum(pre_ref[...] * vec[None], axis=1)


def start_kernel(a_ref, b_ref, c_ref, d_ref, pre_ref, r_ref, z_ref):
    rhs = a_ref[...] + b_ref[...] + c_ref[...] + d_ref[...]
    r_ref[...] = rhs
    z_ref[...] = apply_precond(pre_ref, rhs)


def operator(last_ref, own_ref, left_ref, right_ref, band_ref, edge_ref, edge_left_ref):
    own = own_ref[...]
    padded = jnp.concatenate([left_ref[...], own, right_ref[...]], axis=1)
    totals = [jnp.zeros((CP, FR), F32) for _ in range(CP)]
    for k in range(BANDW):
        at = FR - REACH + k
        shifted = padded[:, at : at + FR]
        for i in range(CP):
            totals[i] = totals[i] + band_ref[k, i] * shifted
    banded = jnp.concatenate([jnp.sum(t, axis=0, keepdims=True) for t in totals], axis=0)
    lane = lax.broadcasted_iota(jnp.int32, (1, FR), 1)
    here = jnp.where((lane == FR - 1) & (last_ref[0] == 1), 0.0, edge_ref[...])
    prev = jnp.concatenate([edge_left_ref[...], here], axis=1)[:, FR - 1 : 2 * FR - 1]
    before = padded[:, FR - 1 : 2 * FR - 1]
    after = padded[:, FR + 1 : 2 * FR + 1]
    return banded + prev * (own - before) + here * (own - after)


def first_kernel(last_ref, z_ref, zl_ref, zr_ref, band_ref, e_ref, el_ref, pre_ref, w_ref, u_ref):
    image = operator(last_ref, z_ref, zl_ref, zr_ref, band_ref, e_ref, el_ref)
    w_ref[...] = image
    u_ref[...] = apply_precond(pre_ref, image)


def second_kernel(
    last_ref, u_ref, ul_ref, ur_ref, band_ref, e_ref, el_ref, r_ref, z_ref, w_ref, out_ref
):
    y = operator(last_ref, u_ref, ul_ref, ur_ref, band_ref, e_ref, el_ref)
    r, z, w, u = r_ref[...], z_ref[...], w_ref[...], u_ref[...]
    lane = lax.broadcasted_iota(jnp.int32, (1, 128), 1)
    row = jnp.zeros((1, 128), F32)
    for at, (one, two) in enumerate(((r, z), (z, w), (r, u), (w, u), (z, y), (u, y))):
        total = jnp.sum(jnp.sum(one * two, axis=0, keepdims=True), axis=1, keepdims=True)
        row = row + jnp.where(lane == at, total, 0.0)
    out_ref[...] = jnp.broadcast_to(row, out_ref.shape)


def back_kernel(me_ref, count_ref, pid_ref, fid_ref, jp_ref, jc_ref, z_ref, u_ref, *outs):
    k = pl.program_id(0)
    b = lax.rem(me_ref[0] + GROUPS - 1 - k, GROUPS)
    used = used_row(count_ref[b])
    zero = jnp.zeros((2, FR), F32)
    stacked = jnp.concatenate([z_ref[...], zero, u_ref[...], zero], axis=0)
    table = one_hot(fid_ref[...].astype(F32), FR)
    got = lax.dot_general(
        halves(stacked), table, (((1,), (0,)), ((), ())), preferred_element_type=F32
    )
    got = got[:16] + got[16:]
    terms = []
    for v in range(2):
        seen = got[v * 8 : v * 8 + CP]
        pair = [jnp.sum(jc_ref[a] * seen, axis=0, keepdims=True) * used for a in range(2)]
        terms.append(jp_ref[0] * pair[0] + jp_ref[1] * pair[1])
    sums = scatter_points(jnp.concatenate(terms, axis=0), pid_ref[...])
    for j in range(GROUPS):

        @pl.when(k == j)
        def _():
            outs[j][...] = sums


def final_kernel(g_ref, z_ref, u_ref, ps_ref, a_ref, b_ref, c_ref, d_ref, inv_ref, cam_ref, pt_ref):
    row = jnp.sum(g_ref[...], axis=0, keepdims=True)
    rz, zw, ru, wu, zy, uy = [row[:, i : i + 1] for i in range(6)]
    a0 = rz / zw
    inner = rz - a0 * (ru + zw) + a0 * a0 * wu
    beta = 1.0 + inner / rz
    curve = beta * beta * zw - beta * a0 * (zy + wu) + a0 * a0 * uy
    a1 = inner / curve
    c0 = a0 + a1 * beta
    c1 = -a1 * a0
    cam_ref[...] = c0 * z_ref[...] + c1 * u_ref[...]
    both = a_ref[...] + b_ref[...] + c_ref[...] + d_ref[...]
    grad = c0 * both[:Q] + c1 * both[Q:]
    pt_ref[...] = ps_ref[...] - jnp.sum(inv_ref[...] * grad[None], axis=1)


def shifted(value, axis, step):
    count = lax.axis_size(axis)
    return lax.ppermute(value, axis, [(i, (i + step) % count) for i in range(count)])


def beside(value):
    count = lax.axis_size("frames")
    up = [(i, i + 1) for i in range(count - 1)]
    down = [(i + 1, i) for i in range(count - 1)]
    return lax.ppermute(value, "frames", up), lax.ppermute(value, "frames", down)


def sds(*shape):
    return jax.ShapeDtypeStruct(shape, F32)


def cost(flops, moved):
    return pl.CostEstimate(flops=flops, bytes_accessed=moved, transcendentals=0)


def blocked(kernel, args, specs, outs, out_specs, name, scratch=(), est=None):
    def call(me, count):
        return pl.pallas_call(
            kernel,
            grid_spec=pltpu.PrefetchScalarGridSpec(
                num_scalar_prefetch=2,
                grid=(GROUPS,),
                in_specs=specs,
                out_specs=out_specs,
                scratch_shapes=list(scratch),
            ),
            out_shape=outs,
            cost_estimate=est,
            name=name,
        )(me, count, *args)

    return call


def lanes_spec(shape, turn):
    lead = shape[:-1]

    def index(k, me, count):
        return (0,) * len(lead) + (lax.rem(me[0] + GROUPS + turn(k), GROUPS),)

    return pl.BlockSpec(lead + (CAP,), index)


def whole_spec(shape):
    return pl.BlockSpec(shape, lambda k, me, count: (0,) * len(shape))


def plain(kernel, outs, smem, args, name, est=None):
    specs = [
        pl.BlockSpec(memory_space=pltpu.SMEM if i in smem else pltpu.VMEM) for i in range(len(args))
    ]
    out_specs = jax.tree.map(lambda _: pl.BlockSpec(memory_space=pltpu.VMEM), outs)
    return pl.pallas_call(
        kernel, in_specs=specs, out_specs=out_specs, out_shape=outs, cost_estimate=est, name=name
    )(*args)


def local(
    obs_count,
    obs_point,
    obs_frame,
    jac_cam,
    jac_point,
    residual,
    point_inv,
    band,
    edge_weight,
    precond,
):
    slots = obs_point.shape[0]
    pid = obs_point.reshape(1, slots)
    fid = obs_frame.reshape(1, slots)
    me = lax.axis_index("points").astype(jnp.int32).reshape(1)
    count = lax.axis_size("frames")
    last = (lax.axis_index("frames") == count - 1).astype(jnp.int32).reshape(1)
    edge = edge_weight.reshape(1, FR)
    edge_left = lax.ppermute(edge, "frames", [(i, i + 1) for i in range(count - 1)])

    ahead = lambda k: GROUPS - 1 - k
    behind = lambda k: -k

    sums = blocked(
        grad_kernel,
        (pid, residual, jac_point),
        [lanes_spec((1, slots), ahead), lanes_spec((2, slots), ahead), lanes_spec((2, Q, slots), ahead)],
        [sds(Q, PT)] * GROUPS,
        [whole_spec((Q, PT))] * GROUPS,
        "point_grad",
        est=cost(2 * 192 * 256 * 8192, 2 * 24 * 8192 * 4),
    )(me, obs_count)
    got = [shifted(sums[GROUPS - 1 - s], "points", s) for s in (3, 2, 1)] + [sums[GROUPS - 1]]

    inv_spec = [pl.BlockSpec((Q, 256), lambda k: (0, k))] * GROUPS + [
        pl.BlockSpec((Q, Q, 256), lambda k: (0, 0, k))
    ]
    solved = pl.pallas_call(
        solve_kernel,
        grid=(PT // 256,),
        in_specs=inv_spec,
        out_specs=pl.BlockSpec((Q, 256), lambda k: (0, k)),
        out_shape=sds(Q, PT),
        cost_estimate=cost(2 * Q * Q * PT, Q * Q * PT * 4),
        name="point_solve",
    )(*got, point_inv)
    all_solved = [solved] + [shifted(solved, "points", s) for s in (1, 2, 3)]

    partial = blocked(
        rhs_kernel,
        (pid, fid, residual, jac_point, jac_cam, *all_solved),
        [
            lanes_spec((1, slots), behind),
            lanes_spec((1, slots), behind),
            lanes_spec((2, slots), behind),
            lanes_spec((2, Q, slots), behind),
            lanes_spec((2, CP, slots), behind),
        ]
        + [whole_spec((Q, PT))] * GROUPS,
        sds(CP, FR),
        whole_spec((CP, FR)),
        "camera_rhs",
        scratch=[pltpu.VMEM((Q, PT), F32)],
        est=cost(2 * 256 * 256 * 8192, 2 * 32 * 8192 * 4),
    )(me, obs_count)
    parts = [partial] + [shifted(partial, "points", s) for s in (1, 2, 3)]

    rhs, z = plain(
        start_kernel, [sds(CP, FR)] * 2, (), (*parts, precond), "start", est=cost(20000, 100000)
    )
    z_left, z_right = beside(z)
    w, u = plain(
        first_kernel,
        [sds(CP, FR)] * 2,
        (0,),
        (last, z, z_left, z_right, band, edge, edge_left, precond),
        "operator_one",
        est=cost(2 * 127 * 36 * 256, 127 * 48 * 256 * 4),
    )
    u_left, u_right = beside(u)
    back = blocked(
        back_kernel,
        (pid, fid, jac_point, jac_cam, z, u),
        [
            lanes_spec((1, slots), ahead),
            lanes_spec((1, slots), ahead),
            lanes_spec((2, Q, slots), ahead),
            lanes_spec((2, CP, slots), ahead),
            whole_spec((CP, FR)),
            whole_spec((CP, FR)),
        ],
        [sds(2 * Q, PT)] * GROUPS,
        [whole_spec((2 * Q, PT))] * GROUPS,
        "back_terms",
        est=cost(2 * 400 * 256 * 8192, 2 * 32 * 8192 * 4),
    )(me, obs_count)
    returned = [shifted(back[GROUPS - 1 - s], "points", s) for s in (3, 2, 1)] + [back[GROUPS - 1]]
    gram = plain(
        second_kernel,
        sds(count, 128),
        (0,),
        (last, u, u_left, u_right, band, edge, edge_left, rhs, z, w),
        "operator_two",
        est=cost(2 * 127 * 36 * 256, 127 * 48 * 256 * 4),
    )
    gram = lax.all_to_all(gram, "frames", split_axis=0, concat_axis=0, tiled=True)

    whole = lambda shape: pl.BlockSpec(shape, lambda k: (0,) * len(shape))
    camera_step, point_step = pl.pallas_call(
        final_kernel,
        grid=(PT // 256,),
        in_specs=[
            whole((count, 128)),
            whole((CP, FR)),
            whole((CP, FR)),
            pl.BlockSpec((Q, 256), lambda k: (0, k)),
        ]
        + [pl.BlockSpec((2 * Q, 256), lambda k: (0, k))] * GROUPS
        + [pl.BlockSpec((Q, Q, 256), lambda k: (0, 0, k))],
        out_specs=[whole((CP, FR)), pl.BlockSpec((Q, 256), lambda k: (0, k))],
        out_shape=[sds(CP, FR), sds(Q, PT)],
        cost_estimate=cost(2 * Q * Q * PT, Q * Q * PT * 4),
        name="final",
    )(gram, z, u, solved, *returned, point_inv)
    return camera_step, point_step


def solution(mesh):
    placed = (
        P(("frames", "points")),
        P(("frames", "points")),
        P(("frames", "points")),
        P(None, None, ("frames", "points")),
        P(None, None, ("frames", "points")),
        P(None, ("frames", "points")),
        P(None, None, ("frames", "points")),
        P(None, None, None, "frames"),
        P("frames"),
        P(None, None, "frames"),
    )
    return jax.shard_map(
        local,
        mesh=mesh,
        in_specs=placed,
        out_specs=(P(None, "frames"), P(None, ("frames", "points"))),
        check_vma=False,
    )
```

time: 668 us -> 110 us (0.16)
  local copies, waits for them, and re-layouts: 221 us -> 13.3 us
  blocking collectives: 210 us -> 17.7 us
  other arithmetic: 163 us -> 0 us
  Pallas kernels: 0 us -> 35.2 us
  matrix products: 14.3 us -> 0 us
    psum x4 -> x0, blocking collectives: 197 us -> none  [the longest x2 129 us: precond_inner(): return lax.psum(jnp.sum(remainder * scaled), 'frames')]
    gather x6 -> x0, local copies, waits for them, and re-layouts: 180 us -> none  [the longest x2 120 us: apply_operator(): window = padded[:, window_idx]]
    scatter-add x3 -> x0, other arithmetic: 137 us -> none  [the longest x2 88.9 us: collect(): return jax.ops.segment_sum(values_in.T, point_ids, num_segments=pt_rows).T]
    pallas_call x0 -> x8, Pallas kernels: none -> 35.2 us  [the longest x3 17.8 us: call(): pl.pallas_call(kernel, grid_spec=pltpu.PrefetchScalarGridSpec(num_scalar_...]
    unnamed x23 -> x42, local copies, waits for them, and re-layouts: 30.5 us -> 13.3 us
    dot_general x1 -> x0, matrix products: 14.3 us -> none  [invert_points(): return jnp.einsum('ijp,jp->ip', point_inv, gradient, precision=HIGHEST)]
    all_to_all x3 -> x0, waiting for transfers between devices: 14.1 us -> none  [the longest x1 10.7 us: local(): lax.all_to_all(grad_terms.reshape(coeffs, groups, slot_width), 'points',...]
    all_to_all x3 -> x0, starting transfers between devices: 12.6 us -> none  [the longest x1 4.83 us: local(): lax.all_to_all(slot_ids, 'points', split_axis=1, concat_axis=1, tiled=True)]
  transfers between devices with their start and end apart: 8 -> 17, of which waited for: 4 -> 9; matrix products, arithmetic and copies ran while one was open for 10% -> 8% of each run, Pallas kernels for 0% -> 4%
where the time goes in v1:
time: 110 us; the launch traced here: 109 us
  Pallas kernels  35.2 us (32%)
  starting transfers between devices  26.9 us (24%)
  blocking collectives  17.7 us (16%)
  waiting for transfers between devices  15.4 us (14%)
  local copies, waits for them, and re-layouts  13.3 us (12%)
    pallas_call x3, Pallas kernels, call(): pl.pallas_call(kernel, grid_spec=pltpu.PrefetchScalarGridSpec(num_scalar_...  17.8 us
    all_to_all x1, blocking collectives, local(): lax.all_to_all(gram, 'frames', split_axis=0, concat_axis=0, tiled=True)  17.7 us
    ppermute x12, waiting for transfers between devices, shifted(): lax.ppermute(value, axis, [(i, (i + step) % count) for i in range(count)])  14.6 us
    unnamed x42, local copies, waits for them, and re-layouts  13.3 us
    ppermute x12, starting transfers between devices, shifted(): lax.ppermute(value, axis, [(i, (i + step) % count) for i in range(count)])  11 us
    pallas_call x3, Pallas kernels, plain(): pl.pallas_call(kernel, in_specs=specs, out_specs=out_specs, out_shape=out...  9.45 us
    ppermute x2, starting transfers between devices, beside(): lax.ppermute(value, 'frames', down)  7.29 us
    ppermute x2, starting transfers between devices, beside(): lax.ppermute(value, 'frames', up)  6.2 us
  transfers between devices with their start and end apart: 17, of which 9 were waited for; matrix products, arithmetic and copies ran while one was open for 8% of the time, Pallas kernels for 4%

profile of v1, /device:TPU:1, one launch (start us, length us, event | category | flops | bytes accessed | tf_op | source)
XLA Modules:
  0.0 109.2 jit_solution(2723003575312738179)
XLA Ops:
  0.7 5.3 %point_grad.1 = (f32[24,1024]{1,0:T(8,128)}, f32[24,1024]{1,0:T(8,128)}, f32[24,1024]{1,0:T(8,128)}, f32[24,1024]{1,0:T(8,128)}) custom-call(s32[1]{0:T(128)} %bitcast.1.me_ref, s32[4]{0:T(128)} %count_ref.5, s32[1,8192]{1,0:T(1,128)} %bitcast.14, f32[2,8192]{1,0:T(2,128)} %res_ref.3, f32[2,24,8192]{2,1,0:T(8,128)} %jp_ref.5), custom_call_target="tpu_custom_call" | custom-call | flops 805306368 | bytes 1572864 | tf_op jit(solution)/shard_map/point_grad/pallas_call | solution.py:246
  5.9 3.3 %collective-permute-start = (f32[24,1024]{1,0:T(8,128)}, f32[24,1024]{1,0:T(8,128)S(1)}, u32[]{:S(2)}, u32[]{:S(2)}) collective-permute-start(f32[24,1024]{1,0:T(8,128)} %get-tuple-element.14), channel_id=1, source_target_pairs={{0,3},{1,0},{2,1},{3,2},{4,7},{5,4},{6,5},{7,6},{8,11},{9,8},{10,9... | collective-permute-start | bytes 294920 | tf_op jit(solution)/shard_map/ppermute | solution.py:226
  10.4 0.8 collective-permute-done.a_ref
  11.2 3.3 %collective-permute-done.1.b_ref = f32[24,1024]{1,0:T(8,128)S(1)} collective-permute-done((f32[24,1024]{1,0:T(8,128)}, f32[24,1024]{1,0:T(8,128)S(1)}, u32[]{:S(2)}, u32[]{:S(2)}) %collective-permute-start.1) | collective-permute-done | bytes 98336 | tf_op jit(solution)/shard_map/ppermute | solution.py:226
  14.5 2.7 %collective-permute-done.2.c_ref = f32[24,1024]{1,0:T(8,128)S(1)} collective-permute-done((f32[24,1024]{1,0:T(8,128)}, f32[24,1024]{1,0:T(8,128)S(1)}, u32[]{:S(2)}, u32[]{:S(2)}) %collective-permute-start.2) | collective-permute-done | bytes 98336 | tf_op jit(solution)/shard_map/ppermute | solution.py:226
  17.9 3.7 %point_solve.1.rest_0_.ps_ref = f32[24,1024]{1,0:T(8,128)} custom-call(f32[24,1024]{1,0:T(8,128)} %copy-done.4, f32[24,1024]{1,0:T(8,128)} %copy-done.5, f32[24,1024]{1,0:T(8,128)} %copy-done.6, f32[24,1024]{1,0:T(8,128)} %get-tuple-element.17.d_ref, f32[24,24,1024]{2,1,0:T(8,128)} %inv_ref.3), custom_call_target="tpu_custom_call" | custom-call | flops 1179648 | bytes 2359296 | tf_op jit(solution)/shard_map/point_solve/pallas_call | solution.py:324
  21.8 1.3 %collective-permute-start.3 = (f32[24,1024]{1,0:T(8,128)}, f32[24,1024]{1,0:T(8,128)S(1)}, u32[]{:S(2)}, u32[]{:S(2)}) collective-permute-start(f32[24,1024]{1,0:T(8,128)} %point_solve.1.rest_0_.ps_ref), channel_id=1, source_target_pairs={{0,1},{1,2},{2,3},{3,0},{4,5},{5,6},{6,7},{7,4},{8,9},{9,10},{10,1... | collective-permute-start | bytes 294920 | tf_op jit(solution)/shard_map/ppermute | solution.py:226
  23.1 1.0 copy.16.jc_ref
  24.1 1.2 %collective-permute-done.5.rest_3_ = f32[24,1024]{1,0:T(8,128)S(1)} collective-permute-done((f32[24,1024]{1,0:T(8,128)}, f32[24,1024]{1,0:T(8,128)S(1)}, u32[]{:S(2)}, u32[]{:S(2)}) %collective-permute-start.5) | collective-permute-done | bytes 98336 | tf_op jit(solution)/shard_map/ppermute | solution.py:226
  25.3 1.5 %collective-permute-done.4.rest_2_ = f32[24,1024]{1,0:T(8,128)S(1)} collective-permute-done((f32[24,1024]{1,0:T(8,128)}, f32[24,1024]{1,0:T(8,128)S(1)}, u32[]{:S(2)}, u32[]{:S(2)}) %collective-permute-start.4) | collective-permute-done | bytes 98336 | tf_op jit(solution)/shard_map/ppermute | solution.py:226
  26.8 1.4 %collective-permute-done.3.rest_1_ = f32[24,1024]{1,0:T(8,128)S(1)} collective-permute-done((f32[24,1024]{1,0:T(8,128)}, f32[24,1024]{1,0:T(8,128)S(1)}, u32[]{:S(2)}, u32[]{:S(2)}) %collective-permute-start.3) | collective-permute-done | bytes 98336 | tf_op jit(solution)/shard_map/ppermute | solution.py:226
  28.2 0.6 copy-done.19
  28.9 6.0 %camera_rhs.1.a_ref = f32[6,256]{1,0:T(8,128)} custom-call(s32[1]{0:T(128)} %bitcast.1.me_ref, s32[4]{0:T(128)} %count_ref.5, s32[1,8192]{1,0:T(1,128)} %bitcast.15, s32[1,8192]{1,0:T(1,128)} %bitcast.17, f32[2,8192]{1,0:T(2,128)} %res_ref.3, f32[2,24,8192]{2,1,0:T(8,128)} %jp_ref.5, f32[2,6,8192]{2,1,0:T(8,128)} %copy.16.jc_ref, ...), custom_call_target="tpu_custom_call" | custom-call | flops 1073741824 | bytes 2097152 | tf_op jit(solution)/shard_map/camera_rhs/pallas_call | solution.py:246
  34.9 2.2 %collective-permute-start.8 = (f32[6,256]{1,0:T(8,128)}, f32[6,256]{1,0:T(8,128)S(1)}, u32[]{:S(2)}, u32[]{:S(2)}) collective-permute-start(f32[6,256]{1,0:T(8,128)} %camera_rhs.1.a_ref), channel_id=1, source_target_pairs={{0,3},{1,0},{2,1},{3,2},{4,7},{5,4},{6,5},{7,6},{8,11},{9,8},{10,9... | collective-permute-start | bytes 18440 | tf_op jit(solution)/shard_map/ppermute | solution.py:226
  37.1 0.7 collective-permute-start.6
  38.1 3.2 %collective-permute-done.7.c_ref = f32[6,256]{1,0:T(8,128)S(1)} collective-permute-done((f32[6,256]{1,0:T(8,128)}, f32[6,256]{1,0:T(8,128)S(1)}, u32[]{:S(2)}, u32[]{:S(2)}) %collective-permute-start.7) | collective-permute-done | bytes 6176 | tf_op jit(solution)/shard_map/ppermute | solution.py:226
  42.6 1.5 %start.1 = (f32[6,256]{1,0:T(8,128)}, f32[6,256]{1,0:T(8,128)}) custom-call(f32[6,256]{1,0:T(8,128)} %camera_rhs.1.a_ref, f32[6,256]{1,0:T(8,128)} %copy-done.14, f32[6,256]{1,0:T(8,128)} %copy-done.13, f32[6,256]{1,0:T(8,128)} %copy-done.12, f32[6,6,256]{2,1,0:T(8,128)} %pre_ref.3), custom_call_target="tpu_custom_call" | custom-call | flops 20000 | bytes 100000 | tf_op jit(solution)/shard_map/start/pallas_call | solution.py:281
  44.0 4.7 %collective-permute-start.10 = (f32[6,256]{1,0:T(8,128)}, f32[6,256]{1,0:T(8,128)S(1)}, u32[]{:S(2)}, u32[]{:S(2)}) collective-permute-start(f32[6,256]{1,0:T(8,128)} %get-tuple-element.18.z_ref), channel_id=1, source_target_pairs={{4,0},{8,4},{12,8},{16,12},{20,16},{24,20},{28,24},{32,28},{36,32}... | collective-permute-start | bytes 18440 | tf_op jit(solution)/shard_map/ppermute | solution.py:233
  48.8 3.1 %collective-permute-start.9 = (f32[6,256]{1,0:T(8,128)}, f32[6,256]{1,0:T(8,128)S(1)}, u32[]{:S(2)}, u32[]{:S(2)}) collective-permute-start(f32[6,256]{1,0:T(8,128)} %get-tuple-element.18.z_ref), channel_id=1, source_target_pairs={{0,4},{4,8},{8,12},{12,16},{16,20},{20,24},{24,28},{28,32},{32,36}... | collective-permute-start | bytes 18440 | tf_op jit(solution)/shard_map/ppermute | solution.py:233
  51.9 2.4 %collective-permute-start.11 = (f32[1,256]{1,0:T(1,128)S(1)}, f32[1,256]{1,0:T(1,128)S(1)}, u32[]{:S(2)}, u32[]{:S(2)}) collective-permute-start(f32[1,256]{1,0:T(1,128)S(1)} %bitcast.13), channel_id=1, source_target_pairs={{0,4},{4,8},{8,12},{12,16},{16,20},{20,24},{24,28},{28,32},{32,36}... | collective-permute-start | bytes 3080 | tf_op jit(solution)/shard_map/ppermute | solution.py:305
  54.3 7.8 %copy.17.band_ref = f32[127,6,6,256]{3,2,1,0:T(8,128)} copy(f32[127,6,6,256]{3,0,2,1:T(8,128)} %param.17) | data formatting | bytes 9363456 | tf_op args[7]
  62.7 3.9 %operator_one.1 = (f32[6,256]{1,0:T(8,128)}, f32[6,256]{1,0:T(8,128)}) custom-call(s32[1]{0:T(128)} %bitcast.last_ref, f32[6,256]{1,0:T(8,128)} %get-tuple-element.18.z_ref, f32[6,256]{1,0:T(8,128)} %copy-done.9, f32[6,256]{1,0:T(8,128)} %copy-done.8, f32[127,6,6,256]{3,2,1,0:T(8,128)} %copy.17.band_ref, f32[1,256]{1,0:T(1,128)} %bitcast.11, ...), custom_call_target="tpu_custom_call" | custom-call | flops 2340864 | bytes 6242304 | tf_op jit(solution)/shard_map/operator_one/pallas_call | solution.py:281
  66.7 6.5 %back_terms.1 = (f32[48,1024]{1,0:T(8,128)}, f32[48,1024]{1,0:T(8,128)}, f32[48,1024]{1,0:T(8,128)}, f32[48,1024]{1,0:T(8,128)}) custom-call(s32[1]{0:T(128)} %bitcast.1.me_ref, s32[4]{0:T(128)} %count_ref.5, s32[1,8192]{1,0:T(1,128)} %bitcast.16, s32[1,8192]{1,0:T(1,128)} %bitcast.18, f32[2,24,8192]{2,1,0:T(8,128)} %jp_ref.5, f32[2,6,8192]{2,1,0:T(8,128)} %copy.16.jc_ref, ...), custom_call_target="tpu_custom_call" | custom-call | flops 1677721600 | bytes 2097152 | tf_op jit(solution)/shard_map/back_terms/pallas_call | solution.py:246
  73.2 1.0 collective-permute-start.14
  74.2 1.2 %collective-permute-start.15 = (f32[48,1024]{1,0:T(8,128)}, f32[48,1024]{1,0:T(8,128)S(1)}, u32[]{:S(2)}, u32[]{:S(2)}) collective-permute-start(f32[48,1024]{1,0:T(8,128)} %get-tuple-element.23), channel_id=1, source_target_pairs={{0,2},{1,3},{2,0},{3,1},{4,6},{5,7},{6,4},{7,5},{8,10},{9,11},{10,... | collective-permute-start | bytes 589832 | tf_op jit(solution)/shard_map/ppermute | solution.py:226
  75.4 2.5 %collective-permute-start.13 = (f32[6,256]{1,0:T(8,128)S(1)}, f32[6,256]{1,0:T(8,128)S(1)}, u32[]{:S(2)}, u32[]{:S(2)}) collective-permute-start(f32[6,256]{1,0:T(8,128)S(1)} %copy-done.7), channel_id=1, source_target_pairs={{4,0},{8,4},{12,8},{16,12},{20,16},{24,20},{28,24},{32,28},{36,32}... | collective-permute-start | bytes 18440 | tf_op jit(solution)/shard_map/ppermute | solution.py:233
  77.9 3.1 %collective-permute-start.12 = (f32[6,256]{1,0:T(8,128)S(1)}, f32[6,256]{1,0:T(8,128)S(1)}, u32[]{:S(2)}, u32[]{:S(2)}) collective-permute-start(f32[6,256]{1,0:T(8,128)S(1)} %copy-done.7), channel_id=1, source_target_pairs={{0,4},{4,8},{8,12},{12,16},{16,20},{20,24},{24,28},{28,32},{32,36}... | collective-permute-start | bytes 18440 | tf_op jit(solution)/shard_map/ppermute | solution.py:233
  81.1 0.8 collective-permute-done.12.ul_ref
  82.4 4.0 %operator_two.1 = f32[32,128]{1,0:T(8,128)} custom-call(s32[1]{0:T(128)} %bitcast.last_ref, f32[6,256]{1,0:T(8,128)} %get-tuple-element.19.u_ref, f32[6,256]{1,0:T(8,128)} %copy-done.11, f32[6,256]{1,0:T(8,128)} %copy-done.10, f32[127,6,6,256]{3,2,1,0:T(8,128)} %copy.17.band_ref, f32[1,256]{1,0:T(1,128)} %bitcast.12, f32[1,256]{1,0:T(1,128)} %copy-done.16, ...), custom_call_target="tpu_custom_call" | custom-call | flops 2340864 | bytes 6242304 | tf_op jit(solution)/shard_map/operator_two/pallas_call | solution.py:281
  86.4 17.7 %all_to_all.11 = f32[32,1,128]{2,1,0:T(1,128)} all-to-all(f32[32,1,128]{2,1,0:T(1,128)} %bitcast.10), channel_id=1, replica_groups=mesh['frames'=32,'points'=4] {'frames'}, dimensions={0} | all-to-all | bytes 32768 | tf_op jit(solution)/shard_map/all_to_all | solution.py:392
  104.2 0.6 copy-done.1
  105.0 4.2 %final.1 = (f32[6,256]{1,0:T(8,128)}, f32[24,1024]{1,0:T(8,128)}) custom-call(f32[32,128]{1,0:T(8,128)} %bitcast.9, f32[6,256]{1,0:T(8,128)} %get-tuple-element.18.z_ref, f32[6,256]{1,0:T(8,128)} %get-tuple-element.19.u_ref, f32[24,1024]{1,0:T(8,128)} %point_solve.1.rest_0_.ps_ref, f32[48,1024]{1,0:T(8,128)} %copy-done.1, f32[48,1024]{1,0:T(8,128)} %copy-done.2, ...), custom_call_target="tpu_custom_call" | custom-call | flops 1179648 | bytes 2359296 | tf_op jit(solution)/shard_map/final/pallas_call | solution.py:395
  (53 shorter events, 4.9 us)
Async XLA Ops:
  0.6 22.4 %copy-start = (f32[2,6,8192]{2,0,1:T(2,128)S(1)}, f32[2,6,8192]{2,0,1:T(2,128)}, u32[]{:S(2)}) copy-start(f32[2,6,8192]{2,0,1:T(2,128)} %param.13) | copy-start | bytes 1179652
  0.6 51.3 %copy-start.15 = (f32[256]{0:T(256)S(1)}, f32[256]{0:T(256)}, u32[]{:S(2)}) copy-start(f32[256]{0:T(256)} %param.18) | copy-start | bytes 3076
  5.9 5.3 %collective-permute-start = (f32[24,1024]{1,0:T(8,128)}, f32[24,1024]{1,0:T(8,128)S(1)}, u32[]{:S(2)}, u32[]{:S(2)}) collective-permute-start(f32[24,1024]{1,0:T(8,128)} %get-tuple-element.14), channel_id=1, source_target_pairs={{0,3},{1,0},{2,1},{3,2},{4,7},{5,4},{6,5},{7,6},{8,11},{9,8},{10,9... | collective-permute-start | bytes 294920 | tf_op jit(solution)/shard_map/ppermute | solution.py:226
  9.2 5.3 %collective-permute-start.1 = (f32[24,1024]{1,0:T(8,128)}, f32[24,1024]{1,0:T(8,128)S(1)}, u32[]{:S(2)}, u32[]{:S(2)}) collective-permute-start(f32[24,1024]{1,0:T(8,128)} %get-tuple-element.15), channel_id=1, source_target_pairs={{0,2},{1,3},{2,0},{3,1},{4,6},{5,7},{6,4},{7,5},{8,10},{9,11},{10,... | collective-permute-start | bytes 294920 | tf_op jit(solution)/shard_map/ppermute | solution.py:226
  9.7 7.5 %collective-permute-start.2 = (f32[24,1024]{1,0:T(8,128)}, f32[24,1024]{1,0:T(8,128)S(1)}, u32[]{:S(2)}, u32[]{:S(2)}) collective-permute-start(f32[24,1024]{1,0:T(8,128)} %get-tuple-element.16), channel_id=1, source_target_pairs={{0,1},{1,2},{2,3},{3,0},{4,5},{5,6},{6,7},{7,4},{8,9},{9,10},{10,1... | collective-permute-start | bytes 294920 | tf_op jit(solution)/shard_map/ppermute | solution.py:226
  11.2 6.1 %copy-start.4 = (f32[24,1024]{1,0:T(8,128)}, f32[24,1024]{1,0:T(8,128)S(1)}, u32[]{:S(2)}) copy-start(f32[24,1024]{1,0:T(8,128)S(1)} %collective-permute-done.a_ref) | copy-start | bytes 294916
  14.5 2.8 %copy-start.5 = (f32[24,1024]{1,0:T(8,128)}, f32[24,1024]{1,0:T(8,128)S(1)}, u32[]{:S(2)}) copy-start(f32[24,1024]{1,0:T(8,128)S(1)} %collective-permute-done.1.b_ref) | copy-start | bytes 294916
  17.3 0.6 copy-start.6
  21.6 3.7 %collective-permute-start.5 = (f32[24,1024]{1,0:T(8,128)}, f32[24,1024]{1,0:T(8,128)S(1)}, u32[]{:S(2)}, u32[]{:S(2)}) collective-permute-start(f32[24,1024]{1,0:T(8,128)} %point_solve.1.rest_0_.ps_ref), channel_id=1, source_target_pairs={{0,3},{1,0},{2,1},{3,2},{4,7},{5,4},{6,5},{7,6},{8,11},{9,8},{10,9... | collective-permute-start | bytes 294920 | tf_op jit(solution)/shard_map/ppermute | solution.py:226
  21.6 5.2 %collective-permute-start.4 = (f32[24,1024]{1,0:T(8,128)}, f32[24,1024]{1,0:T(8,128)S(1)}, u32[]{:S(2)}, u32[]{:S(2)}) collective-permute-start(f32[24,1024]{1,0:T(8,128)} %point_solve.1.rest_0_.ps_ref), channel_id=1, source_target_pairs={{0,2},{1,3},{2,0},{3,1},{4,6},{5,7},{6,4},{7,5},{8,10},{9,11},{10,... | collective-permute-start | bytes 294920 | tf_op jit(solution)/shard_map/ppermute | solution.py:226
  21.8 6.5 %collective-permute-start.3 = (f32[24,1024]{1,0:T(8,128)}, f32[24,1024]{1,0:T(8,128)S(1)}, u32[]{:S(2)}, u32[]{:S(2)}) collective-permute-start(f32[24,1024]{1,0:T(8,128)} %point_solve.1.rest_0_.ps_ref), channel_id=1, source_target_pairs={{0,1},{1,2},{2,3},{3,0},{4,5},{5,6},{6,7},{7,4},{8,9},{9,10},{10,1... | collective-permute-start | bytes 294920 | tf_op jit(solution)/shard_map/ppermute | solution.py:226
  25.3 3.0 %copy-start.17 = (f32[24,1024]{1,0:T(8,128)}, f32[24,1024]{1,0:T(8,128)S(1)}, u32[]{:S(2)}) copy-start(f32[24,1024]{1,0:T(8,128)S(1)} %collective-permute-done.5.rest_3_) | copy-start | bytes 294916
  26.8 1.5 %copy-start.18 = (f32[24,1024]{1,0:T(8,128)}, f32[24,1024]{1,0:T(8,128)S(1)}, u32[]{:S(2)}) copy-start(f32[24,1024]{1,0:T(8,128)S(1)} %collective-permute-done.4.rest_2_) | copy-start | bytes 294916
  28.2 0.6 copy-start.19
  34.9 3.2 %collective-permute-start.8 = (f32[6,256]{1,0:T(8,128)}, f32[6,256]{1,0:T(8,128)S(1)}, u32[]{:S(2)}, u32[]{:S(2)}) collective-permute-start(f32[6,256]{1,0:T(8,128)} %camera_rhs.1.a_ref), channel_id=1, source_target_pairs={{0,3},{1,0},{2,1},{3,2},{4,7},{5,4},{6,5},{7,6},{8,11},{9,8},{10,9... | collective-permute-start | bytes 18440 | tf_op jit(solution)/shard_map/ppermute | solution.py:226
  37.1 4.2 %collective-permute-start.7 = (f32[6,256]{1,0:T(8,128)}, f32[6,256]{1,0:T(8,128)S(1)}, u32[]{:S(2)}, u32[]{:S(2)}) collective-permute-start(f32[6,256]{1,0:T(8,128)} %camera_rhs.1.a_ref), channel_id=1, source_target_pairs={{0,2},{1,3},{2,0},{3,1},{4,6},{5,7},{6,4},{7,5},{8,10},{9,11},{10,... | collective-permute-start | bytes 18440 | tf_op jit(solution)/shard_map/ppermute | solution.py:226
  37.1 4.2 %collective-permute-start.6 = (f32[6,256]{1,0:T(8,128)}, f32[6,256]{1,0:T(8,128)S(1)}, u32[]{:S(2)}, u32[]{:S(2)}) collective-permute-start(f32[6,256]{1,0:T(8,128)} %camera_rhs.1.a_ref), channel_id=1, source_target_pairs={{0,1},{1,2},{2,3},{3,0},{4,5},{5,6},{6,7},{7,4},{8,9},{9,10},{10,1... | collective-permute-start | bytes 18440 | tf_op jit(solution)/shard_map/ppermute | solution.py:226
  38.1 3.2 %copy-start.12 = (f32[6,256]{1,0:T(8,128)}, f32[6,256]{1,0:T(8,128)S(1)}, u32[]{:S(2)}) copy-start(f32[6,256]{1,0:T(8,128)S(1)} %collective-permute-done.8.d_ref) | copy-start | bytes 18436
  44.0 18.1 %collective-permute-start.10 = (f32[6,256]{1,0:T(8,128)}, f32[6,256]{1,0:T(8,128)S(1)}, u32[]{:S(2)}, u32[]{:S(2)}) collective-permute-start(f32[6,256]{1,0:T(8,128)} %get-tuple-element.18.z_ref), channel_id=1, source_target_pairs={{4,0},{8,4},{12,8},{16,12},{20,16},{24,20},{28,24},{32,28},{36,32}... | collective-permute-start | bytes 18440 | tf_op jit(solution)/shard_map/ppermute | solution.py:233
  48.8 13.3 %collective-permute-start.9 = (f32[6,256]{1,0:T(8,128)}, f32[6,256]{1,0:T(8,128)S(1)}, u32[]{:S(2)}, u32[]{:S(2)}) collective-permute-start(f32[6,256]{1,0:T(8,128)} %get-tuple-element.18.z_ref), channel_id=1, source_target_pairs={{0,4},{4,8},{8,12},{12,16},{16,20},{20,24},{24,28},{28,32},{32,36}... | collective-permute-start | bytes 18440 | tf_op jit(solution)/shard_map/ppermute | solution.py:233
  51.9 10.2 %collective-permute-start.11 = (f32[1,256]{1,0:T(1,128)S(1)}, f32[1,256]{1,0:T(1,128)S(1)}, u32[]{:S(2)}, u32[]{:S(2)}) collective-permute-start(f32[1,256]{1,0:T(1,128)S(1)} %bitcast.13), channel_id=1, source_target_pairs={{0,4},{4,8},{8,12},{12,16},{16,20},{20,24},{24,28},{28,32},{32,36}... | collective-permute-start | bytes 3080 | tf_op jit(solution)/shard_map/ppermute | solution.py:305
  62.1 0.6 copy-start.8
  66.7 8.7 %copy-start.7 = (f32[6,256]{1,0:T(8,128)S(1)}, f32[6,256]{1,0:T(8,128)}, u32[]{:S(2)}) copy-start(f32[6,256]{1,0:T(8,128)} %get-tuple-element.19.u_ref) | copy-start | bytes 18436
  73.2 31.0 %collective-permute-start.14 = (f32[48,1024]{1,0:T(8,128)}, f32[48,1024]{1,0:T(8,128)S(1)}, u32[]{:S(2)}, u32[]{:S(2)}) collective-permute-start(f32[48,1024]{1,0:T(8,128)} %get-tuple-element.22), channel_id=1, source_target_pairs={{0,3},{1,0},{2,1},{3,2},{4,7},{5,4},{6,5},{7,6},{8,11},{9,8},{10,9... | collective-permute-start | bytes 589832 | tf_op jit(solution)/shard_map/ppermute | solution.py:226
  74.2 30.0 %collective-permute-start.15 = (f32[48,1024]{1,0:T(8,128)}, f32[48,1024]{1,0:T(8,128)S(1)}, u32[]{:S(2)}, u32[]{:S(2)}) collective-permute-start(f32[48,1024]{1,0:T(8,128)} %get-tuple-element.23), channel_id=1, source_target_pairs={{0,2},{1,3},{2,0},{3,1},{4,6},{5,7},{6,4},{7,5},{8,10},{9,11},{10,... | collective-permute-start | bytes 589832 | tf_op jit(solution)/shard_map/ppermute | solution.py:226
  75.4 28.8 %collective-permute-start.16 = (f32[48,1024]{1,0:T(8,128)}, f32[48,1024]{1,0:T(8,128)S(1)}, u32[]{:S(2)}, u32[]{:S(2)}) collective-permute-start(f32[48,1024]{1,0:T(8,128)} %get-tuple-element.24), channel_id=1, source_target_pairs={{0,1},{1,2},{2,3},{3,0},{4,5},{5,6},{6,7},{7,4},{8,9},{9,10},{10,1... | collective-permute-start | bytes 589832 | tf_op jit(solution)/shard_map/ppermute | solution.py:226
  75.4 5.7 %collective-permute-start.13 = (f32[6,256]{1,0:T(8,128)S(1)}, f32[6,256]{1,0:T(8,128)S(1)}, u32[]{:S(2)}, u32[]{:S(2)}) collective-permute-start(f32[6,256]{1,0:T(8,128)S(1)} %copy-done.7), channel_id=1, source_target_pairs={{4,0},{8,4},{12,8},{16,12},{20,16},{24,20},{28,24},{32,28},{36,32}... | collective-permute-start | bytes 18440 | tf_op jit(solution)/shard_map/ppermute | solution.py:233
  77.9 3.9 %collective-permute-start.12 = (f32[6,256]{1,0:T(8,128)S(1)}, f32[6,256]{1,0:T(8,128)S(1)}, u32[]{:S(2)}, u32[]{:S(2)}) collective-permute-start(f32[6,256]{1,0:T(8,128)S(1)} %copy-done.7), channel_id=1, source_target_pairs={{0,4},{4,8},{8,12},{12,16},{16,20},{20,24},{24,28},{28,32},{32,36}... | collective-permute-start | bytes 18440 | tf_op jit(solution)/shard_map/ppermute | solution.py:233
  81.1 0.8 copy-start.10
  104.2 0.7 copy-start.1
  104.2 0.7 copy-start.2
  104.2 0.8 copy-start.3
  (5 other events, 2.9 us)

commit v2 on v1

v2 whole, which is shorter than its diff:
```python
import functools

import jax
import jax.numpy as jnp
from jax import lax
from jax.experimental import pallas as pl
from jax.experimental.pallas import tpu as pltpu
from jax.sharding import PartitionSpec as P

F32 = jnp.float32
BF16 = jnp.bfloat16
CP = 6
Q = 24
BANDW = 127
REACH = 63
FR = 256
PT = 1024
CAP = 2048
GROUPS = 4
LO = 256
HI = PT // LO
LIMIT = pltpu.CompilerParams(vmem_limit_bytes=12 * 2**20)


def halves(x):
    lead = x.astype(BF16).astype(F32)
    return jnp.concatenate([lead, x - lead], axis=0).astype(BF16)


def one_hot(row, rows):
    n = row.shape[1]
    index = lax.broadcasted_iota(jnp.int32, (rows, 128), 0).astype(F32).astype(BF16)
    row = row.astype(BF16)
    cols = []
    for c in range(n // 128):
        here = jnp.broadcast_to(row[:, c * 128 : (c + 1) * 128], (rows, 128))
        cols.append(jnp.where(index == here, jnp.ones_like(index), jnp.zeros_like(index)))
    return jnp.concatenate(cols, axis=1)


def split_ids(ids):
    hi = lax.shift_right_logical(ids, 8)
    lo = lax.bitwise_and(ids, LO - 1)
    return hi.astype(F32), lo.astype(F32)


def used_row(count):
    lane = lax.broadcasted_iota(jnp.int32, (1, CAP), 1)
    return (lane < count).astype(F32)


def scatter_points(terms, ids):
    n = terms.shape[0]
    hi, lo = split_ids(ids)
    parts = halves(terms)
    table = one_hot(lo, LO)
    rows = []
    for h in range(HI):
        mask = jnp.broadcast_to((hi == h).astype(F32), (2 * n, CAP)).astype(BF16)
        rows.append(parts * mask)
    sums = lax.dot_general(
        jnp.concatenate(rows, axis=0), table, (((1,), (1,)), ((), ())), preferred_element_type=F32
    )
    out = []
    for h in range(HI):
        block = sums[h * 2 * n : (h + 1) * 2 * n]
        out.append(block[:n] + block[n:])
    return jnp.concatenate(out, axis=1)


def gather_points(values, ids):
    n = values.shape[0]
    hi, lo = split_ids(ids)
    parts = halves(values)
    table = one_hot(lo, LO)
    stacked = jnp.concatenate([parts[:, h * LO : (h + 1) * LO] for h in range(HI)], axis=0)
    got = lax.dot_general(stacked, table, (((1,), (0,)), ((), ())), preferred_element_type=F32)
    total = None
    for h in range(HI):
        block = got[h * 2 * n : (h + 1) * 2 * n]
        term = (block[:n] + block[n:]) * (hi == h).astype(F32)
        total = term if total is None else total + term
    return total


def block_at(turn):
    return lax.rem(lax.axis_index("points") + GROUPS + turn, GROUPS)


def lanes(b):
    return pl.ds(pl.multiple_of(b * CAP, CAP), CAP)


def grad_kernel(count_ref, ids_hbm, res_hbm, jp_hbm, *rest):
    outs, (ids_ref, res_ref, jp_ref, sems) = rest[:GROUPS], rest[GROUPS:]
    small = [
        pltpu.make_async_copy(ids_hbm, ids_ref, sems.at[GROUPS]),
        pltpu.make_async_copy(res_hbm, res_ref, sems.at[GROUPS + 1]),
    ]
    blocks = [block_at(GROUPS - 1 - j) for j in range(GROUPS)]
    large = [
        pltpu.make_async_copy(jp_hbm.at[:, :, lanes(b)], jp_ref.at[j], sems.at[j])
        for j, b in enumerate(blocks)
    ]
    for copy in small + large:
        copy.start()
    for copy in small:
        copy.wait()
    for j, b in enumerate(blocks):
        at = lanes(b)
        large[j].wait()
        res = res_ref[:, at] * used_row(count_ref[b])
        terms = jp_ref[j, 0] * res[0:1] + jp_ref[j, 1] * res[1:2]
        outs[j][...] = scatter_points(terms, ids_ref[:, at])


def solve_kernel(a_ref, b_ref, c_ref, d_ref, inv_ref, out_ref):
    grad = a_ref[...] + b_ref[...] + c_ref[...] + d_ref[...]
    out_ref[...] = jnp.sum(inv_ref[...] * grad[None], axis=1)


def rhs_kernel(turn, count_ref, pid_ref, fid_ref, res_ref, jp_ref, jc_ref, *rest):
    solved_ref, out_ref = rest[-2:]
    b = block_at(turn)
    at = lanes(b)
    used = used_row(count_ref[b])
    seen = gather_points(solved_ref[...], pid_ref[:, at])
    remain = [
        (res_ref[a : a + 1, at] - jnp.sum(jp_ref[a, :, at] * seen, axis=0, keepdims=True)) * used
        for a in range(2)
    ]
    cam = jc_ref[0, :, at] * remain[0] + jc_ref[1, :, at] * remain[1]
    cam = jnp.concatenate([cam, jnp.zeros((2, CAP), F32)], axis=0)
    table = one_hot(fid_ref[:, at].astype(F32), FR)
    sums = lax.dot_general(
        halves(cam), table, (((1,), (1,)), ((), ())), preferred_element_type=F32
    )
    total = sums[0:CP] + sums[8 : 8 + CP]
    out_ref[...] = total if len(rest) == 2 else total + rest[0][...]


def apply_precond(pre_ref, vec):
    return jnp.sum(pre_ref[...] * vec[None], axis=1)


def start_kernel(a_ref, b_ref, c_ref, d_ref, pre_ref, edge_ref, r_ref, z_ref):
    rhs = a_ref[...] + b_ref[...] + c_ref[...] + d_ref[...]
    r_ref[...] = rhs
    lane = lax.broadcasted_iota(jnp.int32, (1, FR), 1)
    last = lax.axis_index("frames") == lax.axis_size("frames") - 1
    edge = edge_ref[...] * jnp.where((lane == FR - 1) & last, 0.0, 1.0)
    z = apply_precond(pre_ref, rhs)
    z_ref[...] = jnp.concatenate([z, edge, jnp.zeros((1, FR), F32)], axis=0)


def steps_of(row, width):
    n = row.shape[1]
    sub = lax.broadcasted_iota(jnp.int32, (8, n), 0)
    x = jnp.broadcast_to(row, (8, n))
    for bit in (1, 2, 4):
        x = jnp.where((sub & bit) != 0, pltpu.roll(x, n - bit, 1), x)
    return x


def banded_sums(band_ref, rows, tiles, first=None):
    totals = [None] * CP
    ends = [None] * CP
    for j in range(CP):
        stepped = steps_of(rows[j], 0)
        for t in tiles:
            at = 128 - REACH + 8 * t
            shifted = stepped[:, at : at + FR]
            if t == first:
                sub = lax.broadcasted_iota(jnp.int32, (8, FR), 0)
                shifted = jnp.where(sub == 7, 0.5 * shifted, 0.0)
            for i in range(CP):
                if 8 * t + 8 <= BANDW:
                    term = band_ref[i, j, 8 * t : 8 * t + 8, :] * shifted
                    totals[i] = term if totals[i] is None else totals[i] + term
                else:
                    count = BANDW - 8 * t
                    term = band_ref[i, j, 8 * t : BANDW, :] * shifted[:count]
                    ends[i] = term if ends[i] is None else ends[i] + term
    return jnp.concatenate(
        [
            jnp.sum(t, axis=0, keepdims=True) + jnp.sum(e, axis=0, keepdims=True)
            for t, e in zip(totals, ends)
        ],
        axis=0,
    )


def first_kernel(z_ref, left_ref, right_ref, band_ref, pre_ref, w_ref, u_ref):
    padded = jnp.concatenate([left_ref[...], z_ref[...], right_ref[...]], axis=1)
    near = padded[:, FR - 128 : 2 * FR + 128]
    banded = banded_sums(band_ref, [near[j : j + 1] for j in range(CP)], range(16))
    own = z_ref[:CP, :]
    here = z_ref[CP : CP + 1, :]
    prev = padded[CP : CP + 1, FR - 1 : 2 * FR - 1]
    before = padded[:CP, FR - 1 : 2 * FR - 1]
    after = padded[:CP, FR + 1 : 2 * FR + 1]
    image = banded + prev * (own - before) + here * (own - after)
    w_ref[...] = image
    u = apply_precond(pre_ref, image)
    u_ref[...] = jnp.concatenate([u, jnp.zeros((2, FR), F32)], axis=0)


def second_kernel(u_ref, right_ref, band_ref, r_ref, z_ref, w_ref, out_ref):
    ahead = jnp.concatenate([u_ref[...], right_ref[...]], axis=1)
    near = jnp.concatenate([jnp.zeros((8, 128), F32), ahead[:, : FR + 128]], axis=1)
    upper = banded_sums(band_ref, [near[j : j + 1] for j in range(CP)], range(7, 16), first=7)
    u, z, w, r = u_ref[:CP, :], z_ref[:CP, :], w_ref[...], r_ref[...]
    edge = z_ref[CP : CP + 1, :]
    step = u - ahead[:CP, 1 : FR + 1]
    lane = lax.broadcasted_iota(jnp.int32, (1, 128), 1)
    row = jnp.zeros((1, 128), F32)
    for at, term in enumerate((r * z, z * w, w * u, 2.0 * u * upper + edge * step * step)):
        total = jnp.sum(jnp.sum(term, axis=0, keepdims=True), axis=1, keepdims=True)
        row = row + jnp.where(lane == at, total, 0.0)
    out_ref[...] = jnp.broadcast_to(row, out_ref.shape)


def back_kernel(count_ref, pid_ref, fid_ref, jp_ref, jc_ref, z_ref, u_ref, *outs):
    parts = halves(jnp.concatenate([z_ref[...], u_ref[...]], axis=0))
    for j in range(GROUPS):
        b = block_at(GROUPS - 1 - j)
        at = lanes(b)
        used = used_row(count_ref[b])
        table = one_hot(fid_ref[:, at].astype(F32), FR)
        got = lax.dot_general(parts, table, (((1,), (0,)), ((), ())), preferred_element_type=F32)
        got = got[:16] + got[16:]
        terms = []
        for v in range(2):
            seen = got[v * 8 : v * 8 + CP]
            pair = [
                jnp.sum(jc_ref[a, :, at] * seen, axis=0, keepdims=True) * used for a in range(2)
            ]
            terms.append(jp_ref[0, :, at] * pair[0] + jp_ref[1, :, at] * pair[1])
        outs[j][...] = scatter_points(jnp.concatenate(terms, axis=0), pid_ref[:, at])


def undo_kernel(a_ref, b_ref, c_ref, d_ref, inv_ref, z_ref, u_ref):
    both = a_ref[...] + b_ref[...] + c_ref[...] + d_ref[...]
    z_ref[...] = jnp.sum(inv_ref[...] * both[None, :Q], axis=1)
    u_ref[...] = jnp.sum(inv_ref[...] * both[None, Q:], axis=1)


def final_kernel(g_ref, z_ref, u_ref, ps_ref, pz_ref, pu_ref, cam_ref, pt_ref):
    row = jnp.sum(g_ref[...], axis=0, keepdims=True)
    rz, zw, wu, uy = [row[:, i : i + 1] for i in range(4)]
    a0 = rz / zw
    inner = a0 * a0 * wu - rz
    beta = 1.0 + inner / rz
    curve = beta * beta * zw - 2.0 * beta * a0 * wu + a0 * a0 * uy
    a1 = inner / curve
    c0 = a0 + a1 * beta
    c1 = -a1 * a0
    cam_ref[...] = c0 * z_ref[:CP, :] + c1 * u_ref[:CP, :]
    pt_ref[...] = ps_ref[...] - c0 * pz_ref[...] - c1 * pu_ref[...]


def shifted(value, axis, step):
    count = lax.axis_size(axis)
    return lax.ppermute(value, axis, [(i, (i + step) % count) for i in range(count)])


def beside(value):
    count = lax.axis_size("frames")
    up = [(i, i + 1) for i in range(count - 1)]
    down = [(i + 1, i) for i in range(count - 1)]
    return lax.ppermute(value, "frames", up), lax.ppermute(value, "frames", down)


def sds(*shape):
    return jax.ShapeDtypeStruct(shape, F32)


def cost(flops, moved):
    return pl.CostEstimate(flops=flops, bytes_accessed=moved, transcendentals=0)


def plain(kernel, outs, args, name, smem=(), raw=(), scratch=(), est=None, params=LIMIT):
    space = lambda i: pltpu.SMEM if i in smem else pltpu.HBM if i in raw else pltpu.VMEM
    specs = [pl.BlockSpec(memory_space=space(i)) for i in range(len(args))]
    out_specs = jax.tree.map(lambda _: pl.BlockSpec(memory_space=pltpu.VMEM), outs)
    return pl.pallas_call(
        kernel,
        in_specs=specs,
        out_specs=out_specs,
        out_shape=outs,
        scratch_shapes=list(scratch),
        cost_estimate=est,
        compiler_params=params,
        name=name,
    )(*args)


def local(
    obs_count,
    obs_point,
    obs_frame,
    jac_cam,
    jac_point,
    residual,
    point_inv,
    band,
    edge_weight,
    precond,
):
    slots = obs_point.shape[0]
    pid = obs_point.reshape(1, slots)
    fid = obs_frame.reshape(1, slots)
    count = lax.axis_size("frames")
    edge = edge_weight.reshape(1, FR)
    bands = jnp.transpose(band, (1, 2, 0, 3))

    sums = plain(
        grad_kernel,
        [sds(Q, PT)] * GROUPS,
        (obs_count, pid, residual, jac_point),
        "point_grad",
        smem=(0,),
        raw=(1, 2, 3),
        scratch=[
            pltpu.VMEM((1, slots), jnp.int32),
            pltpu.VMEM((2, slots), F32),
            pltpu.VMEM((GROUPS, 2, Q, CAP), F32),
            pltpu.SemaphoreType.DMA((GROUPS + 2,)),
        ],
        est=cost(2 * 192 * 256 * 8192, 2 * 24 * 8192 * 4),
        params=None,
    )
    got = [shifted(sums[GROUPS - 1 - s], "points", s) for s in (3, 2, 1)] + [sums[GROUPS - 1]]
    solved = plain(
        solve_kernel, sds(Q, PT), (*got, point_inv), "point_solve", est=cost(2 * Q * Q * PT, Q * Q * PT * 4)
    )
    partial = ()
    for s in (0, 1, 3, 2):
        piece = shifted(solved, "points", s) if s else solved
        partial = (
            plain(
                functools.partial(rhs_kernel, -s),
                sds(CP, FR),
                (obs_count, pid, fid, residual, jac_point, jac_cam, *partial, piece),
                "camera_rhs",
                smem=(0,),
                est=cost(2 * 256 * 256 * 2048, 2 * 32 * 2048 * 4),
            ),
        )
    (partial,) = partial
    parts = [partial] + [shifted(partial, "points", s) for s in (1, 2, 3)]

    rhs, z = plain(
        start_kernel,
        [sds(CP, FR), sds(8, FR)],
        (*parts, precond, edge),
        "start",
        est=cost(20000, 100000),
    )
    z_left, z_right = beside(z)
    w, u = plain(
        first_kernel,
        [sds(CP, FR), sds(8, FR)],
        (z, z_left, z_right, bands, precond),
        "operator_one",
        est=cost(2 * 127 * 36 * 256, 127 * 36 * 256 * 4),
    )
    u_right = lax.ppermute(u, "frames", [(i + 1, i) for i in range(count - 1)])
    back = plain(
        back_kernel,
        [sds(2 * Q, PT)] * GROUPS,
        (obs_count, pid, fid, jac_point, jac_cam, z, u),
        "back_terms",
        smem=(0,),
        est=cost(2 * 400 * 256 * 8192, 2 * 32 * 8192 * 4),
    )
    returned = [shifted(back[GROUPS - 1 - s], "points", s) for s in (3, 2, 1)] + [back[GROUPS - 1]]
    gram = plain(
        second_kernel,
        sds(count, 128),
        (u, u_right, bands, rhs, z, w),
        "operator_two",
        est=cost(127 * 36 * 256, 127 * 18 * 256 * 4),
    )
    gram = lax.all_to_all(gram, "frames", split_axis=0, concat_axis=0, tiled=True)
    undo_z, undo_u = plain(
        undo_kernel,
        [sds(Q, PT)] * 2,
        (*returned, point_inv),
        "undo",
        est=cost(4 * Q * Q * PT, Q * Q * PT * 4),
    )
    camera_step, point_step = plain(
        final_kernel,
        [sds(CP, FR), sds(Q, PT)],
        (gram, z, u, solved, undo_z, undo_u),
        "final",
        est=cost(6 * Q * PT, 6 * Q * PT * 4),
    )
    return camera_step, point_step


def solution(mesh):
    placed = (
        P(("frames", "points")),
        P(("frames", "points")),
        P(("frames", "points")),
        P(None, None, ("frames", "points")),
        P(None, None, ("frames", "points")),
        P(None, ("frames", "points")),
        P(None, None, ("frames", "points")),
        P(None, None, None, "frames"),
        P("frames"),
        P(None, None, "frames"),
    )
    return jax.shard_map(
        local,
        mesh=mesh,
        in_specs=placed,
        out_specs=(P(None, "frames"), P(None, ("frames", "points"))),
        check_vma=False,
    )
```

time: 110 us -> 76.7 us (0.70)
  blocking collectives: 17.7 us -> 0 us
  Pallas kernels: 35.2 us -> 19.1 us
  local copies, waits for them, and re-layouts: 13.3 us -> 1.23 us
  starting transfers between devices: 26.9 us -> 33.8 us
  waiting for transfers between devices: 15.4 us -> 21.4 us
    pallas_call x5 -> x0, Pallas kernels: 25.7 us -> none  [the longest x3 17.8 us: call(): pl.pallas_call(kernel, grid_spec=pltpu.PrefetchScalarGridSpec(num_scalar_...]
    all_to_all x1 -> x0, blocking collectives: 17.7 us -> none  [local(): lax.all_to_all(gram, 'frames', split_axis=0, concat_axis=0, tiled=True)]
    unnamed x42 -> x25, local copies, waits for them, and re-layouts: 13.3 us -> 1.23 us
    pallas_call x3 -> x12, Pallas kernels: 9.45 us -> 19.1 us  [plain(): pl.pallas_call(kernel, in_specs=specs, out_specs=out_specs, out_shape=out...]
    all_to_all x0 -> x1, starting transfers between devices: none -> 9.57 us  [local(): lax.all_to_all(gram, 'frames', split_axis=0, concat_axis=0, tiled=True)]
    all_to_all x0 -> x1, waiting for transfers between devices: none -> 5.18 us  [local(): lax.all_to_all(gram, 'frames', split_axis=0, concat_axis=0, tiled=True)]
    ppermute x1, waiting for transfers between devices: 0.01 us -> 4.65 us  [local(): u_right = lax.ppermute(u, 'frames', [(i + 1, i) for i in range(count - 1)])]
    ppermute x12, waiting for transfers between devices: 14.6 us -> 10.8 us  [shifted(): lax.ppermute(value, axis, [(i, (i + step) % count) for i in range(count)])]
  transfers between devices with their start and end apart: 17 -> 16, of which waited for: 9 -> 9; matrix products, arithmetic and copies ran while one was open for 8% -> 0% of each run, Pallas kernels for 4% -> 9%
where the time goes in v2:
time: 76.7 us; the launch traced here: 76.4 us
  starting transfers between devices  33.8 us (44%)
  waiting for transfers between devices  21.4 us (28%)
  Pallas kernels  19.1 us (25%)
  local copies, waits for them, and re-layouts  1.23 us (2%)
  between operations  0.88 us (1%)
    pallas_call x12, Pallas kernels, plain(): pl.pallas_call(kernel, in_specs=specs, out_specs=out_specs, out_shape=out...  19.1 us
    ppermute x12, starting transfers between devices, shifted(): lax.ppermute(value, axis, [(i, (i + step) % count) for i in range(count)])  13 us
    ppermute x12, waiting for transfers between devices, shifted(): lax.ppermute(value, axis, [(i, (i + step) % count) for i in range(count)])  10.8 us
    all_to_all x1, starting transfers between devices, local(): lax.all_to_all(gram, 'frames', split_axis=0, concat_axis=0, tiled=True)  9.57 us
    ppermute x1, starting transfers between devices, beside(): lax.ppermute(value, 'frames', down)  6.09 us
    all_to_all x1, waiting for transfers between devices, local(): lax.all_to_all(gram, 'frames', split_axis=0, concat_axis=0, tiled=True)  5.18 us
    ppermute x1, waiting for transfers between devices, local(): u_right = lax.ppermute(u, 'frames', [(i + 1, i) for i in range(count - 1)])  4.65 us
    ppermute x1, starting transfers between devices, beside(): lax.ppermute(value, 'frames', up)  3.1 us
  transfers between devices with their start and end apart: 16, of which 9 were waited for; matrix products, arithmetic and copies ran while one was open for 0% of the time, Pallas kernels for 9%

profile of v2, /device:TPU:1, one launch (start us, length us, event | category | flops | bytes accessed | tf_op | source)
XLA Modules:
  0.0 76.4 jit_solution(4268908934257723479)
XLA Ops:
  0.7 5.5 %point_grad.1 = (f32[24,1024]{1,0:T(8,128)}, f32[24,1024]{1,0:T(8,128)}, f32[24,1024]{1,0:T(8,128)}, f32[24,1024]{1,0:T(8,128)}) custom-call(s32[4]{0:T(128)} %count_ref.11, s32[1,8192]{1,0:T(1,128)} %bitcast.12, f32[2,8192]{1,0:T(2,128)} %res_ref.7, f32[2,24,8192]{2,1,0:T(8,128)} %jp_ref.9), custom_call_target="tpu_custom_call" | custom-call | flops 805306368 | bytes 1572864 | tf_op jit(solution)/shard_map/point_grad/pallas_call | solution.py:286
  6.2 3.4 %collective-permute-start = (f32[24,1024]{1,0:T(8,128)}, f32[24,1024]{1,0:T(8,128)S(1)}, u32[]{:S(2)}, u32[]{:S(2)}) collective-permute-start(f32[24,1024]{1,0:T(8,128)} %get-tuple-element.16), channel_id=1, source_target_pairs={{0,3},{1,0},{2,1},{3,2},{4,7},{5,4},{6,5},{7,6},{8,11},{9,8},{10,9... | collective-permute-start | bytes 294920 | tf_op jit(solution)/shard_map/ppermute | solution.py:264
  9.6 0.5 collective-permute-start.1
  10.1 0.6 collective-permute-start.2
  10.7 0.8 %collective-permute-done.a_ref = f32[24,1024]{1,0:T(8,128)S(1)} collective-permute-done((f32[24,1024]{1,0:T(8,128)}, f32[24,1024]{1,0:T(8,128)S(1)}, u32[]{:S(2)}, u32[]{:S(2)}) %collective-permute-start) | collective-permute-done | bytes 98336 | tf_op jit(solution)/shard_map/ppermute | solution.py:264
  11.5 3.3 %collective-permute-done.1.b_ref = f32[24,1024]{1,0:T(8,128)S(1)} collective-permute-done((f32[24,1024]{1,0:T(8,128)}, f32[24,1024]{1,0:T(8,128)S(1)}, u32[]{:S(2)}, u32[]{:S(2)}) %collective-permute-start.1) | collective-permute-done | bytes 98336 | tf_op jit(solution)/shard_map/ppermute | solution.py:264
  14.9 2.7 %collective-permute-done.2.c_ref = f32[24,1024]{1,0:T(8,128)S(1)} collective-permute-done((f32[24,1024]{1,0:T(8,128)}, f32[24,1024]{1,0:T(8,128)S(1)}, u32[]{:S(2)}, u32[]{:S(2)}) %collective-permute-start.2) | collective-permute-done | bytes 98336 | tf_op jit(solution)/shard_map/ppermute | solution.py:264
  17.6 0.9 %copy-done.6 = f32[24,1024]{1,0:T(8,128)S(1)} copy-done((f32[24,1024]{1,0:T(8,128)S(1)}, f32[24,1024]{1,0:T(8,128)}, u32[]{:S(2)}) %copy-start.6) | copy-done | bytes 98328
  18.9 2.7 %collective-permute-start.4 = (f32[24,1024]{1,0:T(8,128)S(1)}, f32[24,1024]{1,0:T(8,128)S(1)}, u32[]{:S(2)}, u32[]{:S(2)}) collective-permute-start(f32[24,1024]{1,0:T(8,128)S(1)} %point_solve.1.rest_0_.ps_ref), channel_id=1, source_target_pairs={{0,3},{1,0},{2,1},{3,2},{4,7},{5,4},{6,5},{7,6},{8,11},{9,8},{10,9... | collective-permute-start | bytes 294920 | tf_op jit(solution)/shard_map/ppermute | solution.py:264
  21.9 1.3 %camera_rhs.4.rest_0_ = f32[6,256]{1,0:T(8,128)S(1)} custom-call(s32[4]{0:T(128)S(1)} %copy-done.7, s32[1,8192]{1,0:T(1,128)S(1)} %bitcast.13, s32[1,8192]{1,0:T(1,128)S(1)} %bitcast.18, f32[2,8192]{1,0:T(2,128)S(1)} %copy-done.2, f32[2,24,8192]{2,1,0:T(8,128)S(1)} %copy-done, f32[2,6,8192]{2,1,0:T(8,128)S(1)} %copy.20.jc_ref, ...), custom_call_target="tpu_custom_call" | custom-call | flops 268435456 | bytes 524288 | tf_op jit(solution)/shard_map/camera_rhs/pallas_call | solution.py:286
  23.2 0.4 collective-permute-done.3.rest_1_
  23.6 1.2 %camera_rhs.5.rest_0_ = f32[6,256]{1,0:T(8,128)S(1)} custom-call(s32[4]{0:T(128)S(1)} %copy-done.7, s32[1,8192]{1,0:T(1,128)S(1)} %bitcast.14, s32[1,8192]{1,0:T(1,128)S(1)} %bitcast.19, f32[2,8192]{1,0:T(2,128)S(1)} %copy-done.2, f32[2,24,8192]{2,1,0:T(8,128)S(1)} %copy-done, f32[2,6,8192]{2,1,0:T(8,128)S(1)} %copy.20.jc_ref, ...), custom_call_target="tpu_custom_call" | custom-call | flops 268435456 | bytes 524288 | tf_op jit(solution)/shard_map/camera_rhs/pallas_call | solution.py:286
  24.9 1.3 %camera_rhs.6.rest_0_ = f32[6,256]{1,0:T(8,128)S(1)} custom-call(s32[4]{0:T(128)S(1)} %copy-done.7, s32[1,8192]{1,0:T(1,128)S(1)} %bitcast.15, s32[1,8192]{1,0:T(1,128)S(1)} %bitcast.20, f32[2,8192]{1,0:T(2,128)S(1)} %copy-done.2, f32[2,24,8192]{2,1,0:T(8,128)S(1)} %copy-done, f32[2,6,8192]{2,1,0:T(8,128)S(1)} %copy.20.jc_ref, ...), custom_call_target="tpu_custom_call" | custom-call | flops 268435456 | bytes 524288 | tf_op jit(solution)/shard_map/camera_rhs/pallas_call | solution.py:286
  26.6 1.3 %camera_rhs.7.a_ref = f32[6,256]{1,0:T(8,128)S(1)} custom-call(s32[4]{0:T(128)S(1)} %copy-done.7, s32[1,8192]{1,0:T(1,128)S(1)} %bitcast.16, s32[1,8192]{1,0:T(1,128)S(1)} %bitcast.21, f32[2,8192]{1,0:T(2,128)S(1)} %copy-done.2, f32[2,24,8192]{2,1,0:T(8,128)S(1)} %copy-done, f32[2,6,8192]{2,1,0:T(8,128)S(1)} %copy.20.jc_ref, ...), custom_call_target="tpu_custom_call" | custom-call | flops 268435456 | bytes 524288 | tf_op jit(solution)/shard_map/camera_rhs/pallas_call | solution.py:286
  27.8 2.2 %collective-permute-start.8 = (f32[6,256]{1,0:T(8,128)S(1)}, f32[6,256]{1,0:T(8,128)S(1)}, u32[]{:S(2)}, u32[]{:S(2)}) collective-permute-start(f32[6,256]{1,0:T(8,128)S(1)} %camera_rhs.7.a_ref), channel_id=1, source_target_pairs={{0,3},{1,0},{2,1},{3,2},{4,7},{5,4},{6,5},{7,6},{8,11},{9,8},{10,9... | collective-permute-start | bytes 18440 | tf_op jit(solution)/shard_map/ppermute | solution.py:264
  30.2 0.8 %collective-permute-start.6 = (f32[6,256]{1,0:T(8,128)S(1)}, f32[6,256]{1,0:T(8,128)S(1)}, u32[]{:S(2)}, u32[]{:S(2)}) collective-permute-start(f32[6,256]{1,0:T(8,128)S(1)} %camera_rhs.7.a_ref), channel_id=1, source_target_pairs={{0,1},{1,2},{2,3},{3,0},{4,5},{5,6},{6,7},{7,4},{8,9},{9,10},{10,1... | collective-permute-start | bytes 18440 | tf_op jit(solution)/shard_map/ppermute | solution.py:264
  30.9 3.0 %collective-permute-done.7.c_ref = f32[6,256]{1,0:T(8,128)S(1)} collective-permute-done((f32[6,256]{1,0:T(8,128)S(1)}, f32[6,256]{1,0:T(8,128)S(1)}, u32[]{:S(2)}, u32[]{:S(2)}) %collective-permute-start.7) | collective-permute-done | bytes 6176 | tf_op jit(solution)/shard_map/ppermute | solution.py:264
  34.0 6.1 %collective-permute-start.10 = (f32[8,256]{1,0:T(8,128)S(1)}, f32[8,256]{1,0:T(8,128)S(1)}, u32[]{:S(2)}, u32[]{:S(2)}) collective-permute-start(f32[8,256]{1,0:T(8,128)S(1)} %get-tuple-element.20.z_ref), channel_id=1, source_target_pairs={{4,0},{8,4},{12,8},{16,12},{20,16},{24,20},{28,24},{32,28},{36,32}... | collective-permute-start | bytes 24584 | tf_op jit(solution)/shard_map/ppermute | solution.py:271
  40.1 3.1 %collective-permute-start.9 = (f32[8,256]{1,0:T(8,128)S(1)}, f32[8,256]{1,0:T(8,128)S(1)}, u32[]{:S(2)}, u32[]{:S(2)}) collective-permute-start(f32[8,256]{1,0:T(8,128)S(1)} %get-tuple-element.20.z_ref), channel_id=1, source_target_pairs={{0,4},{4,8},{8,12},{12,16},{16,20},{20,24},{24,28},{28,32},{32,36}... | collective-permute-start | bytes 24584 | tf_op jit(solution)/shard_map/ppermute | solution.py:271
  43.2 0.8 collective-permute-done.9.left_ref
  44.0 0.8 %operator_one.1 = (f32[6,256]{1,0:T(8,128)S(1)}, f32[8,256]{1,0:T(8,128)S(1)}) custom-call(f32[8,256]{1,0:T(8,128)S(1)} %get-tuple-element.20.z_ref, f32[8,256]{1,0:T(8,128)S(1)} %collective-permute-done.9.left_ref, f32[8,256]{1,0:T(8,128)S(1)} %collective-permute-done.10.right_ref, f32[6,6,127,256]{3,2,1,0:T(8,128)S(1)} %bitcast.10, f32[6,6,256]{2,1,0:T(8,128)S(1)} %copy-done.5), custom_call_target="tpu_custom_call" | custom-call | flops 2340864 | bytes 4681728 | tf_op jit(solution)/shard_map/operator_one/pallas_call | solution.py:286
  44.8 3.7 %back_terms.1 = (f32[48,1024]{1,0:T(8,128)}, f32[48,1024]{1,0:T(8,128)}, f32[48,1024]{1,0:T(8,128)}, f32[48,1024]{1,0:T(8,128)S(1)}) custom-call(s32[4]{0:T(128)S(1)} %copy-done.7, s32[1,8192]{1,0:T(1,128)S(1)} %bitcast.17, s32[1,8192]{1,0:T(1,128)S(1)} %bitcast.22, f32[2,24,8192]{2,1,0:T(8,128)S(1)} %copy-done, f32[2,6,8192]{2,1,0:T(8,128)S(1)} %copy.20.jc_ref, ...), custom_call_target="tpu_custom_call" | custom-call | flops 1677721600 | bytes 2097152 | tf_op jit(solution)/shard_map/back_terms/pallas_call | solution.py:286
  48.5 0.5 collective-permute-start.12
  49.0 1.2 %collective-permute-start.13 = (f32[48,1024]{1,0:T(8,128)}, f32[48,1024]{1,0:T(8,128)}, u32[]{:S(2)}, u32[]{:S(2)}) collective-permute-start(f32[48,1024]{1,0:T(8,128)} %get-tuple-element.25), channel_id=1, source_target_pairs={{0,2},{1,3},{2,0},{3,1},{4,6},{5,7},{6,4},{7,5},{8,10},{9,11},{10,... | collective-permute-start | bytes 589832 | tf_op jit(solution)/shard_map/ppermute | solution.py:264
  50.2 0.9 %collective-permute-start.14 = (f32[48,1024]{1,0:T(8,128)}, f32[48,1024]{1,0:T(8,128)}, u32[]{:S(2)}, u32[]{:S(2)}) collective-permute-start(f32[48,1024]{1,0:T(8,128)} %get-tuple-element.26), channel_id=1, source_target_pairs={{0,1},{1,2},{2,3},{3,0},{4,5},{5,6},{6,7},{7,4},{8,9},{9,10},{10,1... | collective-permute-start | bytes 589832 | tf_op jit(solution)/shard_map/ppermute | solution.py:264
  51.1 2.1 %collective-permute-start.11 = (f32[8,256]{1,0:T(8,128)S(1)}, f32[8,256]{1,0:T(8,128)S(1)}, u32[]{:S(2)}, u32[]{:S(2)}) collective-permute-start(f32[8,256]{1,0:T(8,128)S(1)} %get-tuple-element.21.u_ref), channel_id=1, source_target_pairs={{4,0},{8,4},{12,8},{16,12},{20,16},{24,20},{28,24},{32,28},{36,32}... | collective-permute-start | bytes 24584 | tf_op jit(solution)/shard_map/ppermute | solution.py:368
  53.2 4.7 %collective-permute-done.11.right_ref = f32[8,256]{1,0:T(8,128)S(1)} collective-permute-done((f32[8,256]{1,0:T(8,128)S(1)}, f32[8,256]{1,0:T(8,128)S(1)}, u32[]{:S(2)}, u32[]{:S(2)}) %collective-permute-start.11) | collective-permute-done | bytes 8224 | tf_op jit(solution)/shard_map/ppermute | solution.py:368
  57.8 1.3 %operator_two.1 = f32[32,128]{1,0:T(8,128)} custom-call(f32[8,256]{1,0:T(8,128)S(1)} %get-tuple-element.21.u_ref, f32[8,256]{1,0:T(8,128)S(1)} %collective-permute-done.11.right_ref, f32[6,6,127,256]{3,2,1,0:T(8,128)S(1)} %bitcast.11, f32[6,256]{1,0:T(8,128)S(1)} %get-tuple-element.22.r_ref, f32[8,256]{1,0:T(8,128)S(1)} %get-tuple-element.20.z_ref, ...), custom_call_target="tpu_custom_call" | custom-call | flops 1170432 | bytes 2340864 | tf_op jit(solution)/shard_map/operator_two/pallas_call | solution.py:286
  59.1 9.6 %all-to-all-start = ((f32[32,1,128]{2,1,0:T(1,128)}), f32[32,1,128]{2,1,0:T(1,128)S(1)}, u32[]{:S(2)}, u32[]{:S(2)}) async-start(f32[32,1,128]{2,1,0:T(1,128)} %bitcast.5), calls=%async_computation | async-start | bytes 32768 | tf_op jit(solution)/shard_map/all_to_all | solution.py:385
  68.7 1.7 %undo.1 = (f32[24,1024]{1,0:T(8,128)S(1)}, f32[24,1024]{1,0:T(8,128)S(1)}) custom-call(f32[48,1024]{1,0:T(8,128)S(1)} %collective-permute-done.12.a_ref, f32[48,1024]{1,0:T(8,128)} %collective-permute-done.13.b_ref, f32[48,1024]{1,0:T(8,128)} %collective-permute-done.14.c_ref, f32[48,1024]{1,0:T(8,128)S(1)} %get-tuple-element.27.d_ref, ...), custom_call_target="tpu_custom_call" | custom-call | flops 2359296 | bytes 2359296 | tf_op jit(solution)/shard_map/undo/pallas_call | solution.py:286
  70.4 5.2 %all-to-all-done = f32[32,1,128]{2,1,0:T(1,128)S(1)} async-done(((f32[32,1,128]{2,1,0:T(1,128)}), f32[32,1,128]{2,1,0:T(1,128)S(1)}, u32[]{:S(2)}, u32[]{:S(2)}) %all-to-all-start) | async-done | bytes 16416 | tf_op jit(solution)/shard_map/all_to_all | solution.py:385
  75.6 0.8 %final.1 = (f32[6,256]{1,0:T(8,128)}, f32[24,1024]{1,0:T(8,128)}) custom-call(f32[32,128]{1,0:T(8,128)S(1)} %bitcast.23, f32[8,256]{1,0:T(8,128)S(1)} %get-tuple-element.20.z_ref, f32[8,256]{1,0:T(8,128)S(1)} %get-tuple-element.21.u_ref, f32[24,1024]{1,0:T(8,128)S(1)} %point_solve.1.rest_0_.ps_ref, f32[24,1024]{1,0:T(8,128)S(1)} %get-tuple-element.28.pz_ref, ...), custom_call_target="tpu_custom_call" | custom-call | flops 147456 | bytes 589824 | tf_op jit(solution)/shard_map/final/pallas_call | solution.py:286
  (38 shorter events, 1.4 us)
Async XLA Ops:
  0.6 17.0 %copy-start.1 = (f32[24,24,1024]{2,1,0:T(8,128)S(1)}, f32[24,24,1024]{2,1,0:T(8,128)}, u32[]{:S(2)}) copy-start(f32[24,24,1024]{2,1,0:T(8,128)} %inv_ref.3) | copy-start | bytes 7077892
  0.6 21.2 %copy-start.7 = (s32[4]{0:T(128)S(1)}, s32[4]{0:T(128)}, u32[]{:S(2)}) copy-start(s32[4]{0:T(128)} %count_ref.11) | copy-start | bytes 52
  0.6 43.4 %slice-start = ((s8[4718592]{0:T(1024)(128)(4,1)}), s8[524288]{0:T(1024)(128)(4,1)S(1)}, s32[]{:S(2)}) async-start(s8[4718592]{0:T(1024)(128)(4,1)} %bitcast.8), calls=%async_computation.1 | async-start | bytes 1048576
  6.2 15.7 %copy-start = (f32[2,24,8192]{2,1,0:T(8,128)S(1)}, f32[2,24,8192]{2,1,0:T(8,128)}, u32[]{:S(2)}) copy-start(f32[2,24,8192]{2,1,0:T(8,128)} %jp_ref.9) | copy-start | bytes 4718596
  6.2 15.7 %copy-start.2 = (f32[2,8192]{1,0:T(2,128)S(1)}, f32[2,8192]{1,0:T(2,128)}, u32[]{:S(2)}) copy-start(f32[2,8192]{1,0:T(2,128)} %res_ref.7) | copy-start | bytes 196612
  6.2 15.7 %copy-start.3 = (s32[8192]{0:T(1024)S(1)}, s32[8192]{0:T(1024)}, u32[]{:S(2)}) copy-start(s32[8192]{0:T(1024)} %param.11) | copy-start | bytes 98308
  6.2 15.7 %copy-start.4 = (s32[8192]{0:T(1024)S(1)}, s32[8192]{0:T(1024)}, u32[]{:S(2)}) copy-start(s32[8192]{0:T(1024)} %param.12) | copy-start | bytes 98308
  6.2 5.3 %collective-permute-start = (f32[24,1024]{1,0:T(8,128)}, f32[24,1024]{1,0:T(8,128)S(1)}, u32[]{:S(2)}, u32[]{:S(2)}) collective-permute-start(f32[24,1024]{1,0:T(8,128)} %get-tuple-element.16), channel_id=1, source_target_pairs={{0,3},{1,0},{2,1},{3,2},{4,7},{5,4},{6,5},{7,6},{8,11},{9,8},{10,9... | collective-permute-start | bytes 294920 | tf_op jit(solution)/shard_map/ppermute | solution.py:264
  9.6 5.3 %collective-permute-start.1 = (f32[24,1024]{1,0:T(8,128)}, f32[24,1024]{1,0:T(8,128)S(1)}, u32[]{:S(2)}, u32[]{:S(2)}) collective-permute-start(f32[24,1024]{1,0:T(8,128)} %get-tuple-element.17), channel_id=1, source_target_pairs={{0,2},{1,3},{2,0},{3,1},{4,6},{5,7},{6,4},{7,5},{8,10},{9,11},{10,... | collective-permute-start | bytes 294920 | tf_op jit(solution)/shard_map/ppermute | solution.py:264
  10.1 7.5 %collective-permute-start.2 = (f32[24,1024]{1,0:T(8,128)}, f32[24,1024]{1,0:T(8,128)S(1)}, u32[]{:S(2)}, u32[]{:S(2)}) collective-permute-start(f32[24,1024]{1,0:T(8,128)} %get-tuple-element.18), channel_id=1, source_target_pairs={{0,1},{1,2},{2,3},{3,0},{4,5},{5,6},{6,7},{7,4},{8,9},{9,10},{10,1... | collective-permute-start | bytes 294920 | tf_op jit(solution)/shard_map/ppermute | solution.py:264
  17.6 0.9 %copy-start.6 = (f32[24,1024]{1,0:T(8,128)S(1)}, f32[24,1024]{1,0:T(8,128)}, u32[]{:S(2)}) copy-start(f32[24,1024]{1,0:T(8,128)} %get-tuple-element.19.d_ref) | copy-start | bytes 294916
  18.5 3.1 %copy-start.9 = (f32[2,6,8192]{2,0,1:T(2,128)S(1)}, f32[2,6,8192]{2,0,1:T(2,128)}, u32[]{:S(2)}) copy-start(f32[2,6,8192]{2,0,1:T(2,128)} %param.13) | copy-start | bytes 1179652
  18.8 4.7 %collective-permute-start.3 = (f32[24,1024]{1,0:T(8,128)S(1)}, f32[24,1024]{1,0:T(8,128)S(1)}, u32[]{:S(2)}, u32[]{:S(2)}) collective-permute-start(f32[24,1024]{1,0:T(8,128)S(1)} %point_solve.1.rest_0_.ps_ref), channel_id=1, source_target_pairs={{0,1},{1,2},{2,3},{3,0},{4,5},{5,6},{6,7},{7,4},{8,9},{9,10},{10,1... | collective-permute-start | bytes 294920 | tf_op jit(solution)/shard_map/ppermute | solution.py:264
  18.9 6.0 %collective-permute-start.4 = (f32[24,1024]{1,0:T(8,128)S(1)}, f32[24,1024]{1,0:T(8,128)S(1)}, u32[]{:S(2)}, u32[]{:S(2)}) collective-permute-start(f32[24,1024]{1,0:T(8,128)S(1)} %point_solve.1.rest_0_.ps_ref), channel_id=1, source_target_pairs={{0,3},{1,0},{2,1},{3,2},{4,7},{5,4},{6,5},{7,6},{8,11},{9,8},{10,9... | collective-permute-start | bytes 294920 | tf_op jit(solution)/shard_map/ppermute | solution.py:264
  21.6 5.0 %collective-permute-start.5 = (f32[24,1024]{1,0:T(8,128)S(1)}, f32[24,1024]{1,0:T(8,128)S(1)}, u32[]{:S(2)}, u32[]{:S(2)}) collective-permute-start(f32[24,1024]{1,0:T(8,128)S(1)} %point_solve.1.rest_0_.ps_ref), channel_id=1, source_target_pairs={{0,2},{1,3},{2,0},{3,1},{4,6},{5,7},{6,4},{7,5},{8,10},{9,11},{10,... | collective-permute-start | bytes 294920 | tf_op jit(solution)/shard_map/ppermute | solution.py:264
  21.9 22.1 %slice-start.1 = ((s8[4718592]{0:T(1024)(128)(4,1)}), s8[4194304]{0:T(1024)(128)(4,1)S(1)}, s32[]{:S(2)}) async-start(s8[4718592]{0:T(1024)(128)(4,1)} %bitcast.8), calls=%async_computation.2 | async-start | bytes 8388608
  24.8 9.1 %copy-start.5 = (f32[6,6,256]{2,1,0:T(8,128)S(1)}, f32[6,6,256]{2,1,0:T(8,128)}, u32[]{:S(2)}) copy-start(f32[6,6,256]{2,1,0:T(8,128)} %pre_ref.3) | copy-start | bytes 110596
  24.8 9.1 %copy-start.8 = (f32[256]{0:T(256)S(1)}, f32[256]{0:T(256)}, u32[]{:S(2)}) copy-start(f32[256]{0:T(256)} %param.18) | copy-start | bytes 3076
  27.8 3.1 %collective-permute-start.8 = (f32[6,256]{1,0:T(8,128)S(1)}, f32[6,256]{1,0:T(8,128)S(1)}, u32[]{:S(2)}, u32[]{:S(2)}) collective-permute-start(f32[6,256]{1,0:T(8,128)S(1)} %camera_rhs.7.a_ref), channel_id=1, source_target_pairs={{0,3},{1,0},{2,1},{3,2},{4,7},{5,4},{6,5},{7,6},{8,11},{9,8},{10,9... | collective-permute-start | bytes 18440 | tf_op jit(solution)/shard_map/ppermute | solution.py:264
  30.0 4.0 %collective-permute-start.7 = (f32[6,256]{1,0:T(8,128)S(1)}, f32[6,256]{1,0:T(8,128)S(1)}, u32[]{:S(2)}, u32[]{:S(2)}) collective-permute-start(f32[6,256]{1,0:T(8,128)S(1)} %camera_rhs.7.a_ref), channel_id=1, source_target_pairs={{0,2},{1,3},{2,0},{3,1},{4,6},{5,7},{6,4},{7,5},{8,10},{9,11},{10,... | collective-permute-start | bytes 18440 | tf_op jit(solution)/shard_map/ppermute | solution.py:264
  30.2 3.8 %collective-permute-start.6 = (f32[6,256]{1,0:T(8,128)S(1)}, f32[6,256]{1,0:T(8,128)S(1)}, u32[]{:S(2)}, u32[]{:S(2)}) collective-permute-start(f32[6,256]{1,0:T(8,128)S(1)} %camera_rhs.7.a_ref), channel_id=1, source_target_pairs={{0,1},{1,2},{2,3},{3,0},{4,5},{5,6},{6,7},{7,4},{8,9},{9,10},{10,1... | collective-permute-start | bytes 18440 | tf_op jit(solution)/shard_map/ppermute | solution.py:264
  34.0 9.2 %collective-permute-start.10 = (f32[8,256]{1,0:T(8,128)S(1)}, f32[8,256]{1,0:T(8,128)S(1)}, u32[]{:S(2)}, u32[]{:S(2)}) collective-permute-start(f32[8,256]{1,0:T(8,128)S(1)} %get-tuple-element.20.z_ref), channel_id=1, source_target_pairs={{4,0},{8,4},{12,8},{16,12},{20,16},{24,20},{28,24},{32,28},{36,32}... | collective-permute-start | bytes 24584 | tf_op jit(solution)/shard_map/ppermute | solution.py:271
  40.1 3.9 %collective-permute-start.9 = (f32[8,256]{1,0:T(8,128)S(1)}, f32[8,256]{1,0:T(8,128)S(1)}, u32[]{:S(2)}, u32[]{:S(2)}) collective-permute-start(f32[8,256]{1,0:T(8,128)S(1)} %get-tuple-element.20.z_ref), channel_id=1, source_target_pairs={{0,4},{4,8},{8,12},{12,16},{16,20},{20,24},{24,28},{28,32},{32,36}... | collective-permute-start | bytes 24584 | tf_op jit(solution)/shard_map/ppermute | solution.py:271
  48.5 20.2 %collective-permute-start.12 = (f32[48,1024]{1,0:T(8,128)}, f32[48,1024]{1,0:T(8,128)S(1)}, u32[]{:S(2)}, u32[]{:S(2)}) collective-permute-start(f32[48,1024]{1,0:T(8,128)} %get-tuple-element.24), channel_id=1, source_target_pairs={{0,3},{1,0},{2,1},{3,2},{4,7},{5,4},{6,5},{7,6},{8,11},{9,8},{10,9... | collective-permute-start | bytes 589832 | tf_op jit(solution)/shard_map/ppermute | solution.py:264
  49.0 19.7 %collective-permute-start.13 = (f32[48,1024]{1,0:T(8,128)}, f32[48,1024]{1,0:T(8,128)}, u32[]{:S(2)}, u32[]{:S(2)}) collective-permute-start(f32[48,1024]{1,0:T(8,128)} %get-tuple-element.25), channel_id=1, source_target_pairs={{0,2},{1,3},{2,0},{3,1},{4,6},{5,7},{6,4},{7,5},{8,10},{9,11},{10,... | collective-permute-start | bytes 589832 | tf_op jit(solution)/shard_map/ppermute | solution.py:264
  50.2 18.5 %collective-permute-start.14 = (f32[48,1024]{1,0:T(8,128)}, f32[48,1024]{1,0:T(8,128)}, u32[]{:S(2)}, u32[]{:S(2)}) collective-permute-start(f32[48,1024]{1,0:T(8,128)} %get-tuple-element.26), channel_id=1, source_target_pairs={{0,1},{1,2},{2,3},{3,0},{4,5},{5,6},{6,7},{7,4},{8,9},{9,10},{10,1... | collective-permute-start | bytes 589832 | tf_op jit(solution)/shard_map/ppermute | solution.py:264
  51.1 6.7 %collective-permute-start.11 = (f32[8,256]{1,0:T(8,128)S(1)}, f32[8,256]{1,0:T(8,128)S(1)}, u32[]{:S(2)}, u32[]{:S(2)}) collective-permute-start(f32[8,256]{1,0:T(8,128)S(1)} %get-tuple-element.21.u_ref), channel_id=1, source_target_pairs={{4,0},{8,4},{12,8},{16,12},{20,16},{24,20},{28,24},{32,28},{36,32}... | collective-permute-start | bytes 24584 | tf_op jit(solution)/shard_map/ppermute | solution.py:368
  59.1 16.5 %all-to-all-start = ((f32[32,1,128]{2,1,0:T(1,128)}), f32[32,1,128]{2,1,0:T(1,128)S(1)}, u32[]{:S(2)}, u32[]{:S(2)}) async-start(f32[32,1,128]{2,1,0:T(1,128)} %bitcast.5), calls=%async_computation | async-start | bytes 32768 | tf_op jit(solution)/shard_map/all_to_all | solution.py:385

commit v3 on v2

--- a/solution.py
+++ b/solution.py
@@ -6,6 +6,7 @@
 from jax.experimental import pallas as pl
 from jax.experimental.pallas import tpu as pltpu
 from jax.sharding import PartitionSpec as P
+
 
 F32 = jnp.float32
 BF16 = jnp.bfloat16
@@ -44,9 +45,9 @@
     return hi.astype(F32), lo.astype(F32)
 
 
-def used_row(count):
-    lane = lax.broadcasted_iota(jnp.int32, (1, CAP), 1)
-    return (lane < count).astype(F32)
+def used_or(ids, count, other):
+    lane = lax.broadcasted_iota(jnp.int32, ids.shape, 1)
+    return jnp.where(lane < count, ids, other)
 
 
 def scatter_points(terms, ids):
@@ -91,27 +92,53 @@
     return pl.ds(pl.multiple_of(b * CAP, CAP), CAP)
 
 
-def grad_kernel(count_ref, ids_hbm, res_hbm, jp_hbm, *rest):
-    outs, (ids_ref, res_ref, jp_ref, sems) = rest[:GROUPS], rest[GROUPS:]
-    small = [
-        pltpu.make_async_copy(ids_hbm, ids_ref, sems.at[GROUPS]),
-        pltpu.make_async_copy(res_hbm, res_ref, sems.at[GROUPS + 1]),
-    ]
-    blocks = [block_at(GROUPS - 1 - j) for j in range(GROUPS)]
-    large = [
-        pltpu.make_async_copy(jp_hbm.at[:, :, lanes(b)], jp_ref.at[j], sems.at[j])
-        for j, b in enumerate(blocks)
-    ]
-    for copy in small + large:
+def fetch(pairs, sems):
+    copies = [pltpu.make_async_copy(src, dst, sems.at[i]) for i, (src, dst) in enumerate(pairs)]
+    for copy in copies:
         copy.start()
-    for copy in small:
+    return copies
+
+
+def grad_kernel(count_hbm, ids_hbm, res_hbm, jp_hbm, *rest):
+    far = GROUPS - 1
+    outs, (count_ref, ids_ref, res_ref, jp_ref, sems) = rest[:far], rest[far:]
+    blocks = [block_at(GROUPS - 1 - j) for j in range(far)]
+    large = [(jp_hbm.at[:, :, lanes(b)], jp_ref.at[j]) for j, b in enumerate(blocks)]
+    small = [(count_hbm, count_ref), (ids_hbm, ids_ref), (res_hbm, res_ref)]
+    copies = fetch(small + large, sems)
+    for copy in copies[:3]:
         copy.wait()
     for j, b in enumerate(blocks):
         at = lanes(b)
-        large[j].wait()
-        res = res_ref[:, at] * used_row(count_ref[b])
-        terms = jp_ref[j, 0] * res[0:1] + jp_ref[j, 1] * res[1:2]
-        outs[j][...] = scatter_points(terms, ids_ref[:, at])
+        copies[3 + j].wait()
+        terms = jp_ref[j, 0] * res_ref[0:1, at] + jp_ref[j, 1] * res_ref[1:2, at]
+        outs[j][...] = scatter_points(terms, used_or(ids_ref[:, at], count_ref[b], PT))
+
+
+def own_kernel(
+    after_ref, count_hbm, pid_hbm, fid_hbm, res_hbm, jp_hbm, out_ref, pid_out, fid_out,
+    count_ref, res_ref, jp_ref, sems,
+):
+    b = block_at(0)
+    at = lanes(b)
+    copies = fetch(
+        [
+            (count_hbm, count_ref),
+            (pid_hbm, pid_out),
+            (fid_hbm, fid_out),
+            (res_hbm.at[:, at], res_ref),
+            (jp_hbm.at[:, :, at], jp_ref),
+        ],
+        sems,
+    )
+    for copy in copies:
+        copy.wait()
+    for g in range(GROUPS):
+        here = slice(g * CAP, (g + 1) * CAP)
+        pid_out[:, here] = used_or(pid_out[:, here], count_ref[g], PT)
+        fid_out[:, here] = used_or(fid_out[:, here], count_ref[g], FR)
+    terms = jp_ref[0] * res_ref[0:1, :] + jp_ref[1] * res_ref[1:2, :]
+    out_ref[...] = scatter_points(terms, pid_out[:, at])
 
 
 def solve_kernel(a_ref, b_ref, c_ref, d_ref, inv_ref, out_ref):
@@ -119,14 +146,13 @@
     out_ref[...] = jnp.sum(inv_ref[...] * grad[None], axis=1)
 
 
-def rhs_kernel(turn, count_ref, pid_ref, fid_ref, res_ref, jp_ref, jc_ref, *rest):
+def rhs_kernel(turn, pid_ref, fid_ref, res_ref, jp_ref, jc_ref, *rest):
     solved_ref, out_ref = rest[-2:]
     b = block_at(turn)
     at = lanes(b)
-    used = used_row(count_ref[b])
     seen = gather_points(solved_ref[...], pid_ref[:, at])
     remain = [
-        (res_ref[a : a + 1, at] - jnp.sum(jp_ref[a, :, at] * seen, axis=0, keepdims=True)) * used
+        res_ref[a : a + 1, at] - jnp.sum(jp_ref[a, :, at] * seen, axis=0, keepdims=True)
         for a in range(2)
     ]
     cam = jc_ref[0, :, at] * remain[0] + jc_ref[1, :, at] * remain[1]
@@ -153,7 +179,7 @@
     z_ref[...] = jnp.concatenate([z, edge, jnp.zeros((1, FR), F32)], axis=0)
 
 
-def steps_of(row, width):
+def steps_of(row):
     n = row.shape[1]
     sub = lax.broadcasted_iota(jnp.int32, (8, n), 0)
     x = jnp.broadcast_to(row, (8, n))
@@ -166,7 +192,7 @@
     totals = [None] * CP
     ends = [None] * CP
     for j in range(CP):
-        stepped = steps_of(rows[j], 0)
+        stepped = steps_of(rows[j])
         for t in tiles:
             at = 128 - REACH + 8 * t
             shifted = stepped[:, at : at + FR]
@@ -220,26 +246,24 @@
     out_ref[...] = jnp.broadcast_to(row, out_ref.shape)
 
 
-def back_kernel(count_ref, pid_ref, fid_ref, jp_ref, jc_ref, z_ref, u_ref, *outs):
+def back_kernel(pid_ref, fid_ref, jp_ref, jc_ref, z_ref, u_ref, *outs):
     parts = halves(jnp.concatenate([z_ref[...], u_ref[...]], axis=0))
     for j in range(GROUPS):
         b = block_at(GROUPS - 1 - j)
         at = lanes(b)
-        used = used_row(count_ref[b])
         table = one_hot(fid_ref[:, at].astype(F32), FR)
         got = lax.dot_general(parts, table, (((1,), (0,)), ((), ())), preferred_element_type=F32)
         got = got[:16] + got[16:]
         terms = []
         for v in range(2):
             seen = got[v * 8 : v * 8 + CP]
-            pair = [
-                jnp.sum(jc_ref[a, :, at] * seen, axis=0, keepdims=True) * used for a in range(2)
-            ]
+            pair = [jnp.sum(jc_ref[a, :, at] * seen, axis=0, keepdims=True) for a in range(2)]
             terms.append(jp_ref[0, :, at] * pair[0] + jp_ref[1, :, at] * pair[1])
         outs[j][...] = scatter_points(jnp.concatenate(terms, axis=0), pid_ref[:, at])
 
 
-def undo_kernel(a_ref, b_ref, c_ref, d_ref, inv_ref, z_ref, u_ref):
+def undo_kernel(a_ref, b_ref, c_ref, d_ref, inv_hbm, z_ref, u_ref, inv_ref, sem):
+    pltpu.async_copy(inv_hbm, inv_ref, sem).wait()
     both = a_ref[...] + b_ref[...] + c_ref[...] + d_ref[...]
     z_ref[...] = jnp.sum(inv_ref[...] * both[None, :Q], axis=1)
     u_ref[...] = jnp.sum(inv_ref[...] * both[None, Q:], axis=1)
@@ -279,9 +303,10 @@
     return pl.CostEstimate(flops=flops, bytes_accessed=moved, transcendentals=0)
 
 
-def plain(kernel, outs, args, name, smem=(), raw=(), scratch=(), est=None, params=LIMIT):
+def plain(kernel, outs, args, smem=(), raw=(), scratch=(), est=None, ):
     space = lambda i: pltpu.SMEM if i in smem else pltpu.HBM if i in raw else pltpu.VMEM
     specs = [pl.BlockSpec(memory_space=space(i)) for i in range(len(args))]
+    args = [pltpu.with_memory_space_constraint(x, pltpu.HBM) if i in raw else x for i, x in enumerate(args)]
     out_specs = jax.tree.map(lambda _: pl.BlockSpec(memory_space=pltpu.VMEM), outs)
     return pl.pallas_call(
         kernel,
@@ -290,12 +315,11 @@
         out_shape=outs,
         scratch_shapes=list(scratch),
         cost_estimate=est,
-        compiler_params=params,
-        name=name,
+        compiler_params=LIMIT,
     )(*args)
 
 
-def local(
+def step(
     obs_count,
     obs_point,
     obs_frame,
@@ -314,25 +338,37 @@
     edge = edge_weight.reshape(1, FR)
     bands = jnp.transpose(band, (1, 2, 0, 3))
 
-    sums = plain(
+    far = plain(
         grad_kernel,
-        [sds(Q, PT)] * GROUPS,
+        [sds(Q, PT)] * (GROUPS - 1),
         (obs_count, pid, residual, jac_point),
-        "point_grad",
-        smem=(0,),
-        raw=(1, 2, 3),
+        raw=(0, 1, 2, 3),
         scratch=[
+            pltpu.SMEM((GROUPS,), jnp.int32),
             pltpu.VMEM((1, slots), jnp.int32),
             pltpu.VMEM((2, slots), F32),
-            pltpu.VMEM((GROUPS, 2, Q, CAP), F32),
+            pltpu.VMEM((GROUPS - 1, 2, Q, CAP), F32),
             pltpu.SemaphoreType.DMA((GROUPS + 2,)),
         ],
-        est=cost(2 * 192 * 256 * 8192, 2 * 24 * 8192 * 4),
-        params=None,
-    )
-    got = [shifted(sums[GROUPS - 1 - s], "points", s) for s in (3, 2, 1)] + [sums[GROUPS - 1]]
+        est=cost(2 * 192 * 256 * 6144, 2 * 24 * 6144 * 4),
+    )
+    ints = jax.ShapeDtypeStruct((1, slots), jnp.int32)
+    near, pid, fid = plain(
+        own_kernel,
+        [sds(Q, PT), ints, ints],
+        (far[0], obs_count, pid, fid, residual, jac_point),
+        raw=(1, 2, 3, 4, 5),
+        scratch=[
+            pltpu.SMEM((GROUPS,), jnp.int32),
+            pltpu.VMEM((2, CAP), F32),
+            pltpu.VMEM((2, Q, CAP), F32),
+            pltpu.SemaphoreType.DMA((5,)),
+        ],
+        est=cost(2 * 192 * 256 * 2048, 2 * 24 * 2048 * 4),
+    )
+    got = [shifted(far[GROUPS - 1 - s], "points", s) for s in (3, 2, 1)] + [near]
     solved = plain(
-        solve_kernel, sds(Q, PT), (*got, point_inv), "point_solve", est=cost(2 * Q * Q * PT, Q * Q * PT * 4)
+        solve_kernel, sds(Q, PT), (*got, point_inv), est=cost(2 * Q * Q * PT, Q * Q * PT * 4)
     )
     partial = ()
     for s in (0, 1, 3, 2):
@@ -341,9 +377,7 @@
             plain(
                 functools.partial(rhs_kernel, -s),
                 sds(CP, FR),
-                (obs_count, pid, fid, residual, jac_point, jac_cam, *partial, piece),
-                "camera_rhs",
-                smem=(0,),
+                (pid, fid, residual, jac_point, jac_cam, *partial, piece),
                 est=cost(2 * 256 * 256 * 2048, 2 * 32 * 2048 * 4),
             ),
         )
@@ -351,27 +385,20 @@
     parts = [partial] + [shifted(partial, "points", s) for s in (1, 2, 3)]
 
     rhs, z = plain(
-        start_kernel,
-        [sds(CP, FR), sds(8, FR)],
-        (*parts, precond, edge),
-        "start",
-        est=cost(20000, 100000),
+        start_kernel, [sds(CP, FR), sds(8, FR)], (*parts, precond, edge), est=cost(20000, 100000)
     )
     z_left, z_right = beside(z)
     w, u = plain(
         first_kernel,
         [sds(CP, FR), sds(8, FR)],
         (z, z_left, z_right, bands, precond),
-        "operator_one",
         est=cost(2 * 127 * 36 * 256, 127 * 36 * 256 * 4),
     )
     u_right = lax.ppermute(u, "frames", [(i + 1, i) for i in range(count - 1)])
     back = plain(
         back_kernel,
         [sds(2 * Q, PT)] * GROUPS,
-        (obs_count, pid, fid, jac_point, jac_cam, z, u),
-        "back_terms",
-        smem=(0,),
+        (pid, fid, jac_point, jac_cam, z, u),
         est=cost(2 * 400 * 256 * 8192, 2 * 32 * 8192 * 4),
     )
     returned = [shifted(back[GROUPS - 1 - s], "points", s) for s in (3, 2, 1)] + [back[GROUPS - 1]]
@@ -379,7 +406,6 @@
         second_kernel,
         sds(count, 128),
         (u, u_right, bands, rhs, z, w),
-        "operator_two",
         est=cost(127 * 36 * 256, 127 * 18 * 256 * 4),
     )
     gram = lax.all_to_all(gram, "frames", split_axis=0, concat_axis=0, tiled=True)
@@ -387,14 +413,14 @@
         undo_kernel,
         [sds(Q, PT)] * 2,
         (*returned, point_inv),
-        "undo",
+        raw=(4,),
+        scratch=[pltpu.VMEM((Q, Q, PT), F32), pltpu.SemaphoreType.DMA],
         est=cost(4 * Q * Q * PT, Q * Q * PT * 4),
     )
     camera_step, point_step = plain(
         final_kernel,
         [sds(CP, FR), sds(Q, PT)],
         (gram, z, u, solved, undo_z, undo_u),
-        "final",
         est=cost(6 * Q * PT, 6 * Q * PT * 4),
     )
     return camera_step, point_step
@@ -414,7 +440,7 @@
         P(None, None, "frames"),
     )
     return jax.shard_map(
-        local,
+        step,
         mesh=mesh,
         in_specs=placed,
         out_specs=(P(None, "frames"), P(None, ("frames", "points"))),

time: 76.7 us -> 69.5 us (0.906)
  waiting for transfers between devices: 21.4 us -> 15.1 us
  starting transfers between devices: 33.8 us -> 36.9 us
  Pallas kernels: 19.1 us -> 16.1 us
  local copies, waits for them, and re-layouts: 1.23 us -> 0.31 us
    ppermute x12, waiting for transfers between devices: 10.8 us -> 5.29 us  [shifted(): lax.ppermute(value, axis, [(i, (i + step) % count) for i in range(count)])]
    pallas_call x12 -> x13, Pallas kernels: 19.1 us -> 16.1 us  [plain(): pl.pallas_call(kernel, in_specs=specs, out_specs=out_specs, out_shape=out...]
    ppermute x12, starting transfers between devices: 13 us -> 15.6 us  [shifted(): lax.ppermute(value, axis, [(i, (i + step) % count) for i in range(count)])]
    unnamed x25 -> x17, local copies, waits for them, and re-layouts: 1.23 us -> 0.31 us
  transfers between devices with their start and end apart: 16 -> 16, of which waited for: 9 -> 8; matrix products, arithmetic and copies ran while one was open for 0% -> 0% of each run, Pallas kernels for 9% -> 11%
where the time goes in v3:
time: 69.5 us; the launch traced here: 69.2 us
  starting transfers between devices  36.9 us (53%)
  Pallas kernels  16.1 us (23%)
  waiting for transfers between devices  15.1 us (22%)
  between operations  0.83 us (1%)
    pallas_call x13, Pallas kernels, plain(): pl.pallas_call(kernel, in_specs=specs, out_specs=out_specs, out_shape=out...  16.1 us
    ppermute x12, starting transfers between devices, shifted(): lax.ppermute(value, axis, [(i, (i + step) % count) for i in range(count)])  15.6 us
    all_to_all x1, starting transfers between devices, step(): lax.all_to_all(gram, 'frames', split_axis=0, concat_axis=0, tiled=True)  9.69 us
    ppermute x1, starting transfers between devices, beside(): lax.ppermute(value, 'frames', down)  6.44 us
    ppermute x12, waiting for transfers between devices, shifted(): lax.ppermute(value, axis, [(i, (i + step) % count) for i in range(count)])  5.29 us
    ppermute x1, waiting for transfers between devices, step(): u_right = lax.ppermute(u, 'frames', [(i + 1, i) for i in range(count - 1)])  4.55 us
    all_to_all x1, waiting for transfers between devices, step(): lax.all_to_all(gram, 'frames', split_axis=0, concat_axis=0, tiled=True)  4.52 us
    ppermute x1, starting transfers between devices, beside(): lax.ppermute(value, 'frames', up)  3.1 us
  transfers between devices with their start and end apart: 16, of which 8 were waited for; matrix products, arithmetic and copies ran while one was open for 0% of the time, Pallas kernels for 11%

profile of v3, /device:TPU:1, one launch (start us, length us, event | category | flops | bytes accessed | tf_op | source)
XLA Modules:
  0.0 69.2 jit_solution(14699453451435002002)
XLA Ops:
  0.6 3.2 %shard_map.113 = (f32[24,1024]{1,0:T(8,128)S(1)}, f32[24,1024]{1,0:T(8,128)S(1)}, f32[24,1024]{1,0:T(8,128)S(1)}) custom-call(s32[4]{0:T(128)} %count_hbm.3, s32[1,8192]{1,0:T(1,128)} %bitcast.14, f32[2,8192]{1,0:T(2,128)} %res_ref.7, f32[2,24,8192]{2,1,0:T(8,128)} %jp_ref.9), custom_call_target="tpu_custom_call" | custom-call | flops 603979776 | bytes 1179648 | tf_op jit(solution)/shard_map/pallas_call | solution.py:311
  3.9 3.6 %collective-permute-start.1 = (f32[24,1024]{1,0:T(8,128)S(1)}, f32[24,1024]{1,0:T(8,128)S(1)}, u32[]{:S(2)}, u32[]{:S(2)}) collective-permute-start(f32[24,1024]{1,0:T(8,128)S(1)} %get-tuple-element.21), channel_id=1, source_target_pairs={{0,2},{1,3},{2,0},{3,1},{4,6},{5,7},{6,4},{7,5},{8,10},{9,11},{10,... | collective-permute-start | bytes 294920 | tf_op jit(solution)/shard_map/ppermute | solution.py:288
  7.5 0.3 collective-permute-start.2
  7.8 2.4 %collective-permute-start = (f32[24,1024]{1,0:T(8,128)S(1)}, f32[24,1024]{1,0:T(8,128)S(1)}, u32[]{:S(2)}, u32[]{:S(2)}) collective-permute-start(f32[24,1024]{1,0:T(8,128)S(1)} %get-tuple-element.18.after_ref), channel_id=1, source_target_pairs={{0,3},{1,0},{2,1},{3,2},{4,7},{5,4},{6,5},{7,6},{8,11},{9,8},{10,9... | collective-permute-start | bytes 294920 | tf_op jit(solution)/shard_map/ppermute | solution.py:288
  10.2 1.8 %shard_map.114 = (f32[24,1024]{1,0:T(8,128)S(1)}, s32[1,8192]{1,0:T(1,128)S(1)}, s32[1,8192]{1,0:T(1,128)S(1)}) custom-call(f32[24,1024]{1,0:T(8,128)S(1)} %get-tuple-element.18.after_ref, s32[4]{0:T(128)} %count_hbm.3, s32[1,8192]{1,0:T(1,128)} %bitcast.15, s32[1,8192]{1,0:T(1,128)} %bitcast.16, f32[2,8192]{1,0:T(2,128)} %res_ref.7, f32[2,24,8192]{2,1,0:T(8,128)} %jp_ref.9), custom_call_target="tpu_custom_call" | custom-call | flops 201326592 | bytes 393216 | tf_op jit(solution)/shard_map/pallas_call | solution.py:311
  12.4 0.3 shard_map.115.rest_0_.ps_ref
  12.7 2.0 %collective-permute-start.3 = (f32[24,1024]{1,0:T(8,128)S(1)}, f32[24,1024]{1,0:T(8,128)S(1)}, u32[]{:S(2)}, u32[]{:S(2)}) collective-permute-start(f32[24,1024]{1,0:T(8,128)S(1)} %shard_map.115.rest_0_.ps_ref), channel_id=1, source_target_pairs={{0,1},{1,2},{2,3},{3,0},{4,5},{5,6},{6,7},{7,4},{8,9},{9,10},{10,1... | collective-permute-start | bytes 294920 | tf_op jit(solution)/shard_map/ppermute | solution.py:288
  14.7 0.8 %collective-permute-start.4 = (f32[24,1024]{1,0:T(8,128)S(1)}, f32[24,1024]{1,0:T(8,128)S(1)}, u32[]{:S(2)}, u32[]{:S(2)}) collective-permute-start(f32[24,1024]{1,0:T(8,128)S(1)} %shard_map.115.rest_0_.ps_ref), channel_id=1, source_target_pairs={{0,3},{1,0},{2,1},{3,2},{4,7},{5,4},{6,5},{7,6},{8,11},{9,8},{10,9... | collective-permute-start | bytes 294920 | tf_op jit(solution)/shard_map/ppermute | solution.py:288
  15.5 1.1 %collective-permute-start.5 = (f32[24,1024]{1,0:T(8,128)S(1)}, f32[24,1024]{1,0:T(8,128)S(1)}, u32[]{:S(2)}, u32[]{:S(2)}) collective-permute-start(f32[24,1024]{1,0:T(8,128)S(1)} %shard_map.115.rest_0_.ps_ref), channel_id=1, source_target_pairs={{0,2},{1,3},{2,0},{3,1},{4,6},{5,7},{6,4},{7,5},{8,10},{9,11},{10,... | collective-permute-start | bytes 294920 | tf_op jit(solution)/shard_map/ppermute | solution.py:288
  16.9 0.7 %shard_map.116.rest_0_ = f32[6,256]{1,0:T(8,128)S(1)} custom-call(s32[1,8192]{1,0:T(1,128)S(1)} %get-tuple-element.19.pid_ref, s32[1,8192]{1,0:T(1,128)S(1)} %get-tuple-element.20.fid_ref, f32[2,8192]{1,0:T(2,128)S(1)} %copy-done.2, f32[2,24,8192]{2,1,0:T(8,128)S(1)} %copy-done, f32[2,6,8192]{2,1,0:T(8,128)S(1)} %copy.20.jc_ref, ...), custom_call_target="tpu_custom_call" | custom-call | flops 268435456 | bytes 524288 | tf_op jit(solution)/shard_map/pallas_call | solution.py:311
  17.6 0.8 %shard_map.117.rest_0_ = f32[6,256]{1,0:T(8,128)S(1)} custom-call(s32[1,8192]{1,0:T(1,128)S(1)} %get-tuple-element.19.pid_ref, s32[1,8192]{1,0:T(1,128)S(1)} %get-tuple-element.20.fid_ref, f32[2,8192]{1,0:T(2,128)S(1)} %copy-done.2, f32[2,24,8192]{2,1,0:T(8,128)S(1)} %copy-done, f32[2,6,8192]{2,1,0:T(8,128)S(1)} %copy.20.jc_ref, ...), custom_call_target="tpu_custom_call" | custom-call | flops 268435456 | bytes 524288 | tf_op jit(solution)/shard_map/pallas_call | solution.py:311
  18.4 0.7 %shard_map.118.rest_0_ = f32[6,256]{1,0:T(8,128)S(1)} custom-call(s32[1,8192]{1,0:T(1,128)S(1)} %get-tuple-element.19.pid_ref, s32[1,8192]{1,0:T(1,128)S(1)} %get-tuple-element.20.fid_ref, f32[2,8192]{1,0:T(2,128)S(1)} %copy-done.2, f32[2,24,8192]{2,1,0:T(8,128)S(1)} %copy-done, f32[2,6,8192]{2,1,0:T(8,128)S(1)} %copy.20.jc_ref, ...), custom_call_target="tpu_custom_call" | custom-call | flops 268435456 | bytes 524288 | tf_op jit(solution)/shard_map/pallas_call | solution.py:311
  19.1 1.5 %collective-permute-done.5.rest_1_ = f32[24,1024]{1,0:T(8,128)S(1)} collective-permute-done((f32[24,1024]{1,0:T(8,128)S(1)}, f32[24,1024]{1,0:T(8,128)S(1)}, u32[]{:S(2)}, u32[]{:S(2)}) %collective-permute-start.5) | collective-permute-done | bytes 98336 | tf_op jit(solution)/shard_map/ppermute | solution.py:288
  20.7 0.7 %shard_map.119.a_ref = f32[6,256]{1,0:T(8,128)S(1)} custom-call(s32[1,8192]{1,0:T(1,128)S(1)} %get-tuple-element.19.pid_ref, s32[1,8192]{1,0:T(1,128)S(1)} %get-tuple-element.20.fid_ref, f32[2,8192]{1,0:T(2,128)S(1)} %copy-done.2, f32[2,24,8192]{2,1,0:T(8,128)S(1)} %copy-done, f32[2,6,8192]{2,1,0:T(8,128)S(1)} %copy.20.jc_ref, ...), custom_call_target="tpu_custom_call" | custom-call | flops 268435456 | bytes 524288 | tf_op jit(solution)/shard_map/pallas_call | solution.py:311
  21.4 2.2 %collective-permute-start.8 = (f32[6,256]{1,0:T(8,128)S(1)}, f32[6,256]{1,0:T(8,128)S(1)}, u32[]{:S(2)}, u32[]{:S(2)}) collective-permute-start(f32[6,256]{1,0:T(8,128)S(1)} %shard_map.119.a_ref), channel_id=1, source_target_pairs={{0,3},{1,0},{2,1},{3,2},{4,7},{5,4},{6,5},{7,6},{8,11},{9,8},{10,9... | collective-permute-start | bytes 18440 | tf_op jit(solution)/shard_map/ppermute | solution.py:288
  23.8 0.5 collective-permute-start.6
  24.4 3.2 %collective-permute-done.7.c_ref = f32[6,256]{1,0:T(8,128)S(1)} collective-permute-done((f32[6,256]{1,0:T(8,128)S(1)}, f32[6,256]{1,0:T(8,128)S(1)}, u32[]{:S(2)}, u32[]{:S(2)}) %collective-permute-start.7) | collective-permute-done | bytes 6176 | tf_op jit(solution)/shard_map/ppermute | solution.py:288
  27.7 6.4 %collective-permute-start.10 = (f32[8,256]{1,0:T(8,128)S(1)}, f32[8,256]{1,0:T(8,128)S(1)}, u32[]{:S(2)}, u32[]{:S(2)}) collective-permute-start(f32[8,256]{1,0:T(8,128)S(1)} %get-tuple-element.24.z_ref), channel_id=1, source_target_pairs={{4,0},{8,4},{12,8},{16,12},{20,16},{24,20},{28,24},{32,28},{36,32}... | collective-permute-start | bytes 24584 | tf_op jit(solution)/shard_map/ppermute | solution.py:295
  34.1 3.1 %collective-permute-start.9 = (f32[8,256]{1,0:T(8,128)S(1)}, f32[8,256]{1,0:T(8,128)S(1)}, u32[]{:S(2)}, u32[]{:S(2)}) collective-permute-start(f32[8,256]{1,0:T(8,128)S(1)} %get-tuple-element.24.z_ref), channel_id=1, source_target_pairs={{0,4},{4,8},{8,12},{12,16},{16,20},{20,24},{24,28},{28,32},{32,36}... | collective-permute-start | bytes 24584 | tf_op jit(solution)/shard_map/ppermute | solution.py:295
  37.2 0.8 %collective-permute-done.9.left_ref = f32[8,256]{1,0:T(8,128)S(1)} collective-permute-done((f32[8,256]{1,0:T(8,128)S(1)}, f32[8,256]{1,0:T(8,128)S(1)}, u32[]{:S(2)}, u32[]{:S(2)}) %collective-permute-start.9) | collective-permute-done | bytes 8224 | tf_op jit(solution)/shard_map/ppermute | solution.py:295
  38.0 0.8 %shard_map.121 = (f32[6,256]{1,0:T(8,128)S(1)}, f32[8,256]{1,0:T(8,128)S(1)}) custom-call(f32[8,256]{1,0:T(8,128)S(1)} %get-tuple-element.24.z_ref, f32[8,256]{1,0:T(8,128)S(1)} %collective-permute-done.9.left_ref, f32[8,256]{1,0:T(8,128)S(1)} %collective-permute-done.10.right_ref, f32[6,6,127,256]{3,2,1,0:T(8,128)S(1)} %bitcast.10, f32[6,6,256]{2,1,0:T(8,128)S(1)} %copy-done.3), custom_call_target="tpu_custom_call" | custom-call | flops 2340864 | bytes 4681728 | tf_op jit(solution)/shard_map/pallas_call | solution.py:311
  38.9 2.5 %shard_map.123 = (f32[48,1024]{1,0:T(8,128)S(1)}, f32[48,1024]{1,0:T(8,128)S(1)}, f32[48,1024]{1,0:T(8,128)S(1)}, f32[48,1024]{1,0:T(8,128)S(1)}) custom-call(s32[1,8192]{1,0:T(1,128)S(1)} %get-tuple-element.19.pid_ref, s32[1,8192]{1,0:T(1,128)S(1)} %get-tuple-element.20.fid_ref, f32[2,24,8192]{2,1,0:T(8,128)S(1)} %copy-done, ...), custom_call_target="tpu_custom_call" | custom-call | flops 1677721600 | bytes 2097152 | tf_op jit(solution)/shard_map/pallas_call | solution.py:311
  41.4 0.9 %collective-permute-start.12 = (f32[48,1024]{1,0:T(8,128)S(1)}, f32[48,1024]{1,0:T(8,128)S(1)}, u32[]{:S(2)}, u32[]{:S(2)}) collective-permute-start(f32[48,1024]{1,0:T(8,128)S(1)} %get-tuple-element.28), channel_id=1, source_target_pairs={{0,3},{1,0},{2,1},{3,2},{4,7},{5,4},{6,5},{7,6},{8,11},{9,8},{10,9... | collective-permute-start | bytes 589832 | tf_op jit(solution)/shard_map/ppermute | solution.py:288
  42.2 0.9 %collective-permute-start.13 = (f32[48,1024]{1,0:T(8,128)S(1)}, f32[48,1024]{1,0:T(8,128)S(1)}, u32[]{:S(2)}, u32[]{:S(2)}) collective-permute-start(f32[48,1024]{1,0:T(8,128)S(1)} %get-tuple-element.29), channel_id=1, source_target_pairs={{0,2},{1,3},{2,0},{3,1},{4,6},{5,7},{6,4},{7,5},{8,10},{9,11},{10,... | collective-permute-start | bytes 589832 | tf_op jit(solution)/shard_map/ppermute | solution.py:288
  43.1 0.8 %collective-permute-start.14 = (f32[48,1024]{1,0:T(8,128)S(1)}, f32[48,1024]{1,0:T(8,128)S(1)}, u32[]{:S(2)}, u32[]{:S(2)}) collective-permute-start(f32[48,1024]{1,0:T(8,128)S(1)} %get-tuple-element.30), channel_id=1, source_target_pairs={{0,1},{1,2},{2,3},{3,0},{4,5},{5,6},{6,7},{7,4},{8,9},{9,10},{10,1... | collective-permute-start | bytes 589832 | tf_op jit(solution)/shard_map/ppermute | solution.py:288
  43.9 2.1 %collective-permute-start.11 = (f32[8,256]{1,0:T(8,128)S(1)}, f32[8,256]{1,0:T(8,128)S(1)}, u32[]{:S(2)}, u32[]{:S(2)}) collective-permute-start(f32[8,256]{1,0:T(8,128)S(1)} %get-tuple-element.25.u_ref), channel_id=1, source_target_pairs={{4,0},{8,4},{12,8},{16,12},{20,16},{24,20},{28,24},{32,28},{36,32}... | collective-permute-start | bytes 24584 | tf_op jit(solution)/shard_map/ppermute | solution.py:397
  46.0 4.5 %collective-permute-done.11.right_ref = f32[8,256]{1,0:T(8,128)S(1)} collective-permute-done((f32[8,256]{1,0:T(8,128)S(1)}, f32[8,256]{1,0:T(8,128)S(1)}, u32[]{:S(2)}, u32[]{:S(2)}) %collective-permute-start.11) | collective-permute-done | bytes 8224 | tf_op jit(solution)/shard_map/ppermute | solution.py:397
  50.5 1.3 %shard_map.122 = f32[32,128]{1,0:T(8,128)} custom-call(f32[8,256]{1,0:T(8,128)S(1)} %get-tuple-element.25.u_ref, f32[8,256]{1,0:T(8,128)S(1)} %collective-permute-done.11.right_ref, f32[6,6,127,256]{3,2,1,0:T(8,128)S(1)} %bitcast.11, f32[6,256]{1,0:T(8,128)S(1)} %get-tuple-element.26.r_ref, f32[8,256]{1,0:T(8,128)S(1)} %get-tuple-element.24.z_ref, ...), custom_call_target="tpu_custom_call" | custom-call | flops 1170432 | bytes 2340864 | tf_op jit(solution)/shard_map/pallas_call | solution.py:311
  51.8 9.7 %all-to-all-start = ((f32[32,1,128]{2,1,0:T(1,128)}), f32[32,1,128]{2,1,0:T(1,128)S(1)}, u32[]{:S(2)}, u32[]{:S(2)}) async-start(f32[32,1,128]{2,1,0:T(1,128)} %bitcast.5), calls=%async_computation | async-start | bytes 32768 | tf_op jit(solution)/shard_map/all_to_all | solution.py:411
  61.6 2.3 %shard_map.124 = (f32[24,1024]{1,0:T(8,128)S(1)}, f32[24,1024]{1,0:T(8,128)S(1)}) custom-call(f32[48,1024]{1,0:T(8,128)S(1)} %collective-permute-done.12.a_ref, f32[48,1024]{1,0:T(8,128)S(1)} %collective-permute-done.13.b_ref, f32[48,1024]{1,0:T(8,128)S(1)} %collective-permute-done.14.c_ref, f32[48,1024]{1,0:T(8,128)S(1)} %get-tuple-element.31.d_ref, ...), custom_call_target="tpu_custom_call" | custom-call | flops 2359296 | bytes 2359296 | tf_op jit(solution)/shard_map/pallas_call | solution.py:311
  63.9 4.5 %all-to-all-done = f32[32,1,128]{2,1,0:T(1,128)S(1)} async-done(((f32[32,1,128]{2,1,0:T(1,128)}), f32[32,1,128]{2,1,0:T(1,128)S(1)}, u32[]{:S(2)}, u32[]{:S(2)}) %all-to-all-start) | async-done | bytes 16416 | tf_op jit(solution)/shard_map/all_to_all | solution.py:411
  68.4 0.8 %shard_map.125 = (f32[6,256]{1,0:T(8,128)}, f32[24,1024]{1,0:T(8,128)}) custom-call(f32[32,128]{1,0:T(8,128)S(1)} %bitcast.12, f32[8,256]{1,0:T(8,128)S(1)} %get-tuple-element.24.z_ref, f32[8,256]{1,0:T(8,128)S(1)} %get-tuple-element.25.u_ref, f32[24,1024]{1,0:T(8,128)S(1)} %shard_map.115.rest_0_.ps_ref, f32[24,1024]{1,0:T(8,128)S(1)} %get-tuple-element.32.pz_ref, ...), custom_call_target="tpu_custom_call" | custom-call | flops 147456 | bytes 589824 | tf_op jit(solution)/shard_map/pallas_call | solution.py:311
  (31 shorter events, 1.1 us)
Async XLA Ops:
  0.6 11.8 %copy-start.1 = (f32[24,24,1024]{2,1,0:T(8,128)S(1)}, f32[24,24,1024]{2,1,0:T(8,128)}, u32[]{:S(2)}) copy-start(f32[24,24,1024]{2,1,0:T(8,128)} %inv_hbm.1) | copy-start | bytes 7077892
  3.9 12.7 %copy-start.5 = (f32[2,6,8192]{2,0,1:T(2,128)S(1)}, f32[2,6,8192]{2,0,1:T(2,128)}, u32[]{:S(2)}) copy-start(f32[2,6,8192]{2,0,1:T(2,128)} %param.13) | copy-start | bytes 1179652
  3.9 8.1 %collective-permute-start.1 = (f32[24,1024]{1,0:T(8,128)S(1)}, f32[24,1024]{1,0:T(8,128)S(1)}, u32[]{:S(2)}, u32[]{:S(2)}) collective-permute-start(f32[24,1024]{1,0:T(8,128)S(1)} %get-tuple-element.21), channel_id=1, source_target_pairs={{0,2},{1,3},{2,0},{3,1},{4,6},{5,7},{6,4},{7,5},{8,10},{9,11},{10,... | collective-permute-start | bytes 294920 | tf_op jit(solution)/shard_map/ppermute | solution.py:288
  7.5 4.7 %collective-permute-start.2 = (f32[24,1024]{1,0:T(8,128)S(1)}, f32[24,1024]{1,0:T(8,128)S(1)}, u32[]{:S(2)}, u32[]{:S(2)}) collective-permute-start(f32[24,1024]{1,0:T(8,128)S(1)} %get-tuple-element.22), channel_id=1, source_target_pairs={{0,1},{1,2},{2,3},{3,0},{4,5},{5,6},{6,7},{7,4},{8,9},{9,10},{10,1... | collective-permute-start | bytes 294920 | tf_op jit(solution)/shard_map/ppermute | solution.py:288
  7.8 4.6 %collective-permute-start = (f32[24,1024]{1,0:T(8,128)S(1)}, f32[24,1024]{1,0:T(8,128)S(1)}, u32[]{:S(2)}, u32[]{:S(2)}) collective-permute-start(f32[24,1024]{1,0:T(8,128)S(1)} %get-tuple-element.18.after_ref), channel_id=1, source_target_pairs={{0,3},{1,0},{2,1},{3,2},{4,7},{5,4},{6,5},{7,6},{8,11},{9,8},{10,9... | collective-permute-start | bytes 294920 | tf_op jit(solution)/shard_map/ppermute | solution.py:288
  10.2 6.6 %copy-start.2 = (f32[2,8192]{1,0:T(2,128)S(1)}, f32[2,8192]{1,0:T(2,128)}, u32[]{:S(2)}) copy-start(f32[2,8192]{1,0:T(2,128)} %res_ref.7) | copy-start | bytes 196612
  10.2 6.7 %copy-start = (f32[2,24,8192]{2,1,0:T(8,128)S(1)}, f32[2,24,8192]{2,1,0:T(8,128)}, u32[]{:S(2)}) copy-start(f32[2,24,8192]{2,1,0:T(8,128)} %jp_ref.9) | copy-start | bytes 4718596
  10.2 27.8 %slice-start = ((s8[4718592]{0:T(1024)(128)(4,1)}), s8[4194304]{0:T(1024)(128)(4,1)S(1)}, s32[]{:S(2)}) async-start(s8[4718592]{0:T(1024)(128)(4,1)} %bitcast.8), calls=%async_computation.1 | async-start | bytes 8388608
  12.7 4.9 %collective-permute-start.3 = (f32[24,1024]{1,0:T(8,128)S(1)}, f32[24,1024]{1,0:T(8,128)S(1)}, u32[]{:S(2)}, u32[]{:S(2)}) collective-permute-start(f32[24,1024]{1,0:T(8,128)S(1)} %shard_map.115.rest_0_.ps_ref), channel_id=1, source_target_pairs={{0,1},{1,2},{2,3},{3,0},{4,5},{5,6},{6,7},{7,4},{8,9},{9,10},{10,1... | collective-permute-start | bytes 294920 | tf_op jit(solution)/shard_map/ppermute | solution.py:288
  14.7 3.7 %collective-permute-start.4 = (f32[24,1024]{1,0:T(8,128)S(1)}, f32[24,1024]{1,0:T(8,128)S(1)}, u32[]{:S(2)}, u32[]{:S(2)}) collective-permute-start(f32[24,1024]{1,0:T(8,128)S(1)} %shard_map.115.rest_0_.ps_ref), channel_id=1, source_target_pairs={{0,3},{1,0},{2,1},{3,2},{4,7},{5,4},{6,5},{7,6},{8,11},{9,8},{10,9... | collective-permute-start | bytes 294920 | tf_op jit(solution)/shard_map/ppermute | solution.py:288
  15.5 5.2 %collective-permute-start.5 = (f32[24,1024]{1,0:T(8,128)S(1)}, f32[24,1024]{1,0:T(8,128)S(1)}, u32[]{:S(2)}, u32[]{:S(2)}) collective-permute-start(f32[24,1024]{1,0:T(8,128)S(1)} %shard_map.115.rest_0_.ps_ref), channel_id=1, source_target_pairs={{0,2},{1,3},{2,0},{3,1},{4,6},{5,7},{6,4},{7,5},{8,10},{9,11},{10,... | collective-permute-start | bytes 294920 | tf_op jit(solution)/shard_map/ppermute | solution.py:288
  16.9 21.1 %slice-start.1 = ((s8[4718592]{0:T(1024)(128)(4,1)}), s8[524288]{0:T(1024)(128)(4,1)S(1)}, s32[]{:S(2)}) async-start(s8[4718592]{0:T(1024)(128)(4,1)} %bitcast.8), calls=%async_computation.2 | async-start | bytes 1048576
  18.4 9.3 %copy-start.3 = (f32[6,6,256]{2,1,0:T(8,128)S(1)}, f32[6,6,256]{2,1,0:T(8,128)}, u32[]{:S(2)}) copy-start(f32[6,6,256]{2,1,0:T(8,128)} %pre_ref.3) | copy-start | bytes 110596
  18.4 9.3 %copy-start.4 = (f32[256]{0:T(256)S(1)}, f32[256]{0:T(256)}, u32[]{:S(2)}) copy-start(f32[256]{0:T(256)} %param.18) | copy-start | bytes 3076
  21.4 3.0 %collective-permute-start.8 = (f32[6,256]{1,0:T(8,128)S(1)}, f32[6,256]{1,0:T(8,128)S(1)}, u32[]{:S(2)}, u32[]{:S(2)}) collective-permute-start(f32[6,256]{1,0:T(8,128)S(1)} %shard_map.119.a_ref), channel_id=1, source_target_pairs={{0,3},{1,0},{2,1},{3,2},{4,7},{5,4},{6,5},{7,6},{8,11},{9,8},{10,9... | collective-permute-start | bytes 18440 | tf_op jit(solution)/shard_map/ppermute | solution.py:288
  23.6 4.0 %collective-permute-start.7 = (f32[6,256]{1,0:T(8,128)S(1)}, f32[6,256]{1,0:T(8,128)S(1)}, u32[]{:S(2)}, u32[]{:S(2)}) collective-permute-start(f32[6,256]{1,0:T(8,128)S(1)} %shard_map.119.a_ref), channel_id=1, source_target_pairs={{0,2},{1,3},{2,0},{3,1},{4,6},{5,7},{6,4},{7,5},{8,10},{9,11},{10,... | collective-permute-start | bytes 18440 | tf_op jit(solution)/shard_map/ppermute | solution.py:288
  23.8 3.8 %collective-permute-start.6 = (f32[6,256]{1,0:T(8,128)S(1)}, f32[6,256]{1,0:T(8,128)S(1)}, u32[]{:S(2)}, u32[]{:S(2)}) collective-permute-start(f32[6,256]{1,0:T(8,128)S(1)} %shard_map.119.a_ref), channel_id=1, source_target_pairs={{0,1},{1,2},{2,3},{3,0},{4,5},{5,6},{6,7},{7,4},{8,9},{9,10},{10,1... | collective-permute-start | bytes 18440 | tf_op jit(solution)/shard_map/ppermute | solution.py:288
  27.7 9.6 %collective-permute-start.10 = (f32[8,256]{1,0:T(8,128)S(1)}, f32[8,256]{1,0:T(8,128)S(1)}, u32[]{:S(2)}, u32[]{:S(2)}) collective-permute-start(f32[8,256]{1,0:T(8,128)S(1)} %get-tuple-element.24.z_ref), channel_id=1, source_target_pairs={{4,0},{8,4},{12,8},{16,12},{20,16},{24,20},{28,24},{32,28},{36,32}... | collective-permute-start | bytes 24584 | tf_op jit(solution)/shard_map/ppermute | solution.py:295
  34.1 3.9 %collective-permute-start.9 = (f32[8,256]{1,0:T(8,128)S(1)}, f32[8,256]{1,0:T(8,128)S(1)}, u32[]{:S(2)}, u32[]{:S(2)}) collective-permute-start(f32[8,256]{1,0:T(8,128)S(1)} %get-tuple-element.24.z_ref), channel_id=1, source_target_pairs={{0,4},{4,8},{8,12},{12,16},{16,20},{20,24},{24,28},{28,32},{32,36}... | collective-permute-start | bytes 24584 | tf_op jit(solution)/shard_map/ppermute | solution.py:295
  41.4 20.2 %collective-permute-start.12 = (f32[48,1024]{1,0:T(8,128)S(1)}, f32[48,1024]{1,0:T(8,128)S(1)}, u32[]{:S(2)}, u32[]{:S(2)}) collective-permute-start(f32[48,1024]{1,0:T(8,128)S(1)} %get-tuple-element.28), channel_id=1, source_target_pairs={{0,3},{1,0},{2,1},{3,2},{4,7},{5,4},{6,5},{7,6},{8,11},{9,8},{10,9... | collective-permute-start | bytes 589832 | tf_op jit(solution)/shard_map/ppermute | solution.py:288
  42.2 19.3 %collective-permute-start.13 = (f32[48,1024]{1,0:T(8,128)S(1)}, f32[48,1024]{1,0:T(8,128)S(1)}, u32[]{:S(2)}, u32[]{:S(2)}) collective-permute-start(f32[48,1024]{1,0:T(8,128)S(1)} %get-tuple-element.29), channel_id=1, source_target_pairs={{0,2},{1,3},{2,0},{3,1},{4,6},{5,7},{6,4},{7,5},{8,10},{9,11},{10,... | collective-permute-start | bytes 589832 | tf_op jit(solution)/shard_map/ppermute | solution.py:288
  43.1 18.4 %collective-permute-start.14 = (f32[48,1024]{1,0:T(8,128)S(1)}, f32[48,1024]{1,0:T(8,128)S(1)}, u32[]{:S(2)}, u32[]{:S(2)}) collective-permute-start(f32[48,1024]{1,0:T(8,128)S(1)} %get-tuple-element.30), channel_id=1, source_target_pairs={{0,1},{1,2},{2,3},{3,0},{4,5},{5,6},{6,7},{7,4},{8,9},{9,10},{10,1... | collective-permute-start | bytes 589832 | tf_op jit(solution)/shard_map/ppermute | solution.py:288
  43.9 6.6 %collective-permute-start.11 = (f32[8,256]{1,0:T(8,128)S(1)}, f32[8,256]{1,0:T(8,128)S(1)}, u32[]{:S(2)}, u32[]{:S(2)}) collective-permute-start(f32[8,256]{1,0:T(8,128)S(1)} %get-tuple-element.25.u_ref), channel_id=1, source_target_pairs={{4,0},{8,4},{12,8},{16,12},{20,16},{24,20},{28,24},{32,28},{36,32}... | collective-permute-start | bytes 24584 | tf_op jit(solution)/shard_map/ppermute | solution.py:397
  51.8 16.6 %all-to-all-start = ((f32[32,1,128]{2,1,0:T(1,128)}), f32[32,1,128]{2,1,0:T(1,128)S(1)}, u32[]{:S(2)}, u32[]{:S(2)}) async-start(f32[32,1,128]{2,1,0:T(1,128)} %bitcast.5), calls=%async_computation | async-start | bytes 32768 | tf_op jit(solution)/shard_map/all_to_all | solution.py:411

commit v4 on v3

--- a/solution.py
+++ b/solution.py
@@ -85,7 +85,7 @@
 
 
 def block_at(turn):
-    return lax.rem(lax.axis_index("points") + GROUPS + turn, GROUPS)
+    return lax.bitwise_xor(lax.axis_index("points"), abs(turn))
 
 
 def lanes(b):
@@ -99,46 +99,37 @@
     return copies
 
 
-def grad_kernel(count_hbm, ids_hbm, res_hbm, jp_hbm, *rest):
-    far = GROUPS - 1
-    outs, (count_ref, ids_ref, res_ref, jp_ref, sems) = rest[:far], rest[far:]
-    blocks = [block_at(GROUPS - 1 - j) for j in range(far)]
-    large = [(jp_hbm.at[:, :, lanes(b)], jp_ref.at[j]) for j, b in enumerate(blocks)]
-    small = [(count_hbm, count_ref), (ids_hbm, ids_ref), (res_hbm, res_ref)]
-    copies = fetch(small + large, sems)
+def sums_toward(b, ids_ref, res_ref, jp_ref):
+    at = lanes(b)
+    terms = jp_ref[0, :, at] * res_ref[0:1, at] + jp_ref[1, :, at] * res_ref[1:2, at]
+    return scatter_points(terms, ids_ref[:, at])
+
+
+def load_kernel(
+    count_hbm, pid_hbm, fid_hbm, res_hbm, jp_hbm, out_ref, pid_ref, fid_ref, res_ref, jp_ref, count_ref, sems
+):
+    small = [(count_hbm, count_ref), (pid_hbm, pid_ref), (res_hbm, res_ref), (fid_hbm, fid_ref)]
+    blocks = [block_at(turn) for turn in (2, 1, 3, 0)]
+    large = [(jp_hbm.at[:, :, lanes(b)], jp_ref.at[:, :, lanes(b)]) for b in blocks]
+    copies = fetch(small[:3] + large[:1] + small[3:] + large[1:], sems)
     for copy in copies[:3]:
-        copy.wait()
-    for j, b in enumerate(blocks):
-        at = lanes(b)
-        copies[3 + j].wait()
-        terms = jp_ref[j, 0] * res_ref[0:1, at] + jp_ref[j, 1] * res_ref[1:2, at]
-        outs[j][...] = scatter_points(terms, used_or(ids_ref[:, at], count_ref[b], PT))
-
-
-def own_kernel(
-    after_ref, count_hbm, pid_hbm, fid_hbm, res_hbm, jp_hbm, out_ref, pid_out, fid_out,
-    count_ref, res_ref, jp_ref, sems,
-):
-    b = block_at(0)
-    at = lanes(b)
-    copies = fetch(
-        [
-            (count_hbm, count_ref),
-            (pid_hbm, pid_out),
-            (fid_hbm, fid_out),
-            (res_hbm.at[:, at], res_ref),
-            (jp_hbm.at[:, :, at], jp_ref),
-        ],
-        sems,
-    )
-    for copy in copies:
         copy.wait()
     for g in range(GROUPS):
         here = slice(g * CAP, (g + 1) * CAP)
-        pid_out[:, here] = used_or(pid_out[:, here], count_ref[g], PT)
-        fid_out[:, here] = used_or(fid_out[:, here], count_ref[g], FR)
-    terms = jp_ref[0] * res_ref[0:1, :] + jp_ref[1] * res_ref[1:2, :]
-    out_ref[...] = scatter_points(terms, pid_out[:, at])
+        pid_ref[:, here] = used_or(pid_ref[:, here], count_ref[g], PT)
+    copies[3].wait()
+    out_ref[...] = sums_toward(blocks[0], pid_ref, res_ref, jp_ref)
+    copies[4].wait()
+    for g in range(GROUPS):
+        here = slice(g * CAP, (g + 1) * CAP)
+        fid_ref[:, here] = used_or(fid_ref[:, here], count_ref[g], FR)
+    for copy in copies[5:]:
+        copy.wait()
+
+
+def grad_kernel(turns, ids_ref, res_ref, jp_ref, *outs):
+    for turn, out_ref in zip(turns, outs):
+        out_ref[...] = sums_toward(block_at(turn), ids_ref, res_ref, jp_ref)
 
 
 def solve_kernel(a_ref, b_ref, c_ref, d_ref, inv_ref, out_ref):
@@ -216,8 +207,12 @@
     )
 
 
-def first_kernel(z_ref, left_ref, right_ref, band_ref, pre_ref, w_ref, u_ref):
-    padded = jnp.concatenate([left_ref[...], z_ref[...], right_ref[...]], axis=1)
+def first_kernel(z_ref, outer_ref, inner_ref, band_ref, pre_ref, w_ref, u_ref):
+    even = lax.rem(lax.axis_index("frames"), 2) == 0
+    sides = (outer_ref[...], inner_ref[...])
+    left = jnp.where(even, sides[0], sides[1])
+    right = jnp.where(even, sides[1], sides[0])
+    padded = jnp.concatenate([left, z_ref[...], right], axis=1)
     near = padded[:, FR - 128 : 2 * FR + 128]
     banded = banded_sums(band_ref, [near[j : j + 1] for j in range(CP)], range(16))
     own = z_ref[:CP, :]
@@ -283,16 +278,17 @@
     pt_ref[...] = ps_ref[...] - c0 * pz_ref[...] - c1 * pu_ref[...]
 
 
-def shifted(value, axis, step):
-    count = lax.axis_size(axis)
-    return lax.ppermute(value, axis, [(i, (i + step) % count) for i in range(count)])
+def shifted(value, axis, turn):
+    return lax.ppermute(value, axis, [(i, i ^ turn) for i in range(GROUPS)])
 
 
 def beside(value):
     count = lax.axis_size("frames")
-    up = [(i, i + 1) for i in range(count - 1)]
-    down = [(i + 1, i) for i in range(count - 1)]
-    return lax.ppermute(value, "frames", up), lax.ppermute(value, "frames", down)
+    inner = [(i, i ^ 1) for i in range(count)]
+    outer = [pair for i in range(1, count - 1, 2) for pair in ((i, i + 1), (i + 1, i))]
+    far = lax.ppermute(value, "frames", outer)
+    near = lax.ppermute(value, "frames", inner)
+    return far, near
 
 
 def sds(*shape):
@@ -338,35 +334,25 @@
     edge = edge_weight.reshape(1, FR)
     bands = jnp.transpose(band, (1, 2, 0, 3))
 
-    far = plain(
-        grad_kernel,
-        [sds(Q, PT)] * (GROUPS - 1),
-        (obs_count, pid, residual, jac_point),
-        raw=(0, 1, 2, 3),
-        scratch=[
-            pltpu.SMEM((GROUPS,), jnp.int32),
-            pltpu.VMEM((1, slots), jnp.int32),
-            pltpu.VMEM((2, slots), F32),
-            pltpu.VMEM((GROUPS - 1, 2, Q, CAP), F32),
-            pltpu.SemaphoreType.DMA((GROUPS + 2,)),
-        ],
-        est=cost(2 * 192 * 256 * 6144, 2 * 24 * 6144 * 4),
-    )
     ints = jax.ShapeDtypeStruct((1, slots), jnp.int32)
-    near, pid, fid = plain(
-        own_kernel,
-        [sds(Q, PT), ints, ints],
-        (far[0], obs_count, pid, fid, residual, jac_point),
-        raw=(1, 2, 3, 4, 5),
-        scratch=[
-            pltpu.SMEM((GROUPS,), jnp.int32),
-            pltpu.VMEM((2, CAP), F32),
-            pltpu.VMEM((2, Q, CAP), F32),
-            pltpu.SemaphoreType.DMA((5,)),
-        ],
-        est=cost(2 * 192 * 256 * 2048, 2 * 24 * 2048 * 4),
-    )
-    got = [shifted(far[GROUPS - 1 - s], "points", s) for s in (3, 2, 1)] + [near]
+    far, pid, fid, res, jac = plain(
+        load_kernel,
+        [sds(Q, PT), ints, ints, sds(2, slots), sds(2, Q, slots)],
+        (obs_count, pid, fid, residual, jac_point),
+        raw=(0, 1, 2, 3, 4),
+        scratch=[pltpu.SMEM((GROUPS,), jnp.int32), pltpu.SemaphoreType.DMA((8,))],
+        est=cost(2 * 192 * 256 * 2048, 2 * 24 * 8192 * 4),
+    )
+    grad = lambda *turns: plain(
+        functools.partial(grad_kernel, turns),
+        [sds(Q, PT)] * len(turns),
+        (pid, res, jac),
+        est=cost(2 * 192 * 256 * 2048 * len(turns), 2 * 24 * 2048 * 4 * len(turns)),
+    )
+    got = []
+    for turn, sums in zip((2, 1, 3), [far, *grad(1, 3)]):
+        got.append(shifted(sums, "points", turn))
+    got.extend(grad(0))
     solved = plain(
         solve_kernel, sds(Q, PT), (*got, point_inv), est=cost(2 * Q * Q * PT, Q * Q * PT * 4)
     )
@@ -377,12 +363,14 @@
             plain(
                 functools.partial(rhs_kernel, -s),
                 sds(CP, FR),
-                (pid, fid, residual, jac_point, jac_cam, *partial, piece),
+                (pid, fid, res, jac, jac_cam, *partial, piece),
                 est=cost(2 * 256 * 256 * 2048, 2 * 32 * 2048 * 4),
             ),
         )
     (partial,) = partial
-    parts = [partial] + [shifted(partial, "points", s) for s in (1, 2, 3)]
+    parts = [partial]
+    for s in (1, 2, 3):
+        parts.append(shifted(partial, "points", s))
 
     rhs, z = plain(
         start_kernel, [sds(CP, FR), sds(8, FR)], (*parts, precond, edge), est=cost(20000, 100000)
@@ -398,10 +386,12 @@
     back = plain(
         back_kernel,
         [sds(2 * Q, PT)] * GROUPS,
-        (pid, fid, jac_point, jac_cam, z, u),
+        (pid, fid, jac, jac_cam, z, u),
         est=cost(2 * 400 * 256 * 8192, 2 * 32 * 8192 * 4),
     )
-    returned = [shifted(back[GROUPS - 1 - s], "points", s) for s in (3, 2, 1)] + [back[GROUPS - 1]]
+    returned = [back[GROUPS - 1]]
+    for s in (3, 2, 1):
+        returned.append(shifted(back[GROUPS - 1 - s], "points", s))
     gram = plain(
         second_kernel,
         sds(count, 128),

time: 69.5 us -> 67.7 us (0.974)
  Pallas kernels: 16.1 us -> 14.2 us
  waiting for transfers between devices: 15.1 us -> 16.8 us
  starting transfers between devices: 36.9 us -> 35.4 us
    ppermute x14, waiting for transfers between devices: 6.06 us -> 8.96 us  [the longest x12 7.73 us: shifted(): return lax.ppermute(value, axis, [(i, i ^ turn) for i in range(GROUPS)])]
    ppermute x14, starting transfers between devices: 25.1 us -> 22.9 us  [the longest x12 15.2 us: shifted(): return lax.ppermute(value, axis, [(i, i ^ turn) for i in range(GROUPS)])]
    pallas_call x13 -> x14, Pallas kernels: 16.1 us -> 14.2 us  [plain(): pl.pallas_call(kernel, in_specs=specs, out_specs=out_specs, out_shape=out...]
    ppermute x1, waiting for transfers between devices: 4.55 us -> 3.27 us  [step(): u_right = lax.ppermute(u, 'frames', [(i + 1, i) for i in range(count - 1)])]
    ppermute x1, starting transfers between devices: 2.09 us -> 2.82 us  [step(): u_right = lax.ppermute(u, 'frames', [(i + 1, i) for i in range(count - 1)])]
  transfers between devices with their start and end apart: 16 -> 16, of which waited for: 8 -> 9; matrix products, arithmetic and copies ran while one was open for 0% -> 0% of each run, Pallas kernels for 11% -> 11%
where the time goes in v4:
time: 67.7 us; the launch traced here: 67.5 us
  starting transfers between devices  35.4 us (52%)
  waiting for transfers between devices  16.8 us (25%)
  Pallas kernels  14.2 us (21%)
  between operations  0.8 us (1%)
    ppermute x12, starting transfers between devices, shifted(): return lax.ppermute(value, axis, [(i, i ^ turn) for i in range(GROUPS)])  15.2 us
    pallas_call x14, Pallas kernels, plain(): pl.pallas_call(kernel, in_specs=specs, out_specs=out_specs, out_shape=out...  14.2 us
    all_to_all x1, starting transfers between devices, step(): lax.all_to_all(gram, 'frames', split_axis=0, concat_axis=0, tiled=True)  9.69 us
    ppermute x12, waiting for transfers between devices, shifted(): return lax.ppermute(value, axis, [(i, i ^ turn) for i in range(GROUPS)])  7.73 us
    ppermute x1, starting transfers between devices, beside(): far = lax.ppermute(value, 'frames', outer)  7.58 us
    all_to_all x1, waiting for transfers between devices, step(): lax.all_to_all(gram, 'frames', split_axis=0, concat_axis=0, tiled=True)  4.52 us
    ppermute x1, waiting for transfers between devices, step(): u_right = lax.ppermute(u, 'frames', [(i + 1, i) for i in range(count - 1)])  3.27 us
    ppermute x1, starting transfers between devices, step(): u_right = lax.ppermute(u, 'frames', [(i + 1, i) for i in range(count - 1)])  2.82 us
  transfers between devices with their start and end apart: 16, of which 9 were waited for; matrix products, arithmetic and copies ran while one was open for 0% of the time, Pallas kernels for 11%

profile of v4, /device:TPU:1, one launch (start us, length us, event | category | flops | bytes accessed | tf_op | source)
XLA Modules:
  0.0 67.5 jit_solution(4208952528634087266)
XLA Ops:
  0.6 1.8 %shard_map.113 = (f32[24,1024]{1,0:T(8,128)S(1)}, s32[1,8192]{1,0:T(1,128)S(1)}, s32[1,8192]{1,0:T(1,128)S(1)}, f32[2,8192]{1,0:T(2,128)S(1)}, f32[2,24,8192]{2,1,0:T(8,128)S(1)}) custom-call(s32[4]{0:T(128)} %count_hbm.1, s32[1,8192]{1,0:T(1,128)} %bitcast.14, s32[1,8192]{1,0:T(1,128)} %bitcast.15, f32[2,8192]{1,0:T(2,128)} %res_hbm.1, f32[2,24,8192]{2,1,0:T(8,128)} %jp_hbm.1), custom_call_target="tpu_custom_call" | custom-call | flops 201326592 | bytes 1572864 | tf_op jit(solution)/shard_map/pallas_call | solution.py:307
  2.5 3.6 %collective-permute-start = (f32[24,1024]{1,0:T(8,128)S(1)}, f32[24,1024]{1,0:T(8,128)S(1)}, u32[]{:S(2)}, u32[]{:S(2)}) collective-permute-start(f32[24,1024]{1,0:T(8,128)S(1)} %get-tuple-element.23), channel_id=1, source_target_pairs={{0,2},{1,3},{2,0},{3,1},{4,6},{5,7},{6,4},{7,5},{8,10},{9,11},{10,... | collective-permute-start | bytes 294920 | tf_op jit(solution)/shard_map/ppermute | solution.py:282
  6.1 0.9 %shard_map.114 = (f32[24,1024]{1,0:T(8,128)S(1)}, f32[24,1024]{1,0:T(8,128)S(1)}) custom-call(s32[1,8192]{1,0:T(1,128)S(1)} %get-tuple-element.19.ids_ref.pid_ref, f32[2,8192]{1,0:T(2,128)S(1)} %get-tuple-element.21.res_ref, f32[2,24,8192]{2,1,0:T(8,128)S(1)} %get-tuple-element.22.jp_ref), custom_call_target="tpu_custom_call" | custom-call | flops 402653184 | bytes 786432 | tf_op jit(solution)/shard_map/pallas_call | solution.py:307
  7.0 0.4 collective-permute-start.1
  7.4 0.6 collective-permute-start.2
  8.0 0.5 shard_map.115.d_ref
  8.5 2.1 %collective-permute-done.1.b_ref = f32[24,1024]{1,0:T(8,128)S(1)} collective-permute-done((f32[24,1024]{1,0:T(8,128)S(1)}, f32[24,1024]{1,0:T(8,128)S(1)}, u32[]{:S(2)}, u32[]{:S(2)}) %collective-permute-start.1) | collective-permute-done | bytes 98336 | tf_op jit(solution)/shard_map/ppermute | solution.py:282
  10.6 1.4 %collective-permute-done.2.c_ref = f32[24,1024]{1,0:T(8,128)S(1)} collective-permute-done((f32[24,1024]{1,0:T(8,128)S(1)}, f32[24,1024]{1,0:T(8,128)S(1)}, u32[]{:S(2)}, u32[]{:S(2)}) %collective-permute-start.2) | collective-permute-done | bytes 98336 | tf_op jit(solution)/shard_map/ppermute | solution.py:282
  12.4 0.7 %collective-permute-start.3 = (f32[24,1024]{1,0:T(8,128)S(1)}, f32[24,1024]{1,0:T(8,128)S(1)}, u32[]{:S(2)}, u32[]{:S(2)}) collective-permute-start(f32[24,1024]{1,0:T(8,128)S(1)} %shard_map.116.rest_0_.ps_ref), channel_id=1, source_target_pairs={{0,1},{1,0},{2,3},{3,2},{4,5},{5,4},{6,7},{7,6},{8,9},{9,8},{10,11... | collective-permute-start | bytes 294920 | tf_op jit(solution)/shard_map/ppermute | solution.py:282
  13.1 1.4 %collective-permute-start.4 = (f32[24,1024]{1,0:T(8,128)S(1)}, f32[24,1024]{1,0:T(8,128)S(1)}, u32[]{:S(2)}, u32[]{:S(2)}) collective-permute-start(f32[24,1024]{1,0:T(8,128)S(1)} %shard_map.116.rest_0_.ps_ref), channel_id=1, source_target_pairs={{0,3},{1,2},{2,1},{3,0},{4,7},{5,6},{6,5},{7,4},{8,11},{9,10},{10,... | collective-permute-start | bytes 294920 | tf_op jit(solution)/shard_map/ppermute | solution.py:282
  14.6 1.2 %collective-permute-start.5 = (f32[24,1024]{1,0:T(8,128)S(1)}, f32[24,1024]{1,0:T(8,128)S(1)}, u32[]{:S(2)}, u32[]{:S(2)}) collective-permute-start(f32[24,1024]{1,0:T(8,128)S(1)} %shard_map.116.rest_0_.ps_ref), channel_id=1, source_target_pairs={{0,2},{1,3},{2,0},{3,1},{4,6},{5,7},{6,4},{7,5},{8,10},{9,11},{10,... | collective-permute-start | bytes 294920 | tf_op jit(solution)/shard_map/ppermute | solution.py:282
  16.0 0.7 %shard_map.117.rest_0_ = f32[6,256]{1,0:T(8,128)S(1)} custom-call(s32[1,8192]{1,0:T(1,128)S(1)} %get-tuple-element.19.ids_ref.pid_ref, s32[1,8192]{1,0:T(1,128)S(1)} %get-tuple-element.20.fid_ref, f32[2,8192]{1,0:T(2,128)S(1)} %get-tuple-element.21.res_ref, f32[2,24,8192]{2,1,0:T(8,128)S(1)} %get-tuple-element.22.jp_ref, f32[2,6,8192]{2,1,0:T(8,128)S(1)} %copy.20.jc_ref, ...), custom_call_target="tpu_custom_call" | custom-call | flops 268435456 | bytes 524288 | tf_op jit(solution)/shard_map/pallas_call | solution.py:307
  16.7 0.8 %shard_map.118.rest_0_ = f32[6,256]{1,0:T(8,128)S(1)} custom-call(s32[1,8192]{1,0:T(1,128)S(1)} %get-tuple-element.19.ids_ref.pid_ref, s32[1,8192]{1,0:T(1,128)S(1)} %get-tuple-element.20.fid_ref, f32[2,8192]{1,0:T(2,128)S(1)} %get-tuple-element.21.res_ref, f32[2,24,8192]{2,1,0:T(8,128)S(1)} %get-tuple-element.22.jp_ref, f32[2,6,8192]{2,1,0:T(8,128)S(1)} %copy.20.jc_ref, ...), custom_call_target="tpu_custom_call" | custom-call | flops 268435456 | bytes 524288 | tf_op jit(solution)/shard_map/pallas_call | solution.py:307
  17.8 0.7 %shard_map.119.rest_0_ = f32[6,256]{1,0:T(8,128)S(1)} custom-call(s32[1,8192]{1,0:T(1,128)S(1)} %get-tuple-element.19.ids_ref.pid_ref, s32[1,8192]{1,0:T(1,128)S(1)} %get-tuple-element.20.fid_ref, f32[2,8192]{1,0:T(2,128)S(1)} %get-tuple-element.21.res_ref, f32[2,24,8192]{2,1,0:T(8,128)S(1)} %get-tuple-element.22.jp_ref, f32[2,6,8192]{2,1,0:T(8,128)S(1)} %copy.20.jc_ref, ...), custom_call_target="tpu_custom_call" | custom-call | flops 268435456 | bytes 524288 | tf_op jit(solution)/shard_map/pallas_call | solution.py:307
  18.5 1.5 %collective-permute-done.5.rest_1_ = f32[24,1024]{1,0:T(8,128)S(1)} collective-permute-done((f32[24,1024]{1,0:T(8,128)S(1)}, f32[24,1024]{1,0:T(8,128)S(1)}, u32[]{:S(2)}, u32[]{:S(2)}) %collective-permute-start.5) | collective-permute-done | bytes 98336 | tf_op jit(solution)/shard_map/ppermute | solution.py:282
  20.0 0.7 %shard_map.120.a_ref = f32[6,256]{1,0:T(8,128)S(1)} custom-call(s32[1,8192]{1,0:T(1,128)S(1)} %get-tuple-element.19.ids_ref.pid_ref, s32[1,8192]{1,0:T(1,128)S(1)} %get-tuple-element.20.fid_ref, f32[2,8192]{1,0:T(2,128)S(1)} %get-tuple-element.21.res_ref, f32[2,24,8192]{2,1,0:T(8,128)S(1)} %get-tuple-element.22.jp_ref, f32[2,6,8192]{2,1,0:T(8,128)S(1)} %copy.20.jc_ref, ...), custom_call_target="tpu_custom_call" | custom-call | flops 268435456 | bytes 524288 | tf_op jit(solution)/shard_map/pallas_call | solution.py:307
  20.8 2.5 %collective-permute-start.7 = (f32[6,256]{1,0:T(8,128)S(1)}, f32[6,256]{1,0:T(8,128)S(1)}, u32[]{:S(2)}, u32[]{:S(2)}) collective-permute-start(f32[6,256]{1,0:T(8,128)S(1)} %shard_map.120.a_ref), channel_id=1, source_target_pairs={{0,2},{1,3},{2,0},{3,1},{4,6},{5,7},{6,4},{7,5},{8,10},{9,11},{10,... | collective-permute-start | bytes 18440 | tf_op jit(solution)/shard_map/ppermute | solution.py:282
  23.3 1.3 %collective-permute-start.8 = (f32[6,256]{1,0:T(8,128)S(1)}, f32[6,256]{1,0:T(8,128)S(1)}, u32[]{:S(2)}, u32[]{:S(2)}) collective-permute-start(f32[6,256]{1,0:T(8,128)S(1)} %shard_map.120.a_ref), channel_id=1, source_target_pairs={{0,3},{1,2},{2,1},{3,0},{4,7},{5,6},{6,5},{7,4},{8,11},{9,10},{10,... | collective-permute-start | bytes 18440 | tf_op jit(solution)/shard_map/ppermute | solution.py:282
  24.9 2.2 %collective-permute-done.8.d_ref = f32[6,256]{1,0:T(8,128)S(1)} collective-permute-done((f32[6,256]{1,0:T(8,128)S(1)}, f32[6,256]{1,0:T(8,128)S(1)}, u32[]{:S(2)}, u32[]{:S(2)}) %collective-permute-start.8) | collective-permute-done | bytes 6176 | tf_op jit(solution)/shard_map/ppermute | solution.py:282
  27.1 7.6 %collective-permute-start.9 = (f32[8,256]{1,0:T(8,128)S(1)}, f32[8,256]{1,0:T(8,128)S(1)}, u32[]{:S(2)}, u32[]{:S(2)}) collective-permute-start(f32[8,256]{1,0:T(8,128)S(1)} %get-tuple-element.26.z_ref), channel_id=1, source_target_pairs={{4,8},{8,4},{12,16},{16,12},{20,24},{24,20},{28,32},{32,28},{36,40... | collective-permute-start | bytes 24584 | tf_op jit(solution)/shard_map/ppermute | solution.py:289
  34.8 1.2 %collective-permute-done.9.outer_ref = f32[8,256]{1,0:T(8,128)S(1)} collective-permute-done((f32[8,256]{1,0:T(8,128)S(1)}, f32[8,256]{1,0:T(8,128)S(1)}, u32[]{:S(2)}, u32[]{:S(2)}) %collective-permute-start.9) | collective-permute-done | bytes 8224 | tf_op jit(solution)/shard_map/ppermute | solution.py:289
  36.0 0.8 %shard_map.122 = (f32[6,256]{1,0:T(8,128)S(1)}, f32[8,256]{1,0:T(8,128)S(1)}) custom-call(f32[8,256]{1,0:T(8,128)S(1)} %get-tuple-element.26.z_ref, f32[8,256]{1,0:T(8,128)S(1)} %collective-permute-done.9.outer_ref, f32[8,256]{1,0:T(8,128)S(1)} %collective-permute-done.10.inner_ref, f32[6,6,127,256]{3,2,1,0:T(8,128)S(1)} %bitcast.10, f32[6,6,256]{2,1,0:T(8,128)S(1)} %copy-done.1), custom_call_target="tpu_custom_call" | custom-call | flops 2340864 | bytes 4681728 | tf_op jit(solution)/shard_map/pallas_call | solution.py:307
  36.8 2.5 %shard_map.124 = (f32[48,1024]{1,0:T(8,128)S(1)}, f32[48,1024]{1,0:T(8,128)S(1)}, f32[48,1024]{1,0:T(8,128)S(1)}, f32[48,1024]{1,0:T(8,128)S(1)}) custom-call(s32[1,8192]{1,0:T(1,128)S(1)} %get-tuple-element.19.ids_ref.pid_ref, s32[1,8192]{1,0:T(1,128)S(1)} %get-tuple-element.20.fid_ref, f32[2,24,8192]{2,1,0:T(8,128)S(1)} %get-tuple-element.22.jp_ref, ...), custom_call_target="tpu_custom_call" | custom-call | flops 1677721600 | bytes 2097152 | tf_op jit(solution)/shard_map/pallas_call | solution.py:307
  39.4 2.0 %collective-permute-start.12 = (f32[48,1024]{1,0:T(8,128)S(1)}, f32[48,1024]{1,0:T(8,128)S(1)}, u32[]{:S(2)}, u32[]{:S(2)}) collective-permute-start(f32[48,1024]{1,0:T(8,128)S(1)} %get-tuple-element.31), channel_id=1, source_target_pairs={{0,3},{1,2},{2,1},{3,0},{4,7},{5,6},{6,5},{7,4},{8,11},{9,10},{10,... | collective-permute-start | bytes 589832 | tf_op jit(solution)/shard_map/ppermute | solution.py:282
  41.4 1.3 %collective-permute-start.14 = (f32[48,1024]{1,0:T(8,128)S(1)}, f32[48,1024]{1,0:T(8,128)S(1)}, u32[]{:S(2)}, u32[]{:S(2)}) collective-permute-start(f32[48,1024]{1,0:T(8,128)S(1)} %get-tuple-element.33), channel_id=1, source_target_pairs={{0,1},{1,0},{2,3},{3,2},{4,5},{5,4},{6,7},{7,6},{8,9},{9,8},{10,11... | collective-permute-start | bytes 589832 | tf_op jit(solution)/shard_map/ppermute | solution.py:282
  42.7 2.8 %collective-permute-start.11 = (f32[8,256]{1,0:T(8,128)S(1)}, f32[8,256]{1,0:T(8,128)S(1)}, u32[]{:S(2)}, u32[]{:S(2)}) collective-permute-start(f32[8,256]{1,0:T(8,128)S(1)} %get-tuple-element.27.u_ref), channel_id=1, source_target_pairs={{4,0},{8,4},{12,8},{16,12},{20,16},{24,20},{28,24},{32,28},{36,32}... | collective-permute-start | bytes 24584 | tf_op jit(solution)/shard_map/ppermute | solution.py:385
  45.5 3.3 %collective-permute-done.11.right_ref = f32[8,256]{1,0:T(8,128)S(1)} collective-permute-done((f32[8,256]{1,0:T(8,128)S(1)}, f32[8,256]{1,0:T(8,128)S(1)}, u32[]{:S(2)}, u32[]{:S(2)}) %collective-permute-start.11) | collective-permute-done | bytes 8224 | tf_op jit(solution)/shard_map/ppermute | solution.py:385
  48.8 1.3 %shard_map.123 = f32[32,128]{1,0:T(8,128)} custom-call(f32[8,256]{1,0:T(8,128)S(1)} %get-tuple-element.27.u_ref, f32[8,256]{1,0:T(8,128)S(1)} %collective-permute-done.11.right_ref, f32[6,6,127,256]{3,2,1,0:T(8,128)S(1)} %bitcast.11, f32[6,256]{1,0:T(8,128)S(1)} %get-tuple-element.28.r_ref, f32[8,256]{1,0:T(8,128)S(1)} %get-tuple-element.26.z_ref, ...), custom_call_target="tpu_custom_call" | custom-call | flops 1170432 | bytes 2340864 | tf_op jit(solution)/shard_map/pallas_call | solution.py:307
  50.1 9.7 %all-to-all-start = ((f32[32,1,128]{2,1,0:T(1,128)}), f32[32,1,128]{2,1,0:T(1,128)S(1)}, u32[]{:S(2)}, u32[]{:S(2)}) async-start(f32[32,1,128]{2,1,0:T(1,128)} %bitcast.5), calls=%async_computation | async-start | bytes 32768 | tf_op jit(solution)/shard_map/all_to_all | solution.py:401
  59.8 2.3 %shard_map.125 = (f32[24,1024]{1,0:T(8,128)S(1)}, f32[24,1024]{1,0:T(8,128)S(1)}) custom-call(f32[48,1024]{1,0:T(8,128)S(1)} %get-tuple-element.30.a_ref, f32[48,1024]{1,0:T(8,128)S(1)} %collective-permute-done.12.b_ref, f32[48,1024]{1,0:T(8,128)S(1)} %collective-permute-done.13.c_ref, f32[48,1024]{1,0:T(8,128)S(1)} %collective-permute-done.14.d_ref, ...), custom_call_target="tpu_custom_call" | custom-call | flops 2359296 | bytes 2359296 | tf_op jit(solution)/shard_map/pallas_call | solution.py:307
  62.2 4.5 %all-to-all-done = f32[32,1,128]{2,1,0:T(1,128)S(1)} async-done(((f32[32,1,128]{2,1,0:T(1,128)}), f32[32,1,128]{2,1,0:T(1,128)S(1)}, u32[]{:S(2)}, u32[]{:S(2)}) %all-to-all-start) | async-done | bytes 16416 | tf_op jit(solution)/shard_map/all_to_all | solution.py:401
  66.7 0.8 %shard_map.126 = (f32[6,256]{1,0:T(8,128)}, f32[24,1024]{1,0:T(8,128)}) custom-call(f32[32,128]{1,0:T(8,128)S(1)} %bitcast.12, f32[8,256]{1,0:T(8,128)S(1)} %get-tuple-element.26.z_ref, f32[8,256]{1,0:T(8,128)S(1)} %get-tuple-element.27.u_ref, f32[24,1024]{1,0:T(8,128)S(1)} %shard_map.116.rest_0_.ps_ref, f32[24,1024]{1,0:T(8,128)S(1)} %get-tuple-element.34.pz_ref, ...), custom_call_target="tpu_custom_call" | custom-call | flops 147456 | bytes 589824 | tf_op jit(solution)/shard_map/pallas_call | solution.py:307
  (28 shorter events, 1.3 us)
Async XLA Ops:
  0.6 11.4 %copy-start = (f32[24,24,1024]{2,1,0:T(8,128)S(1)}, f32[24,24,1024]{2,1,0:T(8,128)}, u32[]{:S(2)}) copy-start(f32[24,24,1024]{2,1,0:T(8,128)} %inv_hbm.1) | copy-start | bytes 7077892
  2.5 6.1 %collective-permute-start = (f32[24,1024]{1,0:T(8,128)S(1)}, f32[24,1024]{1,0:T(8,128)S(1)}, u32[]{:S(2)}, u32[]{:S(2)}) collective-permute-start(f32[24,1024]{1,0:T(8,128)S(1)} %get-tuple-element.23), channel_id=1, source_target_pairs={{0,2},{1,3},{2,0},{3,1},{4,6},{5,7},{6,4},{7,5},{8,10},{9,11},{10,... | collective-permute-start | bytes 294920 | tf_op jit(solution)/shard_map/ppermute | solution.py:282
  7.0 8.8 %copy-start.3 = (f32[2,6,8192]{2,0,1:T(2,128)S(1)}, f32[2,6,8192]{2,0,1:T(2,128)}, u32[]{:S(2)}) copy-start(f32[2,6,8192]{2,0,1:T(2,128)} %param.13) | copy-start | bytes 1179652
  7.0 3.6 %collective-permute-start.1 = (f32[24,1024]{1,0:T(8,128)S(1)}, f32[24,1024]{1,0:T(8,128)S(1)}, u32[]{:S(2)}, u32[]{:S(2)}) collective-permute-start(f32[24,1024]{1,0:T(8,128)S(1)} %get-tuple-element.24), channel_id=1, source_target_pairs={{0,1},{1,0},{2,3},{3,2},{4,5},{5,4},{6,7},{7,6},{8,9},{9,8},{10,11... | collective-permute-start | bytes 294920 | tf_op jit(solution)/shard_map/ppermute | solution.py:282
  7.4 4.7 %collective-permute-start.2 = (f32[24,1024]{1,0:T(8,128)S(1)}, f32[24,1024]{1,0:T(8,128)S(1)}, u32[]{:S(2)}, u32[]{:S(2)}) collective-permute-start(f32[24,1024]{1,0:T(8,128)S(1)} %get-tuple-element.25), channel_id=1, source_target_pairs={{0,3},{1,2},{2,1},{3,0},{4,7},{5,6},{6,5},{7,4},{8,11},{9,10},{10,... | collective-permute-start | bytes 294920 | tf_op jit(solution)/shard_map/ppermute | solution.py:282
  8.0 28.0 %slice-start = ((s8[4718592]{0:T(1024)(128)(4,1)}), s8[4194304]{0:T(1024)(128)(4,1)S(1)}, s32[]{:S(2)}) async-start(s8[4718592]{0:T(1024)(128)(4,1)} %bitcast.8), calls=%async_computation.1 | async-start | bytes 8388608
  12.4 4.3 %collective-permute-start.3 = (f32[24,1024]{1,0:T(8,128)S(1)}, f32[24,1024]{1,0:T(8,128)S(1)}, u32[]{:S(2)}, u32[]{:S(2)}) collective-permute-start(f32[24,1024]{1,0:T(8,128)S(1)} %shard_map.116.rest_0_.ps_ref), channel_id=1, source_target_pairs={{0,1},{1,0},{2,3},{3,2},{4,5},{5,4},{6,7},{7,6},{8,9},{9,8},{10,11... | collective-permute-start | bytes 294920 | tf_op jit(solution)/shard_map/ppermute | solution.py:282
  13.1 4.7 %collective-permute-start.4 = (f32[24,1024]{1,0:T(8,128)S(1)}, f32[24,1024]{1,0:T(8,128)S(1)}, u32[]{:S(2)}, u32[]{:S(2)}) collective-permute-start(f32[24,1024]{1,0:T(8,128)S(1)} %shard_map.116.rest_0_.ps_ref), channel_id=1, source_target_pairs={{0,3},{1,2},{2,1},{3,0},{4,7},{5,6},{6,5},{7,4},{8,11},{9,10},{10,... | collective-permute-start | bytes 294920 | tf_op jit(solution)/shard_map/ppermute | solution.py:282
  14.6 5.5 %collective-permute-start.5 = (f32[24,1024]{1,0:T(8,128)S(1)}, f32[24,1024]{1,0:T(8,128)S(1)}, u32[]{:S(2)}, u32[]{:S(2)}) collective-permute-start(f32[24,1024]{1,0:T(8,128)S(1)} %shard_map.116.rest_0_.ps_ref), channel_id=1, source_target_pairs={{0,2},{1,3},{2,0},{3,1},{4,6},{5,7},{6,4},{7,5},{8,10},{9,11},{10,... | collective-permute-start | bytes 294920 | tf_op jit(solution)/shard_map/ppermute | solution.py:282
  16.0 20.0 %slice-start.1 = ((s8[4718592]{0:T(1024)(128)(4,1)}), s8[524288]{0:T(1024)(128)(4,1)S(1)}, s32[]{:S(2)}) async-start(s8[4718592]{0:T(1024)(128)(4,1)} %bitcast.8), calls=%async_computation.2 | async-start | bytes 1048576
  17.5 9.6 %copy-start.1 = (f32[6,6,256]{2,1,0:T(8,128)S(1)}, f32[6,6,256]{2,1,0:T(8,128)}, u32[]{:S(2)}) copy-start(f32[6,6,256]{2,1,0:T(8,128)} %pre_ref.3) | copy-start | bytes 110596
  17.5 9.6 %copy-start.2 = (f32[256]{0:T(256)S(1)}, f32[256]{0:T(256)}, u32[]{:S(2)}) copy-start(f32[256]{0:T(256)} %param.18) | copy-start | bytes 3076
  20.7 3.9 %collective-permute-start.6 = (f32[6,256]{1,0:T(8,128)S(1)}, f32[6,256]{1,0:T(8,128)S(1)}, u32[]{:S(2)}, u32[]{:S(2)}) collective-permute-start(f32[6,256]{1,0:T(8,128)S(1)} %shard_map.120.a_ref), channel_id=1, source_target_pairs={{0,1},{1,0},{2,3},{3,2},{4,5},{5,4},{6,7},{7,6},{8,9},{9,8},{10,11... | collective-permute-start | bytes 18440 | tf_op jit(solution)/shard_map/ppermute | solution.py:282
  20.8 4.1 %collective-permute-start.7 = (f32[6,256]{1,0:T(8,128)S(1)}, f32[6,256]{1,0:T(8,128)S(1)}, u32[]{:S(2)}, u32[]{:S(2)}) collective-permute-start(f32[6,256]{1,0:T(8,128)S(1)} %shard_map.120.a_ref), channel_id=1, source_target_pairs={{0,2},{1,3},{2,0},{3,1},{4,6},{5,7},{6,4},{7,5},{8,10},{9,11},{10,... | collective-permute-start | bytes 18440 | tf_op jit(solution)/shard_map/ppermute | solution.py:282
  23.3 3.7 %collective-permute-start.8 = (f32[6,256]{1,0:T(8,128)S(1)}, f32[6,256]{1,0:T(8,128)S(1)}, u32[]{:S(2)}, u32[]{:S(2)}) collective-permute-start(f32[6,256]{1,0:T(8,128)S(1)} %shard_map.120.a_ref), channel_id=1, source_target_pairs={{0,3},{1,2},{2,1},{3,0},{4,7},{5,6},{6,5},{7,4},{8,11},{9,10},{10,... | collective-permute-start | bytes 18440 | tf_op jit(solution)/shard_map/ppermute | solution.py:282
  27.1 8.9 %collective-permute-start.9 = (f32[8,256]{1,0:T(8,128)S(1)}, f32[8,256]{1,0:T(8,128)S(1)}, u32[]{:S(2)}, u32[]{:S(2)}) collective-permute-start(f32[8,256]{1,0:T(8,128)S(1)} %get-tuple-element.26.z_ref), channel_id=1, source_target_pairs={{4,8},{8,4},{12,16},{16,12},{20,24},{24,20},{28,32},{32,28},{36,40... | collective-permute-start | bytes 24584 | tf_op jit(solution)/shard_map/ppermute | solution.py:289
  34.7 1.3 %collective-permute-start.10 = (f32[8,256]{1,0:T(8,128)S(1)}, f32[8,256]{1,0:T(8,128)S(1)}, u32[]{:S(2)}, u32[]{:S(2)}) collective-permute-start(f32[8,256]{1,0:T(8,128)S(1)} %get-tuple-element.26.z_ref), channel_id=1, source_target_pairs={{0,4},{4,0},{8,12},{12,8},{16,20},{20,16},{24,28},{28,24},{32,36},... | collective-permute-start | bytes 24584 | tf_op jit(solution)/shard_map/ppermute | solution.py:290
  39.4 20.4 %collective-permute-start.12 = (f32[48,1024]{1,0:T(8,128)S(1)}, f32[48,1024]{1,0:T(8,128)S(1)}, u32[]{:S(2)}, u32[]{:S(2)}) collective-permute-start(f32[48,1024]{1,0:T(8,128)S(1)} %get-tuple-element.31), channel_id=1, source_target_pairs={{0,3},{1,2},{2,1},{3,0},{4,7},{5,6},{6,5},{7,4},{8,11},{9,10},{10,... | collective-permute-start | bytes 589832 | tf_op jit(solution)/shard_map/ppermute | solution.py:282
  41.4 18.4 %collective-permute-start.13 = (f32[48,1024]{1,0:T(8,128)S(1)}, f32[48,1024]{1,0:T(8,128)S(1)}, u32[]{:S(2)}, u32[]{:S(2)}) collective-permute-start(f32[48,1024]{1,0:T(8,128)S(1)} %get-tuple-element.32), channel_id=1, source_target_pairs={{0,2},{1,3},{2,0},{3,1},{4,6},{5,7},{6,4},{7,5},{8,10},{9,11},{10,... | collective-permute-start | bytes 589832 | tf_op jit(solution)/shard_map/ppermute | solution.py:282
  41.4 18.5 %collective-permute-start.14 = (f32[48,1024]{1,0:T(8,128)S(1)}, f32[48,1024]{1,0:T(8,128)S(1)}, u32[]{:S(2)}, u32[]{:S(2)}) collective-permute-start(f32[48,1024]{1,0:T(8,128)S(1)} %get-tuple-element.33), channel_id=1, source_target_pairs={{0,1},{1,0},{2,3},{3,2},{4,5},{5,4},{6,7},{7,6},{8,9},{9,8},{10,11... | collective-permute-start | bytes 589832 | tf_op jit(solution)/shard_map/ppermute | solution.py:282
  42.7 6.1 %collective-permute-start.11 = (f32[8,256]{1,0:T(8,128)S(1)}, f32[8,256]{1,0:T(8,128)S(1)}, u32[]{:S(2)}, u32[]{:S(2)}) collective-permute-start(f32[8,256]{1,0:T(8,128)S(1)} %get-tuple-element.27.u_ref), channel_id=1, source_target_pairs={{4,0},{8,4},{12,8},{16,12},{20,16},{24,20},{28,24},{32,28},{36,32}... | collective-permute-start | bytes 24584 | tf_op jit(solution)/shard_map/ppermute | solution.py:385
  50.1 16.6 %all-to-all-start = ((f32[32,1,128]{2,1,0:T(1,128)}), f32[32,1,128]{2,1,0:T(1,128)S(1)}, u32[]{:S(2)}, u32[]{:S(2)}) async-start(f32[32,1,128]{2,1,0:T(1,128)} %bitcast.5), calls=%async_computation | async-start | bytes 32768 | tf_op jit(solution)/shard_map/all_to_all | solution.py:401

commit v5 on v4

--- a/solution.py
+++ b/solution.py
@@ -20,6 +20,10 @@
 GROUPS = 4
 LO = 256
 HI = PT // LO
+SUM_TURNS = ((2, 2), (1, 3), (3, 1))
+SOLVED_TURNS = ((3, 1), (1, 3), (2, 2))
+CAMERA_TURNS = ((3, 1), (2, 2), (1, 3))
+SELF = ((0, 0),)
 LIMIT = pltpu.CompilerParams(vmem_limit_bytes=12 * 2**20)
 
 
@@ -85,7 +89,8 @@
 
 
 def block_at(turn):
-    return lax.bitwise_xor(lax.axis_index("points"), abs(turn))
+    first = lax.rem(lax.axis_index("frames"), 2) == 0
+    return lax.bitwise_xor(lax.axis_index("points"), jnp.where(first, turn[0], turn[1]))
 
 
 def lanes(b):
@@ -109,7 +114,7 @@
     count_hbm, pid_hbm, fid_hbm, res_hbm, jp_hbm, out_ref, pid_ref, fid_ref, res_ref, jp_ref, count_ref, sems
 ):
     small = [(count_hbm, count_ref), (pid_hbm, pid_ref), (res_hbm, res_ref), (fid_hbm, fid_ref)]
-    blocks = [block_at(turn) for turn in (2, 1, 3, 0)]
+    blocks = [block_at(turn) for turn in SUM_TURNS + SELF]
     large = [(jp_hbm.at[:, :, lanes(b)], jp_ref.at[:, :, lanes(b)]) for b in blocks]
     copies = fetch(small[:3] + large[:1] + small[3:] + large[1:], sems)
     for copy in copies[:3]:
@@ -244,7 +249,7 @@
 def back_kernel(pid_ref, fid_ref, jp_ref, jc_ref, z_ref, u_ref, *outs):
     parts = halves(jnp.concatenate([z_ref[...], u_ref[...]], axis=0))
     for j in range(GROUPS):
-        b = block_at(GROUPS - 1 - j)
+        b = block_at((GROUPS - 1 - j,) * 2)
         at = lanes(b)
         table = one_hot(fid_ref[:, at].astype(F32), FR)
         got = lax.dot_general(parts, table, (((1,), (0,)), ((), ())), preferred_element_type=F32)
@@ -278,8 +283,13 @@
     pt_ref[...] = ps_ref[...] - c0 * pz_ref[...] - c1 * pu_ref[...]
 
 
-def shifted(value, axis, turn):
-    return lax.ppermute(value, axis, [(i, i ^ turn) for i in range(GROUPS)])
+def swapped(value, turn):
+    pairs = [
+        (GROUPS * f + p, GROUPS * f + (p ^ turn[f % 2]))
+        for f in range(lax.axis_size("frames"))
+        for p in range(GROUPS)
+    ]
+    return lax.ppermute(value, ("frames", "points"), pairs)
 
 
 def beside(value):
@@ -350,18 +360,18 @@
         est=cost(2 * 192 * 256 * 2048 * len(turns), 2 * 24 * 2048 * 4 * len(turns)),
     )
     got = []
-    for turn, sums in zip((2, 1, 3), [far, *grad(1, 3)]):
-        got.append(shifted(sums, "points", turn))
-    got.extend(grad(0))
+    for n, sums in enumerate([far, *grad(*SUM_TURNS[1:])]):
+        got.append(swapped(sums, SUM_TURNS[n]))
+    got.extend(grad(*SELF))
     solved = plain(
         solve_kernel, sds(Q, PT), (*got, point_inv), est=cost(2 * Q * Q * PT, Q * Q * PT * 4)
     )
     partial = ()
-    for s in (0, 1, 3, 2):
-        piece = shifted(solved, "points", s) if s else solved
+    for n, turn in enumerate(SELF + SOLVED_TURNS):
+        piece = swapped(solved, turn) if n else solved
         partial = (
             plain(
-                functools.partial(rhs_kernel, -s),
+                functools.partial(rhs_kernel, turn),
                 sds(CP, FR),
                 (pid, fid, res, jac, jac_cam, *partial, piece),
                 est=cost(2 * 256 * 256 * 2048, 2 * 32 * 2048 * 4),
@@ -369,8 +379,8 @@
         )
     (partial,) = partial
     parts = [partial]
-    for s in (1, 2, 3):
-        parts.append(shifted(partial, "points", s))
+    for turn in CAMERA_TURNS:
+        parts.append(swapped(partial, turn))
 
     rhs, z = plain(
         start_kernel, [sds(CP, FR), sds(8, FR)], (*parts, precond, edge), est=cost(20000, 100000)
@@ -391,7 +401,7 @@
     )
     returned = [back[GROUPS - 1]]
     for s in (3, 2, 1):
-        returned.append(shifted(back[GROUPS - 1 - s], "points", s))
+        returned.append(swapped(back[GROUPS - 1 - s], (s, s)))
     gram = plain(
         second_kernel,
         sds(count, 128),

time: 67.7 us -> 66.3 us (0.979)
  waiting for transfers between devices: 16.8 us -> 16.1 us
  starting transfers between devices: 35.4 us -> 34.7 us
    ppermute x1, starting transfers between devices: 7.58 us -> 6.8 us  [beside(): far = lax.ppermute(value, 'frames', outer)]
    ppermute x12, waiting for transfers between devices: 7.73 us -> 7.04 us  [swapped(): return lax.ppermute(value, ('frames', 'points'), pairs)]
where the time goes in v5:
time: 66.3 us; the launch traced here: 66.1 us
  starting transfers between devices  34.7 us (52%)
  waiting for transfers between devices  16.1 us (24%)
  Pallas kernels  14.2 us (21%)
  between operations  0.8 us (1%)
    ppermute x12, starting transfers between devices, swapped(): return lax.ppermute(value, ('frames', 'points'), pairs)  15.3 us
    pallas_call x14, Pallas kernels, plain(): pl.pallas_call(kernel, in_specs=specs, out_specs=out_specs, out_shape=out...  14.2 us
    all_to_all x1, starting transfers between devices, step(): lax.all_to_all(gram, 'frames', split_axis=0, concat_axis=0, tiled=True)  9.69 us
    ppermute x12, waiting for transfers between devices, swapped(): return lax.ppermute(value, ('frames', 'points'), pairs)  7.04 us
    ppermute x1, starting transfers between devices, beside(): far = lax.ppermute(value, 'frames', outer)  6.8 us
    all_to_all x1, waiting for transfers between devices, step(): lax.all_to_all(gram, 'frames', split_axis=0, concat_axis=0, tiled=True)  4.52 us
    ppermute x1, waiting for transfers between devices, step(): u_right = lax.ppermute(u, 'frames', [(i + 1, i) for i in range(count - 1)])  3.27 us
    ppermute x1, starting transfers between devices, step(): u_right = lax.ppermute(u, 'frames', [(i + 1, i) for i in range(count - 1)])  2.82 us
  transfers between devices with their start and end apart: 16, of which 9 were waited for; matrix products, arithmetic and copies ran while one was open for 0% of the time, Pallas kernels for 11%

profile of v5, /device:TPU:1, one launch (start us, length us, event | category | flops | bytes accessed | tf_op | source)
XLA Modules:
  0.0 66.1 jit_solution(15478553846863087335)
XLA Ops:
  0.6 1.8 %shard_map.113 = (f32[24,1024]{1,0:T(8,128)S(1)}, s32[1,8192]{1,0:T(1,128)S(1)}, s32[1,8192]{1,0:T(1,128)S(1)}, f32[2,8192]{1,0:T(2,128)S(1)}, f32[2,24,8192]{2,1,0:T(8,128)S(1)}) custom-call(s32[4]{0:T(128)} %count_hbm.1, s32[1,8192]{1,0:T(1,128)} %bitcast.14, s32[1,8192]{1,0:T(1,128)} %bitcast.15, f32[2,8192]{1,0:T(2,128)} %res_hbm.1, f32[2,24,8192]{2,1,0:T(8,128)} %jp_hbm.1), custom_call_target="tpu_custom_call" | custom-call | flops 201326592 | bytes 1572864 | tf_op jit(solution)/shard_map/pallas_call | solution.py:317
  2.5 3.6 %collective-permute-start = (f32[24,1024]{1,0:T(8,128)S(1)}, f32[24,1024]{1,0:T(8,128)S(1)}, u32[]{:S(2)}, u32[]{:S(2)}) collective-permute-start(f32[24,1024]{1,0:T(8,128)S(1)} %get-tuple-element.23), channel_id=1, source_target_pairs={{0,2},{1,3},{2,0},{3,1},{4,6},{5,7},{6,4},{7,5},{8,10},{9,11},{10,... | collective-permute-start | bytes 294920 | tf_op jit(solution)/shard_map/ppermute | solution.py:292
  6.1 0.9 %shard_map.114 = (f32[24,1024]{1,0:T(8,128)S(1)}, f32[24,1024]{1,0:T(8,128)S(1)}) custom-call(s32[1,8192]{1,0:T(1,128)S(1)} %get-tuple-element.19.ids_ref.pid_ref, f32[2,8192]{1,0:T(2,128)S(1)} %get-tuple-element.21.res_ref, f32[2,24,8192]{2,1,0:T(8,128)S(1)} %get-tuple-element.22.jp_ref), custom_call_target="tpu_custom_call" | custom-call | flops 402653184 | bytes 786432 | tf_op jit(solution)/shard_map/pallas_call | solution.py:317
  7.0 0.9 %collective-permute-start.1 = (f32[24,1024]{1,0:T(8,128)S(1)}, f32[24,1024]{1,0:T(8,128)S(1)}, u32[]{:S(2)}, u32[]{:S(2)}) collective-permute-start(f32[24,1024]{1,0:T(8,128)S(1)} %get-tuple-element.24), channel_id=1, source_target_pairs={{0,1},{1,0},{2,3},{3,2},{4,7},{5,6},{6,5},{7,4},{8,9},{9,8},{10,11... | collective-permute-start | bytes 294920 | tf_op jit(solution)/shard_map/ppermute | solution.py:292
  7.9 0.5 shard_map.115.d_ref
  8.5 3.3 %collective-permute-done.1.b_ref = f32[24,1024]{1,0:T(8,128)S(1)} collective-permute-done((f32[24,1024]{1,0:T(8,128)S(1)}, f32[24,1024]{1,0:T(8,128)S(1)}, u32[]{:S(2)}, u32[]{:S(2)}) %collective-permute-start.1) | collective-permute-done | bytes 98336 | tf_op jit(solution)/shard_map/ppermute | solution.py:292
  11.7 0.4 collective-permute-done.2.c_ref
  12.5 0.5 collective-permute-start.3
  13.0 1.6 %collective-permute-start.4 = (f32[24,1024]{1,0:T(8,128)S(1)}, f32[24,1024]{1,0:T(8,128)S(1)}, u32[]{:S(2)}, u32[]{:S(2)}) collective-permute-start(f32[24,1024]{1,0:T(8,128)S(1)} %shard_map.116.rest_0_.ps_ref), channel_id=1, source_target_pairs={{0,1},{1,0},{2,3},{3,2},{4,7},{5,6},{6,5},{7,4},{8,9},{9,8},{10,11... | collective-permute-start | bytes 294920 | tf_op jit(solution)/shard_map/ppermute | solution.py:292
  14.7 1.2 %collective-permute-start.5 = (f32[24,1024]{1,0:T(8,128)S(1)}, f32[24,1024]{1,0:T(8,128)S(1)}, u32[]{:S(2)}, u32[]{:S(2)}) collective-permute-start(f32[24,1024]{1,0:T(8,128)S(1)} %shard_map.116.rest_0_.ps_ref), channel_id=1, source_target_pairs={{0,2},{1,3},{2,0},{3,1},{4,6},{5,7},{6,4},{7,5},{8,10},{9,11},{10,... | collective-permute-start | bytes 294920 | tf_op jit(solution)/shard_map/ppermute | solution.py:292
  16.1 0.7 %shard_map.117.rest_0_ = f32[6,256]{1,0:T(8,128)S(1)} custom-call(s32[1,8192]{1,0:T(1,128)S(1)} %get-tuple-element.19.ids_ref.pid_ref, s32[1,8192]{1,0:T(1,128)S(1)} %get-tuple-element.20.fid_ref, f32[2,8192]{1,0:T(2,128)S(1)} %get-tuple-element.21.res_ref, f32[2,24,8192]{2,1,0:T(8,128)S(1)} %get-tuple-element.22.jp_ref, f32[2,6,8192]{2,1,0:T(8,128)S(1)} %copy.20.jc_ref, ...), custom_call_target="tpu_custom_call" | custom-call | flops 268435456 | bytes 524288 | tf_op jit(solution)/shard_map/pallas_call | solution.py:317
  16.8 0.8 %shard_map.118.rest_0_ = f32[6,256]{1,0:T(8,128)S(1)} custom-call(s32[1,8192]{1,0:T(1,128)S(1)} %get-tuple-element.19.ids_ref.pid_ref, s32[1,8192]{1,0:T(1,128)S(1)} %get-tuple-element.20.fid_ref, f32[2,8192]{1,0:T(2,128)S(1)} %get-tuple-element.21.res_ref, f32[2,24,8192]{2,1,0:T(8,128)S(1)} %get-tuple-element.22.jp_ref, f32[2,6,8192]{2,1,0:T(8,128)S(1)} %copy.20.jc_ref, ...), custom_call_target="tpu_custom_call" | custom-call | flops 268435456 | bytes 524288 | tf_op jit(solution)/shard_map/pallas_call | solution.py:317
  17.7 0.7 %shard_map.119.rest_0_ = f32[6,256]{1,0:T(8,128)S(1)} custom-call(s32[1,8192]{1,0:T(1,128)S(1)} %get-tuple-element.19.ids_ref.pid_ref, s32[1,8192]{1,0:T(1,128)S(1)} %get-tuple-element.20.fid_ref, f32[2,8192]{1,0:T(2,128)S(1)} %get-tuple-element.21.res_ref, f32[2,24,8192]{2,1,0:T(8,128)S(1)} %get-tuple-element.22.jp_ref, f32[2,6,8192]{2,1,0:T(8,128)S(1)} %copy.20.jc_ref, ...), custom_call_target="tpu_custom_call" | custom-call | flops 268435456 | bytes 524288 | tf_op jit(solution)/shard_map/pallas_call | solution.py:317
  18.4 1.3 %collective-permute-done.5.rest_1_ = f32[24,1024]{1,0:T(8,128)S(1)} collective-permute-done((f32[24,1024]{1,0:T(8,128)S(1)}, f32[24,1024]{1,0:T(8,128)S(1)}, u32[]{:S(2)}, u32[]{:S(2)}) %collective-permute-start.5) | collective-permute-done | bytes 98336 | tf_op jit(solution)/shard_map/ppermute | solution.py:292
  19.7 0.7 %shard_map.120.a_ref = f32[6,256]{1,0:T(8,128)S(1)} custom-call(s32[1,8192]{1,0:T(1,128)S(1)} %get-tuple-element.19.ids_ref.pid_ref, s32[1,8192]{1,0:T(1,128)S(1)} %get-tuple-element.20.fid_ref, f32[2,8192]{1,0:T(2,128)S(1)} %get-tuple-element.21.res_ref, f32[2,24,8192]{2,1,0:T(8,128)S(1)} %get-tuple-element.22.jp_ref, f32[2,6,8192]{2,1,0:T(8,128)S(1)} %copy.20.jc_ref, ...), custom_call_target="tpu_custom_call" | custom-call | flops 268435456 | bytes 524288 | tf_op jit(solution)/shard_map/pallas_call | solution.py:317
  20.4 1.6 %collective-permute-start.6 = (f32[6,256]{1,0:T(8,128)S(1)}, f32[6,256]{1,0:T(8,128)S(1)}, u32[]{:S(2)}, u32[]{:S(2)}) collective-permute-start(f32[6,256]{1,0:T(8,128)S(1)} %shard_map.120.a_ref), channel_id=1, source_target_pairs={{0,3},{1,2},{2,1},{3,0},{4,5},{5,4},{6,7},{7,6},{8,11},{9,10},{10,... | collective-permute-start | bytes 18440 | tf_op jit(solution)/shard_map/ppermute | solution.py:292
  22.1 0.7 %collective-permute-start.7 = (f32[6,256]{1,0:T(8,128)S(1)}, f32[6,256]{1,0:T(8,128)S(1)}, u32[]{:S(2)}, u32[]{:S(2)}) collective-permute-start(f32[6,256]{1,0:T(8,128)S(1)} %shard_map.120.a_ref), channel_id=1, source_target_pairs={{0,2},{1,3},{2,0},{3,1},{4,6},{5,7},{6,4},{7,5},{8,10},{9,11},{10,... | collective-permute-start | bytes 18440 | tf_op jit(solution)/shard_map/ppermute | solution.py:292
  22.7 1.8 %collective-permute-start.8 = (f32[6,256]{1,0:T(8,128)S(1)}, f32[6,256]{1,0:T(8,128)S(1)}, u32[]{:S(2)}, u32[]{:S(2)}) collective-permute-start(f32[6,256]{1,0:T(8,128)S(1)} %shard_map.120.a_ref), channel_id=1, source_target_pairs={{0,1},{1,0},{2,3},{3,2},{4,7},{5,6},{6,5},{7,4},{8,9},{9,8},{10,11... | collective-permute-start | bytes 18440 | tf_op jit(solution)/shard_map/ppermute | solution.py:292
  24.5 1.5 %collective-permute-done.7.c_ref = f32[6,256]{1,0:T(8,128)S(1)} collective-permute-done((f32[6,256]{1,0:T(8,128)S(1)}, f32[6,256]{1,0:T(8,128)S(1)}, u32[]{:S(2)}, u32[]{:S(2)}) %collective-permute-start.7) | collective-permute-done | bytes 6176 | tf_op jit(solution)/shard_map/ppermute | solution.py:292
  26.5 6.8 %collective-permute-start.9 = (f32[8,256]{1,0:T(8,128)S(1)}, f32[8,256]{1,0:T(8,128)S(1)}, u32[]{:S(2)}, u32[]{:S(2)}) collective-permute-start(f32[8,256]{1,0:T(8,128)S(1)} %get-tuple-element.26.z_ref), channel_id=1, source_target_pairs={{4,8},{8,4},{12,16},{16,12},{20,24},{24,20},{28,32},{32,28},{36,40... | collective-permute-start | bytes 24584 | tf_op jit(solution)/shard_map/ppermute | solution.py:299
  33.4 1.2 %collective-permute-done.9.outer_ref = f32[8,256]{1,0:T(8,128)S(1)} collective-permute-done((f32[8,256]{1,0:T(8,128)S(1)}, f32[8,256]{1,0:T(8,128)S(1)}, u32[]{:S(2)}, u32[]{:S(2)}) %collective-permute-start.9) | collective-permute-done | bytes 8224 | tf_op jit(solution)/shard_map/ppermute | solution.py:299
  34.6 0.8 %shard_map.122 = (f32[6,256]{1,0:T(8,128)S(1)}, f32[8,256]{1,0:T(8,128)S(1)}) custom-call(f32[8,256]{1,0:T(8,128)S(1)} %get-tuple-element.26.z_ref, f32[8,256]{1,0:T(8,128)S(1)} %collective-permute-done.9.outer_ref, f32[8,256]{1,0:T(8,128)S(1)} %collective-permute-done.10.inner_ref, f32[6,6,127,256]{3,2,1,0:T(8,128)S(1)} %bitcast.10, f32[6,6,256]{2,1,0:T(8,128)S(1)} %copy-done.1), custom_call_target="tpu_custom_call" | custom-call | flops 2340864 | bytes 4681728 | tf_op jit(solution)/shard_map/pallas_call | solution.py:317
  35.5 2.5 %shard_map.124 = (f32[48,1024]{1,0:T(8,128)S(1)}, f32[48,1024]{1,0:T(8,128)S(1)}, f32[48,1024]{1,0:T(8,128)S(1)}, f32[48,1024]{1,0:T(8,128)S(1)}) custom-call(s32[1,8192]{1,0:T(1,128)S(1)} %get-tuple-element.19.ids_ref.pid_ref, s32[1,8192]{1,0:T(1,128)S(1)} %get-tuple-element.20.fid_ref, f32[2,24,8192]{2,1,0:T(8,128)S(1)} %get-tuple-element.22.jp_ref, ...), custom_call_target="tpu_custom_call" | custom-call | flops 1677721600 | bytes 2097152 | tf_op jit(solution)/shard_map/pallas_call | solution.py:317
  38.0 2.4 %collective-permute-start.12 = (f32[48,1024]{1,0:T(8,128)S(1)}, f32[48,1024]{1,0:T(8,128)S(1)}, u32[]{:S(2)}, u32[]{:S(2)}) collective-permute-start(f32[48,1024]{1,0:T(8,128)S(1)} %get-tuple-element.31), channel_id=1, source_target_pairs={{0,3},{1,2},{2,1},{3,0},{4,7},{5,6},{6,5},{7,4},{8,11},{9,10},{10,... | collective-permute-start | bytes 589832 | tf_op jit(solution)/shard_map/ppermute | solution.py:292
  40.3 0.8 %collective-permute-start.13 = (f32[48,1024]{1,0:T(8,128)S(1)}, f32[48,1024]{1,0:T(8,128)S(1)}, u32[]{:S(2)}, u32[]{:S(2)}) collective-permute-start(f32[48,1024]{1,0:T(8,128)S(1)} %get-tuple-element.32), channel_id=1, source_target_pairs={{0,2},{1,3},{2,0},{3,1},{4,6},{5,7},{6,4},{7,5},{8,10},{9,11},{10,... | collective-permute-start | bytes 589832 | tf_op jit(solution)/shard_map/ppermute | solution.py:292
  41.3 2.8 %collective-permute-start.11 = (f32[8,256]{1,0:T(8,128)S(1)}, f32[8,256]{1,0:T(8,128)S(1)}, u32[]{:S(2)}, u32[]{:S(2)}) collective-permute-start(f32[8,256]{1,0:T(8,128)S(1)} %get-tuple-element.27.u_ref), channel_id=1, source_target_pairs={{4,0},{8,4},{12,8},{16,12},{20,16},{24,20},{28,24},{32,28},{36,32}... | collective-permute-start | bytes 24584 | tf_op jit(solution)/shard_map/ppermute | solution.py:395
  44.1 3.3 %collective-permute-done.11.right_ref = f32[8,256]{1,0:T(8,128)S(1)} collective-permute-done((f32[8,256]{1,0:T(8,128)S(1)}, f32[8,256]{1,0:T(8,128)S(1)}, u32[]{:S(2)}, u32[]{:S(2)}) %collective-permute-start.11) | collective-permute-done | bytes 8224 | tf_op jit(solution)/shard_map/ppermute | solution.py:395
  47.4 1.3 %shard_map.123 = f32[32,128]{1,0:T(8,128)} custom-call(f32[8,256]{1,0:T(8,128)S(1)} %get-tuple-element.27.u_ref, f32[8,256]{1,0:T(8,128)S(1)} %collective-permute-done.11.right_ref, f32[6,6,127,256]{3,2,1,0:T(8,128)S(1)} %bitcast.11, f32[6,256]{1,0:T(8,128)S(1)} %get-tuple-element.28.r_ref, f32[8,256]{1,0:T(8,128)S(1)} %get-tuple-element.26.z_ref, ...), custom_call_target="tpu_custom_call" | custom-call | flops 1170432 | bytes 2340864 | tf_op jit(solution)/shard_map/pallas_call | solution.py:317
  48.7 9.7 %all-to-all-start = ((f32[32,1,128]{2,1,0:T(1,128)}), f32[32,1,128]{2,1,0:T(1,128)S(1)}, u32[]{:S(2)}, u32[]{:S(2)}) async-start(f32[32,1,128]{2,1,0:T(1,128)} %bitcast.5), calls=%async_computation | async-start | bytes 32768 | tf_op jit(solution)/shard_map/all_to_all | solution.py:411
  58.4 2.3 %shard_map.125 = (f32[24,1024]{1,0:T(8,128)S(1)}, f32[24,1024]{1,0:T(8,128)S(1)}) custom-call(f32[48,1024]{1,0:T(8,128)S(1)} %get-tuple-element.30.a_ref, f32[48,1024]{1,0:T(8,128)S(1)} %collective-permute-done.12.b_ref, f32[48,1024]{1,0:T(8,128)S(1)} %collective-permute-done.13.c_ref, f32[48,1024]{1,0:T(8,128)S(1)} %collective-permute-done.14.d_ref, ...), custom_call_target="tpu_custom_call" | custom-call | flops 2359296 | bytes 2359296 | tf_op jit(solution)/shard_map/pallas_call | solution.py:317
  60.8 4.5 %all-to-all-done = f32[32,1,128]{2,1,0:T(1,128)S(1)} async-done(((f32[32,1,128]{2,1,0:T(1,128)}), f32[32,1,128]{2,1,0:T(1,128)S(1)}, u32[]{:S(2)}, u32[]{:S(2)}) %all-to-all-start) | async-done | bytes 16416 | tf_op jit(solution)/shard_map/all_to_all | solution.py:411
  65.3 0.8 %shard_map.126 = (f32[6,256]{1,0:T(8,128)}, f32[24,1024]{1,0:T(8,128)}) custom-call(f32[32,128]{1,0:T(8,128)S(1)} %bitcast.12, f32[8,256]{1,0:T(8,128)S(1)} %get-tuple-element.26.z_ref, f32[8,256]{1,0:T(8,128)S(1)} %get-tuple-element.27.u_ref, f32[24,1024]{1,0:T(8,128)S(1)} %shard_map.116.rest_0_.ps_ref, f32[24,1024]{1,0:T(8,128)S(1)} %get-tuple-element.34.pz_ref, ...), custom_call_target="tpu_custom_call" | custom-call | flops 147456 | bytes 589824 | tf_op jit(solution)/shard_map/pallas_call | solution.py:317
  (28 shorter events, 1.4 us)
Async XLA Ops:
  0.6 11.6 %copy-start = (f32[24,24,1024]{2,1,0:T(8,128)S(1)}, f32[24,24,1024]{2,1,0:T(8,128)}, u32[]{:S(2)}) copy-start(f32[24,24,1024]{2,1,0:T(8,128)} %inv_hbm.1) | copy-start | bytes 7077892
  2.5 6.0 %collective-permute-start = (f32[24,1024]{1,0:T(8,128)S(1)}, f32[24,1024]{1,0:T(8,128)S(1)}, u32[]{:S(2)}, u32[]{:S(2)}) collective-permute-start(f32[24,1024]{1,0:T(8,128)S(1)} %get-tuple-element.23), channel_id=1, source_target_pairs={{0,2},{1,3},{2,0},{3,1},{4,6},{5,7},{6,4},{7,5},{8,10},{9,11},{10,... | collective-permute-start | bytes 294920 | tf_op jit(solution)/shard_map/ppermute | solution.py:292
  7.0 8.9 %copy-start.3 = (f32[2,6,8192]{2,0,1:T(2,128)S(1)}, f32[2,6,8192]{2,0,1:T(2,128)}, u32[]{:S(2)}) copy-start(f32[2,6,8192]{2,0,1:T(2,128)} %param.13) | copy-start | bytes 1179652
  7.0 4.8 %collective-permute-start.1 = (f32[24,1024]{1,0:T(8,128)S(1)}, f32[24,1024]{1,0:T(8,128)S(1)}, u32[]{:S(2)}, u32[]{:S(2)}) collective-permute-start(f32[24,1024]{1,0:T(8,128)S(1)} %get-tuple-element.24), channel_id=1, source_target_pairs={{0,1},{1,0},{2,3},{3,2},{4,7},{5,6},{6,5},{7,4},{8,9},{9,8},{10,11... | collective-permute-start | bytes 294920 | tf_op jit(solution)/shard_map/ppermute | solution.py:292
  7.9 4.3 %collective-permute-start.2 = (f32[24,1024]{1,0:T(8,128)S(1)}, f32[24,1024]{1,0:T(8,128)S(1)}, u32[]{:S(2)}, u32[]{:S(2)}) collective-permute-start(f32[24,1024]{1,0:T(8,128)S(1)} %get-tuple-element.25), channel_id=1, source_target_pairs={{0,3},{1,2},{2,1},{3,0},{4,5},{5,4},{6,7},{7,6},{8,11},{9,10},{10,... | collective-permute-start | bytes 294920 | tf_op jit(solution)/shard_map/ppermute | solution.py:292
  7.9 26.7 %slice-start = ((s8[4718592]{0:T(1024)(128)(4,1)}), s8[4194304]{0:T(1024)(128)(4,1)S(1)}, s32[]{:S(2)}) async-start(s8[4718592]{0:T(1024)(128)(4,1)} %bitcast.8), calls=%async_computation.1 | async-start | bytes 8388608
  12.5 4.3 %collective-permute-start.3 = (f32[24,1024]{1,0:T(8,128)S(1)}, f32[24,1024]{1,0:T(8,128)S(1)}, u32[]{:S(2)}, u32[]{:S(2)}) collective-permute-start(f32[24,1024]{1,0:T(8,128)S(1)} %shard_map.116.rest_0_.ps_ref), channel_id=1, source_target_pairs={{0,3},{1,2},{2,1},{3,0},{4,5},{5,4},{6,7},{7,6},{8,11},{9,10},{10,... | collective-permute-start | bytes 294920 | tf_op jit(solution)/shard_map/ppermute | solution.py:292
  13.0 4.7 %collective-permute-start.4 = (f32[24,1024]{1,0:T(8,128)S(1)}, f32[24,1024]{1,0:T(8,128)S(1)}, u32[]{:S(2)}, u32[]{:S(2)}) collective-permute-start(f32[24,1024]{1,0:T(8,128)S(1)} %shard_map.116.rest_0_.ps_ref), channel_id=1, source_target_pairs={{0,1},{1,0},{2,3},{3,2},{4,7},{5,6},{6,5},{7,4},{8,9},{9,8},{10,11... | collective-permute-start | bytes 294920 | tf_op jit(solution)/shard_map/ppermute | solution.py:292
  14.7 5.0 %collective-permute-start.5 = (f32[24,1024]{1,0:T(8,128)S(1)}, f32[24,1024]{1,0:T(8,128)S(1)}, u32[]{:S(2)}, u32[]{:S(2)}) collective-permute-start(f32[24,1024]{1,0:T(8,128)S(1)} %shard_map.116.rest_0_.ps_ref), channel_id=1, source_target_pairs={{0,2},{1,3},{2,0},{3,1},{4,6},{5,7},{6,4},{7,5},{8,10},{9,11},{10,... | collective-permute-start | bytes 294920 | tf_op jit(solution)/shard_map/ppermute | solution.py:292
  16.1 18.5 %slice-start.1 = ((s8[4718592]{0:T(1024)(128)(4,1)}), s8[524288]{0:T(1024)(128)(4,1)S(1)}, s32[]{:S(2)}) async-start(s8[4718592]{0:T(1024)(128)(4,1)} %bitcast.8), calls=%async_computation.2 | async-start | bytes 1048576
  17.6 8.9 %copy-start.1 = (f32[6,6,256]{2,1,0:T(8,128)S(1)}, f32[6,6,256]{2,1,0:T(8,128)}, u32[]{:S(2)}) copy-start(f32[6,6,256]{2,1,0:T(8,128)} %pre_ref.3) | copy-start | bytes 110596
  17.6 8.9 %copy-start.2 = (f32[256]{0:T(256)S(1)}, f32[256]{0:T(256)}, u32[]{:S(2)}) copy-start(f32[256]{0:T(256)} %param.18) | copy-start | bytes 3076
  20.4 4.1 %collective-permute-start.6 = (f32[6,256]{1,0:T(8,128)S(1)}, f32[6,256]{1,0:T(8,128)S(1)}, u32[]{:S(2)}, u32[]{:S(2)}) collective-permute-start(f32[6,256]{1,0:T(8,128)S(1)} %shard_map.120.a_ref), channel_id=1, source_target_pairs={{0,3},{1,2},{2,1},{3,0},{4,5},{5,4},{6,7},{7,6},{8,11},{9,10},{10,... | collective-permute-start | bytes 18440 | tf_op jit(solution)/shard_map/ppermute | solution.py:292
  22.1 4.0 %collective-permute-start.7 = (f32[6,256]{1,0:T(8,128)S(1)}, f32[6,256]{1,0:T(8,128)S(1)}, u32[]{:S(2)}, u32[]{:S(2)}) collective-permute-start(f32[6,256]{1,0:T(8,128)S(1)} %shard_map.120.a_ref), channel_id=1, source_target_pairs={{0,2},{1,3},{2,0},{3,1},{4,6},{5,7},{6,4},{7,5},{8,10},{9,11},{10,... | collective-permute-start | bytes 18440 | tf_op jit(solution)/shard_map/ppermute | solution.py:292
  22.7 3.7 %collective-permute-start.8 = (f32[6,256]{1,0:T(8,128)S(1)}, f32[6,256]{1,0:T(8,128)S(1)}, u32[]{:S(2)}, u32[]{:S(2)}) collective-permute-start(f32[6,256]{1,0:T(8,128)S(1)} %shard_map.120.a_ref), channel_id=1, source_target_pairs={{0,1},{1,0},{2,3},{3,2},{4,7},{5,6},{6,5},{7,4},{8,9},{9,8},{10,11... | collective-permute-start | bytes 18440 | tf_op jit(solution)/shard_map/ppermute | solution.py:292
  26.5 8.1 %collective-permute-start.9 = (f32[8,256]{1,0:T(8,128)S(1)}, f32[8,256]{1,0:T(8,128)S(1)}, u32[]{:S(2)}, u32[]{:S(2)}) collective-permute-start(f32[8,256]{1,0:T(8,128)S(1)} %get-tuple-element.26.z_ref), channel_id=1, source_target_pairs={{4,8},{8,4},{12,16},{16,12},{20,24},{24,20},{28,32},{32,28},{36,40... | collective-permute-start | bytes 24584 | tf_op jit(solution)/shard_map/ppermute | solution.py:299
  33.3 1.3 %collective-permute-start.10 = (f32[8,256]{1,0:T(8,128)S(1)}, f32[8,256]{1,0:T(8,128)S(1)}, u32[]{:S(2)}, u32[]{:S(2)}) collective-permute-start(f32[8,256]{1,0:T(8,128)S(1)} %get-tuple-element.26.z_ref), channel_id=1, source_target_pairs={{0,4},{4,0},{8,12},{12,8},{16,20},{20,16},{24,28},{28,24},{32,36},... | collective-permute-start | bytes 24584 | tf_op jit(solution)/shard_map/ppermute | solution.py:300
  38.0 20.4 %collective-permute-start.12 = (f32[48,1024]{1,0:T(8,128)S(1)}, f32[48,1024]{1,0:T(8,128)S(1)}, u32[]{:S(2)}, u32[]{:S(2)}) collective-permute-start(f32[48,1024]{1,0:T(8,128)S(1)} %get-tuple-element.31), channel_id=1, source_target_pairs={{0,3},{1,2},{2,1},{3,0},{4,7},{5,6},{6,5},{7,4},{8,11},{9,10},{10,... | collective-permute-start | bytes 589832 | tf_op jit(solution)/shard_map/ppermute | solution.py:292
  40.3 18.1 %collective-permute-start.13 = (f32[48,1024]{1,0:T(8,128)S(1)}, f32[48,1024]{1,0:T(8,128)S(1)}, u32[]{:S(2)}, u32[]{:S(2)}) collective-permute-start(f32[48,1024]{1,0:T(8,128)S(1)} %get-tuple-element.32), channel_id=1, source_target_pairs={{0,2},{1,3},{2,0},{3,1},{4,6},{5,7},{6,4},{7,5},{8,10},{9,11},{10,... | collective-permute-start | bytes 589832 | tf_op jit(solution)/shard_map/ppermute | solution.py:292
  41.1 17.3 %collective-permute-start.14 = (f32[48,1024]{1,0:T(8,128)S(1)}, f32[48,1024]{1,0:T(8,128)S(1)}, u32[]{:S(2)}, u32[]{:S(2)}) collective-permute-start(f32[48,1024]{1,0:T(8,128)S(1)} %get-tuple-element.33), channel_id=1, source_target_pairs={{0,1},{1,0},{2,3},{3,2},{4,5},{5,4},{6,7},{7,6},{8,9},{9,8},{10,11... | collective-permute-start | bytes 589832 | tf_op jit(solution)/shard_map/ppermute | solution.py:292
  41.3 6.1 %collective-permute-start.11 = (f32[8,256]{1,0:T(8,128)S(1)}, f32[8,256]{1,0:T(8,128)S(1)}, u32[]{:S(2)}, u32[]{:S(2)}) collective-permute-start(f32[8,256]{1,0:T(8,128)S(1)} %get-tuple-element.27.u_ref), channel_id=1, source_target_pairs={{4,0},{8,4},{12,8},{16,12},{20,16},{24,20},{28,24},{32,28},{36,32}... | collective-permute-start | bytes 24584 | tf_op jit(solution)/shard_map/ppermute | solution.py:395
  48.7 16.6 %all-to-all-start = ((f32[32,1,128]{2,1,0:T(1,128)}), f32[32,1,128]{2,1,0:T(1,128)S(1)}, u32[]{:S(2)}, u32[]{:S(2)}) async-start(f32[32,1,128]{2,1,0:T(1,128)} %bitcast.5), calls=%async_computation | async-start | bytes 32768 | tf_op jit(solution)/shard_map/all_to_all | solution.py:411

commit v6 on v5

--- a/solution.py
+++ b/solution.py
@@ -23,6 +23,7 @@
 SUM_TURNS = ((2, 2), (1, 3), (3, 1))
 SOLVED_TURNS = ((3, 1), (1, 3), (2, 2))
 CAMERA_TURNS = ((3, 1), (2, 2), (1, 3))
+BACK_TURNS = ((3, 1), (2, 2), (1, 3), (0, 0))
 SELF = ((0, 0),)
 LIMIT = pltpu.CompilerParams(vmem_limit_bytes=12 * 2**20)
 
@@ -249,7 +250,7 @@
 def back_kernel(pid_ref, fid_ref, jp_ref, jc_ref, z_ref, u_ref, *outs):
     parts = halves(jnp.concatenate([z_ref[...], u_ref[...]], axis=0))
     for j in range(GROUPS):
-        b = block_at((GROUPS - 1 - j,) * 2)
+        b = block_at(BACK_TURNS[j])
         at = lanes(b)
         table = one_hot(fid_ref[:, at].astype(F32), FR)
         got = lax.dot_general(parts, table, (((1,), (0,)), ((), ())), preferred_element_type=F32)
@@ -401,7 +402,7 @@
     )
     returned = [back[GROUPS - 1]]
     for s in (3, 2, 1):
-        returned.append(swapped(back[GROUPS - 1 - s], (s, s)))
+        returned.append(swapped(back[GROUPS - 1 - s], BACK_TURNS[GROUPS - 1 - s]))
     gram = plain(
         second_kernel,
         sds(count, 128),

time: 66.3 us -> 66 us (level)
  no operation moved by 1% of the time
where the time goes in v6:
time: 66 us; the launch traced here: 65.8 us
  starting transfers between devices  34.4 us (52%)
  waiting for transfers between devices  16.1 us (24%)
  Pallas kernels  14.2 us (22%)
  between operations  0.8 us (1%)
    ppermute x12, starting transfers between devices, swapped(): return lax.ppermute(value, ('frames', 'points'), pairs)  15.9 us
    pallas_call x14, Pallas kernels, plain(): pl.pallas_call(kernel, in_specs=specs, out_specs=out_specs, out_shape=out...  14.2 us
    all_to_all x1, starting transfers between devices, step(): lax.all_to_all(gram, 'frames', split_axis=0, concat_axis=0, tiled=True)  9.39 us
    ppermute x12, waiting for transfers between devices, swapped(): return lax.ppermute(value, ('frames', 'points'), pairs)  7.04 us
    ppermute x1, starting transfers between devices, beside(): far = lax.ppermute(value, 'frames', outer)  6.8 us
    all_to_all x1, waiting for transfers between devices, step(): lax.all_to_all(gram, 'frames', split_axis=0, concat_axis=0, tiled=True)  4.52 us
    ppermute x1, waiting for transfers between devices, step(): u_right = lax.ppermute(u, 'frames', [(i + 1, i) for i in range(count - 1)])  3.27 us
    ppermute x1, starting transfers between devices, step(): u_right = lax.ppermute(u, 'frames', [(i + 1, i) for i in range(count - 1)])  2.21 us
  transfers between devices with their start and end apart: 16, of which 9 were waited for; matrix products, arithmetic and copies ran while one was open for 0% of the time, Pallas kernels for 11%

profile of v6, /device:TPU:1, one launch (start us, length us, event | category | flops | bytes accessed | tf_op | source)
XLA Modules:
  0.0 65.8 jit_solution(14953745033025988245)
XLA Ops:
  0.6 1.8 %shard_map.113 = (f32[24,1024]{1,0:T(8,128)S(1)}, s32[1,8192]{1,0:T(1,128)S(1)}, s32[1,8192]{1,0:T(1,128)S(1)}, f32[2,8192]{1,0:T(2,128)S(1)}, f32[2,24,8192]{2,1,0:T(8,128)S(1)}) custom-call(s32[4]{0:T(128)} %count_hbm.1, s32[1,8192]{1,0:T(1,128)} %bitcast.14, s32[1,8192]{1,0:T(1,128)} %bitcast.15, f32[2,8192]{1,0:T(2,128)} %res_hbm.1, f32[2,24,8192]{2,1,0:T(8,128)} %jp_hbm.1), custom_call_target="tpu_custom_call" | custom-call | flops 201326592 | bytes 1572864 | tf_op jit(solution)/shard_map/pallas_call | solution.py:318
  2.5 3.6 %collective-permute-start = (f32[24,1024]{1,0:T(8,128)S(1)}, f32[24,1024]{1,0:T(8,128)S(1)}, u32[]{:S(2)}, u32[]{:S(2)}) collective-permute-start(f32[24,1024]{1,0:T(8,128)S(1)} %get-tuple-element.23), channel_id=1, source_target_pairs={{0,2},{1,3},{2,0},{3,1},{4,6},{5,7},{6,4},{7,5},{8,10},{9,11},{10,... | collective-permute-start | bytes 294920 | tf_op jit(solution)/shard_map/ppermute | solution.py:293
  6.1 0.9 %shard_map.114 = (f32[24,1024]{1,0:T(8,128)S(1)}, f32[24,1024]{1,0:T(8,128)S(1)}) custom-call(s32[1,8192]{1,0:T(1,128)S(1)} %get-tuple-element.19.ids_ref.pid_ref, f32[2,8192]{1,0:T(2,128)S(1)} %get-tuple-element.21.res_ref, f32[2,24,8192]{2,1,0:T(8,128)S(1)} %get-tuple-element.22.jp_ref), custom_call_target="tpu_custom_call" | custom-call | flops 402653184 | bytes 786432 | tf_op jit(solution)/shard_map/pallas_call | solution.py:318
  7.0 0.9 %collective-permute-start.1 = (f32[24,1024]{1,0:T(8,128)S(1)}, f32[24,1024]{1,0:T(8,128)S(1)}, u32[]{:S(2)}, u32[]{:S(2)}) collective-permute-start(f32[24,1024]{1,0:T(8,128)S(1)} %get-tuple-element.24), channel_id=1, source_target_pairs={{0,1},{1,0},{2,3},{3,2},{4,7},{5,6},{6,5},{7,4},{8,9},{9,8},{10,11... | collective-permute-start | bytes 294920 | tf_op jit(solution)/shard_map/ppermute | solution.py:293
  7.9 0.5 shard_map.115.d_ref
  8.5 3.3 %collective-permute-done.1.b_ref = f32[24,1024]{1,0:T(8,128)S(1)} collective-permute-done((f32[24,1024]{1,0:T(8,128)S(1)}, f32[24,1024]{1,0:T(8,128)S(1)}, u32[]{:S(2)}, u32[]{:S(2)}) %collective-permute-start.1) | collective-permute-done | bytes 98336 | tf_op jit(solution)/shard_map/ppermute | solution.py:293
  11.7 0.4 collective-permute-done.2.c_ref
  12.5 0.5 collective-permute-start.3
  13.0 1.6 %collective-permute-start.4 = (f32[24,1024]{1,0:T(8,128)S(1)}, f32[24,1024]{1,0:T(8,128)S(1)}, u32[]{:S(2)}, u32[]{:S(2)}) collective-permute-start(f32[24,1024]{1,0:T(8,128)S(1)} %shard_map.116.rest_0_.ps_ref), channel_id=1, source_target_pairs={{0,1},{1,0},{2,3},{3,2},{4,7},{5,6},{6,5},{7,4},{8,9},{9,8},{10,11... | collective-permute-start | bytes 294920 | tf_op jit(solution)/shard_map/ppermute | solution.py:293
  14.7 1.2 %collective-permute-start.5 = (f32[24,1024]{1,0:T(8,128)S(1)}, f32[24,1024]{1,0:T(8,128)S(1)}, u32[]{:S(2)}, u32[]{:S(2)}) collective-permute-start(f32[24,1024]{1,0:T(8,128)S(1)} %shard_map.116.rest_0_.ps_ref), channel_id=1, source_target_pairs={{0,2},{1,3},{2,0},{3,1},{4,6},{5,7},{6,4},{7,5},{8,10},{9,11},{10,... | collective-permute-start | bytes 294920 | tf_op jit(solution)/shard_map/ppermute | solution.py:293
  16.1 0.7 %shard_map.117.rest_0_ = f32[6,256]{1,0:T(8,128)S(1)} custom-call(s32[1,8192]{1,0:T(1,128)S(1)} %get-tuple-element.19.ids_ref.pid_ref, s32[1,8192]{1,0:T(1,128)S(1)} %get-tuple-element.20.fid_ref, f32[2,8192]{1,0:T(2,128)S(1)} %get-tuple-element.21.res_ref, f32[2,24,8192]{2,1,0:T(8,128)S(1)} %get-tuple-element.22.jp_ref, f32[2,6,8192]{2,1,0:T(8,128)S(1)} %copy.20.jc_ref, ...), custom_call_target="tpu_custom_call" | custom-call | flops 268435456 | bytes 524288 | tf_op jit(solution)/shard_map/pallas_call | solution.py:318
  16.8 0.8 %shard_map.118.rest_0_ = f32[6,256]{1,0:T(8,128)S(1)} custom-call(s32[1,8192]{1,0:T(1,128)S(1)} %get-tuple-element.19.ids_ref.pid_ref, s32[1,8192]{1,0:T(1,128)S(1)} %get-tuple-element.20.fid_ref, f32[2,8192]{1,0:T(2,128)S(1)} %get-tuple-element.21.res_ref, f32[2,24,8192]{2,1,0:T(8,128)S(1)} %get-tuple-element.22.jp_ref, f32[2,6,8192]{2,1,0:T(8,128)S(1)} %copy.20.jc_ref, ...), custom_call_target="tpu_custom_call" | custom-call | flops 268435456 | bytes 524288 | tf_op jit(solution)/shard_map/pallas_call | solution.py:318
  17.7 0.7 %shard_map.119.rest_0_ = f32[6,256]{1,0:T(8,128)S(1)} custom-call(s32[1,8192]{1,0:T(1,128)S(1)} %get-tuple-element.19.ids_ref.pid_ref, s32[1,8192]{1,0:T(1,128)S(1)} %get-tuple-element.20.fid_ref, f32[2,8192]{1,0:T(2,128)S(1)} %get-tuple-element.21.res_ref, f32[2,24,8192]{2,1,0:T(8,128)S(1)} %get-tuple-element.22.jp_ref, f32[2,6,8192]{2,1,0:T(8,128)S(1)} %copy.20.jc_ref, ...), custom_call_target="tpu_custom_call" | custom-call | flops 268435456 | bytes 524288 | tf_op jit(solution)/shard_map/pallas_call | solution.py:318
  18.4 1.3 %collective-permute-done.5.rest_1_ = f32[24,1024]{1,0:T(8,128)S(1)} collective-permute-done((f32[24,1024]{1,0:T(8,128)S(1)}, f32[24,1024]{1,0:T(8,128)S(1)}, u32[]{:S(2)}, u32[]{:S(2)}) %collective-permute-start.5) | collective-permute-done | bytes 98336 | tf_op jit(solution)/shard_map/ppermute | solution.py:293
  19.7 0.7 %shard_map.120.a_ref = f32[6,256]{1,0:T(8,128)S(1)} custom-call(s32[1,8192]{1,0:T(1,128)S(1)} %get-tuple-element.19.ids_ref.pid_ref, s32[1,8192]{1,0:T(1,128)S(1)} %get-tuple-element.20.fid_ref, f32[2,8192]{1,0:T(2,128)S(1)} %get-tuple-element.21.res_ref, f32[2,24,8192]{2,1,0:T(8,128)S(1)} %get-tuple-element.22.jp_ref, f32[2,6,8192]{2,1,0:T(8,128)S(1)} %copy.20.jc_ref, ...), custom_call_target="tpu_custom_call" | custom-call | flops 268435456 | bytes 524288 | tf_op jit(solution)/shard_map/pallas_call | solution.py:318
  20.4 1.6 %collective-permute-start.6 = (f32[6,256]{1,0:T(8,128)S(1)}, f32[6,256]{1,0:T(8,128)S(1)}, u32[]{:S(2)}, u32[]{:S(2)}) collective-permute-start(f32[6,256]{1,0:T(8,128)S(1)} %shard_map.120.a_ref), channel_id=1, source_target_pairs={{0,3},{1,2},{2,1},{3,0},{4,5},{5,4},{6,7},{7,6},{8,11},{9,10},{10,... | collective-permute-start | bytes 18440 | tf_op jit(solution)/shard_map/ppermute | solution.py:293
  22.1 0.7 %collective-permute-start.7 = (f32[6,256]{1,0:T(8,128)S(1)}, f32[6,256]{1,0:T(8,128)S(1)}, u32[]{:S(2)}, u32[]{:S(2)}) collective-permute-start(f32[6,256]{1,0:T(8,128)S(1)} %shard_map.120.a_ref), channel_id=1, source_target_pairs={{0,2},{1,3},{2,0},{3,1},{4,6},{5,7},{6,4},{7,5},{8,10},{9,11},{10,... | collective-permute-start | bytes 18440 | tf_op jit(solution)/shard_map/ppermute | solution.py:293
  22.7 1.8 %collective-permute-start.8 = (f32[6,256]{1,0:T(8,128)S(1)}, f32[6,256]{1,0:T(8,128)S(1)}, u32[]{:S(2)}, u32[]{:S(2)}) collective-permute-start(f32[6,256]{1,0:T(8,128)S(1)} %shard_map.120.a_ref), channel_id=1, source_target_pairs={{0,1},{1,0},{2,3},{3,2},{4,7},{5,6},{6,5},{7,4},{8,9},{9,8},{10,11... | collective-permute-start | bytes 18440 | tf_op jit(solution)/shard_map/ppermute | solution.py:293
  24.5 1.5 %collective-permute-done.7.c_ref = f32[6,256]{1,0:T(8,128)S(1)} collective-permute-done((f32[6,256]{1,0:T(8,128)S(1)}, f32[6,256]{1,0:T(8,128)S(1)}, u32[]{:S(2)}, u32[]{:S(2)}) %collective-permute-start.7) | collective-permute-done | bytes 6176 | tf_op jit(solution)/shard_map/ppermute | solution.py:293
  26.5 6.8 %collective-permute-start.9 = (f32[8,256]{1,0:T(8,128)S(1)}, f32[8,256]{1,0:T(8,128)S(1)}, u32[]{:S(2)}, u32[]{:S(2)}) collective-permute-start(f32[8,256]{1,0:T(8,128)S(1)} %get-tuple-element.26.z_ref), channel_id=1, source_target_pairs={{4,8},{8,4},{12,16},{16,12},{20,24},{24,20},{28,32},{32,28},{36,40... | collective-permute-start | bytes 24584 | tf_op jit(solution)/shard_map/ppermute | solution.py:300
  33.4 1.2 %collective-permute-done.9.outer_ref = f32[8,256]{1,0:T(8,128)S(1)} collective-permute-done((f32[8,256]{1,0:T(8,128)S(1)}, f32[8,256]{1,0:T(8,128)S(1)}, u32[]{:S(2)}, u32[]{:S(2)}) %collective-permute-start.9) | collective-permute-done | bytes 8224 | tf_op jit(solution)/shard_map/ppermute | solution.py:300
  34.6 0.8 %shard_map.122 = (f32[6,256]{1,0:T(8,128)S(1)}, f32[8,256]{1,0:T(8,128)S(1)}) custom-call(f32[8,256]{1,0:T(8,128)S(1)} %get-tuple-element.26.z_ref, f32[8,256]{1,0:T(8,128)S(1)} %collective-permute-done.9.outer_ref, f32[8,256]{1,0:T(8,128)S(1)} %collective-permute-done.10.inner_ref, f32[6,6,127,256]{3,2,1,0:T(8,128)S(1)} %bitcast.10, f32[6,6,256]{2,1,0:T(8,128)S(1)} %copy-done.1), custom_call_target="tpu_custom_call" | custom-call | flops 2340864 | bytes 4681728 | tf_op jit(solution)/shard_map/pallas_call | solution.py:318
  35.5 2.5 %shard_map.124 = (f32[48,1024]{1,0:T(8,128)S(1)}, f32[48,1024]{1,0:T(8,128)S(1)}, f32[48,1024]{1,0:T(8,128)S(1)}, f32[48,1024]{1,0:T(8,128)S(1)}) custom-call(s32[1,8192]{1,0:T(1,128)S(1)} %get-tuple-element.19.ids_ref.pid_ref, s32[1,8192]{1,0:T(1,128)S(1)} %get-tuple-element.20.fid_ref, f32[2,24,8192]{2,1,0:T(8,128)S(1)} %get-tuple-element.22.jp_ref, ...), custom_call_target="tpu_custom_call" | custom-call | flops 1677721600 | bytes 2097152 | tf_op jit(solution)/shard_map/pallas_call | solution.py:318
  38.0 1.3 %collective-permute-start.12 = (f32[48,1024]{1,0:T(8,128)S(1)}, f32[48,1024]{1,0:T(8,128)S(1)}, u32[]{:S(2)}, u32[]{:S(2)}) collective-permute-start(f32[48,1024]{1,0:T(8,128)S(1)} %get-tuple-element.31), channel_id=1, source_target_pairs={{0,3},{1,2},{2,1},{3,0},{4,5},{5,4},{6,7},{7,6},{8,11},{9,10},{10,... | collective-permute-start | bytes 589832 | tf_op jit(solution)/shard_map/ppermute | solution.py:293
  39.3 2.2 %collective-permute-start.13 = (f32[48,1024]{1,0:T(8,128)S(1)}, f32[48,1024]{1,0:T(8,128)S(1)}, u32[]{:S(2)}, u32[]{:S(2)}) collective-permute-start(f32[48,1024]{1,0:T(8,128)S(1)} %get-tuple-element.32), channel_id=1, source_target_pairs={{0,2},{1,3},{2,0},{3,1},{4,6},{5,7},{6,4},{7,5},{8,10},{9,11},{10,... | collective-permute-start | bytes 589832 | tf_op jit(solution)/shard_map/ppermute | solution.py:293
  41.9 2.2 %collective-permute-start.11 = (f32[8,256]{1,0:T(8,128)S(1)}, f32[8,256]{1,0:T(8,128)S(1)}, u32[]{:S(2)}, u32[]{:S(2)}) collective-permute-start(f32[8,256]{1,0:T(8,128)S(1)} %get-tuple-element.27.u_ref), channel_id=1, source_target_pairs={{4,0},{8,4},{12,8},{16,12},{20,16},{24,20},{28,24},{32,28},{36,32}... | collective-permute-start | bytes 24584 | tf_op jit(solution)/shard_map/ppermute | solution.py:396
  44.1 3.3 %collective-permute-done.11.right_ref = f32[8,256]{1,0:T(8,128)S(1)} collective-permute-done((f32[8,256]{1,0:T(8,128)S(1)}, f32[8,256]{1,0:T(8,128)S(1)}, u32[]{:S(2)}, u32[]{:S(2)}) %collective-permute-start.11) | collective-permute-done | bytes 8224 | tf_op jit(solution)/shard_map/ppermute | solution.py:396
  47.4 1.3 %shard_map.123 = f32[32,128]{1,0:T(8,128)} custom-call(f32[8,256]{1,0:T(8,128)S(1)} %get-tuple-element.27.u_ref, f32[8,256]{1,0:T(8,128)S(1)} %collective-permute-done.11.right_ref, f32[6,6,127,256]{3,2,1,0:T(8,128)S(1)} %bitcast.11, f32[6,256]{1,0:T(8,128)S(1)} %get-tuple-element.28.r_ref, f32[8,256]{1,0:T(8,128)S(1)} %get-tuple-element.26.z_ref, ...), custom_call_target="tpu_custom_call" | custom-call | flops 1170432 | bytes 2340864 | tf_op jit(solution)/shard_map/pallas_call | solution.py:318
  48.7 9.4 %all-to-all-start = ((f32[32,1,128]{2,1,0:T(1,128)}), f32[32,1,128]{2,1,0:T(1,128)S(1)}, u32[]{:S(2)}, u32[]{:S(2)}) async-start(f32[32,1,128]{2,1,0:T(1,128)} %bitcast.5), calls=%async_computation | async-start | bytes 32768 | tf_op jit(solution)/shard_map/all_to_all | solution.py:412
  58.2 2.3 %shard_map.125 = (f32[24,1024]{1,0:T(8,128)S(1)}, f32[24,1024]{1,0:T(8,128)S(1)}) custom-call(f32[48,1024]{1,0:T(8,128)S(1)} %get-tuple-element.30.a_ref, f32[48,1024]{1,0:T(8,128)S(1)} %collective-permute-done.12.b_ref, f32[48,1024]{1,0:T(8,128)S(1)} %collective-permute-done.13.c_ref, f32[48,1024]{1,0:T(8,128)S(1)} %collective-permute-done.14.d_ref, ...), custom_call_target="tpu_custom_call" | custom-call | flops 2359296 | bytes 2359296 | tf_op jit(solution)/shard_map/pallas_call | solution.py:318
  60.5 4.5 %all-to-all-done = f32[32,1,128]{2,1,0:T(1,128)S(1)} async-done(((f32[32,1,128]{2,1,0:T(1,128)}), f32[32,1,128]{2,1,0:T(1,128)S(1)}, u32[]{:S(2)}, u32[]{:S(2)}) %all-to-all-start) | async-done | bytes 16416 | tf_op jit(solution)/shard_map/all_to_all | solution.py:412
  65.0 0.8 %shard_map.126 = (f32[6,256]{1,0:T(8,128)}, f32[24,1024]{1,0:T(8,128)}) custom-call(f32[32,128]{1,0:T(8,128)S(1)} %bitcast.12, f32[8,256]{1,0:T(8,128)S(1)} %get-tuple-element.26.z_ref, f32[8,256]{1,0:T(8,128)S(1)} %get-tuple-element.27.u_ref, f32[24,1024]{1,0:T(8,128)S(1)} %shard_map.116.rest_0_.ps_ref, f32[24,1024]{1,0:T(8,128)S(1)} %get-tuple-element.34.pz_ref, ...), custom_call_target="tpu_custom_call" | custom-call | flops 147456 | bytes 589824 | tf_op jit(solution)/shard_map/pallas_call | solution.py:318
  (28 shorter events, 1.6 us)
Async XLA Ops:
  0.6 11.6 %copy-start = (f32[24,24,1024]{2,1,0:T(8,128)S(1)}, f32[24,24,1024]{2,1,0:T(8,128)}, u32[]{:S(2)}) copy-start(f32[24,24,1024]{2,1,0:T(8,128)} %inv_hbm.1) | copy-start | bytes 7077892
  2.5 6.0 %collective-permute-start = (f32[24,1024]{1,0:T(8,128)S(1)}, f32[24,1024]{1,0:T(8,128)S(1)}, u32[]{:S(2)}, u32[]{:S(2)}) collective-permute-start(f32[24,1024]{1,0:T(8,128)S(1)} %get-tuple-element.23), channel_id=1, source_target_pairs={{0,2},{1,3},{2,0},{3,1},{4,6},{5,7},{6,4},{7,5},{8,10},{9,11},{10,... | collective-permute-start | bytes 294920 | tf_op jit(solution)/shard_map/ppermute | solution.py:293
  7.0 8.9 %copy-start.3 = (f32[2,6,8192]{2,0,1:T(2,128)S(1)}, f32[2,6,8192]{2,0,1:T(2,128)}, u32[]{:S(2)}) copy-start(f32[2,6,8192]{2,0,1:T(2,128)} %param.13) | copy-start | bytes 1179652
  7.0 4.8 %collective-permute-start.1 = (f32[24,1024]{1,0:T(8,128)S(1)}, f32[24,1024]{1,0:T(8,128)S(1)}, u32[]{:S(2)}, u32[]{:S(2)}) collective-permute-start(f32[24,1024]{1,0:T(8,128)S(1)} %get-tuple-element.24), channel_id=1, source_target_pairs={{0,1},{1,0},{2,3},{3,2},{4,7},{5,6},{6,5},{7,4},{8,9},{9,8},{10,11... | collective-permute-start | bytes 294920 | tf_op jit(solution)/shard_map/ppermute | solution.py:293
  7.9 4.3 %collective-permute-start.2 = (f32[24,1024]{1,0:T(8,128)S(1)}, f32[24,1024]{1,0:T(8,128)S(1)}, u32[]{:S(2)}, u32[]{:S(2)}) collective-permute-start(f32[24,1024]{1,0:T(8,128)S(1)} %get-tuple-element.25), channel_id=1, source_target_pairs={{0,3},{1,2},{2,1},{3,0},{4,5},{5,4},{6,7},{7,6},{8,11},{9,10},{10,... | collective-permute-start | bytes 294920 | tf_op jit(solution)/shard_map/ppermute | solution.py:293
  7.9 26.7 %slice-start = ((s8[4718592]{0:T(1024)(128)(4,1)}), s8[4194304]{0:T(1024)(128)(4,1)S(1)}, s32[]{:S(2)}) async-start(s8[4718592]{0:T(1024)(128)(4,1)} %bitcast.8), calls=%async_computation.1 | async-start | bytes 8388608
  12.5 4.3 %collective-permute-start.3 = (f32[24,1024]{1,0:T(8,128)S(1)}, f32[24,1024]{1,0:T(8,128)S(1)}, u32[]{:S(2)}, u32[]{:S(2)}) collective-permute-start(f32[24,1024]{1,0:T(8,128)S(1)} %shard_map.116.rest_0_.ps_ref), channel_id=1, source_target_pairs={{0,3},{1,2},{2,1},{3,0},{4,5},{5,4},{6,7},{7,6},{8,11},{9,10},{10,... | collective-permute-start | bytes 294920 | tf_op jit(solution)/shard_map/ppermute | solution.py:293
  13.0 4.7 %collective-permute-start.4 = (f32[24,1024]{1,0:T(8,128)S(1)}, f32[24,1024]{1,0:T(8,128)S(1)}, u32[]{:S(2)}, u32[]{:S(2)}) collective-permute-start(f32[24,1024]{1,0:T(8,128)S(1)} %shard_map.116.rest_0_.ps_ref), channel_id=1, source_target_pairs={{0,1},{1,0},{2,3},{3,2},{4,7},{5,6},{6,5},{7,4},{8,9},{9,8},{10,11... | collective-permute-start | bytes 294920 | tf_op jit(solution)/shard_map/ppermute | solution.py:293
  14.7 5.0 %collective-permute-start.5 = (f32[24,1024]{1,0:T(8,128)S(1)}, f32[24,1024]{1,0:T(8,128)S(1)}, u32[]{:S(2)}, u32[]{:S(2)}) collective-permute-start(f32[24,1024]{1,0:T(8,128)S(1)} %shard_map.116.rest_0_.ps_ref), channel_id=1, source_target_pairs={{0,2},{1,3},{2,0},{3,1},{4,6},{5,7},{6,4},{7,5},{8,10},{9,11},{10,... | collective-permute-start | bytes 294920 | tf_op jit(solution)/shard_map/ppermute | solution.py:293
  16.1 18.5 %slice-start.1 = ((s8[4718592]{0:T(1024)(128)(4,1)}), s8[524288]{0:T(1024)(128)(4,1)S(1)}, s32[]{:S(2)}) async-start(s8[4718592]{0:T(1024)(128)(4,1)} %bitcast.8), calls=%async_computation.2 | async-start | bytes 1048576
  17.6 8.9 %copy-start.1 = (f32[6,6,256]{2,1,0:T(8,128)S(1)}, f32[6,6,256]{2,1,0:T(8,128)}, u32[]{:S(2)}) copy-start(f32[6,6,256]{2,1,0:T(8,128)} %pre_ref.3) | copy-start | bytes 110596
  17.6 8.9 %copy-start.2 = (f32[256]{0:T(256)S(1)}, f32[256]{0:T(256)}, u32[]{:S(2)}) copy-start(f32[256]{0:T(256)} %param.18) | copy-start | bytes 3076
  20.4 4.1 %collective-permute-start.6 = (f32[6,256]{1,0:T(8,128)S(1)}, f32[6,256]{1,0:T(8,128)S(1)}, u32[]{:S(2)}, u32[]{:S(2)}) collective-permute-start(f32[6,256]{1,0:T(8,128)S(1)} %shard_map.120.a_ref), channel_id=1, source_target_pairs={{0,3},{1,2},{2,1},{3,0},{4,5},{5,4},{6,7},{7,6},{8,11},{9,10},{10,... | collective-permute-start | bytes 18440 | tf_op jit(solution)/shard_map/ppermute | solution.py:293
  22.1 4.0 %collective-permute-start.7 = (f32[6,256]{1,0:T(8,128)S(1)}, f32[6,256]{1,0:T(8,128)S(1)}, u32[]{:S(2)}, u32[]{:S(2)}) collective-permute-start(f32[6,256]{1,0:T(8,128)S(1)} %shard_map.120.a_ref), channel_id=1, source_target_pairs={{0,2},{1,3},{2,0},{3,1},{4,6},{5,7},{6,4},{7,5},{8,10},{9,11},{10,... | collective-permute-start | bytes 18440 | tf_op jit(solution)/shard_map/ppermute | solution.py:293
  22.7 3.7 %collective-permute-start.8 = (f32[6,256]{1,0:T(8,128)S(1)}, f32[6,256]{1,0:T(8,128)S(1)}, u32[]{:S(2)}, u32[]{:S(2)}) collective-permute-start(f32[6,256]{1,0:T(8,128)S(1)} %shard_map.120.a_ref), channel_id=1, source_target_pairs={{0,1},{1,0},{2,3},{3,2},{4,7},{5,6},{6,5},{7,4},{8,9},{9,8},{10,11... | collective-permute-start | bytes 18440 | tf_op jit(solution)/shard_map/ppermute | solution.py:293
  26.5 8.1 %collective-permute-start.9 = (f32[8,256]{1,0:T(8,128)S(1)}, f32[8,256]{1,0:T(8,128)S(1)}, u32[]{:S(2)}, u32[]{:S(2)}) collective-permute-start(f32[8,256]{1,0:T(8,128)S(1)} %get-tuple-element.26.z_ref), channel_id=1, source_target_pairs={{4,8},{8,4},{12,16},{16,12},{20,24},{24,20},{28,32},{32,28},{36,40... | collective-permute-start | bytes 24584 | tf_op jit(solution)/shard_map/ppermute | solution.py:300
  33.3 1.3 %collective-permute-start.10 = (f32[8,256]{1,0:T(8,128)S(1)}, f32[8,256]{1,0:T(8,128)S(1)}, u32[]{:S(2)}, u32[]{:S(2)}) collective-permute-start(f32[8,256]{1,0:T(8,128)S(1)} %get-tuple-element.26.z_ref), channel_id=1, source_target_pairs={{0,4},{4,0},{8,12},{12,8},{16,20},{20,16},{24,28},{28,24},{32,36},... | collective-permute-start | bytes 24584 | tf_op jit(solution)/shard_map/ppermute | solution.py:301
  38.0 20.1 %collective-permute-start.12 = (f32[48,1024]{1,0:T(8,128)S(1)}, f32[48,1024]{1,0:T(8,128)S(1)}, u32[]{:S(2)}, u32[]{:S(2)}) collective-permute-start(f32[48,1024]{1,0:T(8,128)S(1)} %get-tuple-element.31), channel_id=1, source_target_pairs={{0,3},{1,2},{2,1},{3,0},{4,5},{5,4},{6,7},{7,6},{8,11},{9,10},{10,... | collective-permute-start | bytes 589832 | tf_op jit(solution)/shard_map/ppermute | solution.py:293
  39.3 18.8 %collective-permute-start.13 = (f32[48,1024]{1,0:T(8,128)S(1)}, f32[48,1024]{1,0:T(8,128)S(1)}, u32[]{:S(2)}, u32[]{:S(2)}) collective-permute-start(f32[48,1024]{1,0:T(8,128)S(1)} %get-tuple-element.32), channel_id=1, source_target_pairs={{0,2},{1,3},{2,0},{3,1},{4,6},{5,7},{6,4},{7,5},{8,10},{9,11},{10,... | collective-permute-start | bytes 589832 | tf_op jit(solution)/shard_map/ppermute | solution.py:293
  41.5 16.6 %collective-permute-start.14 = (f32[48,1024]{1,0:T(8,128)S(1)}, f32[48,1024]{1,0:T(8,128)S(1)}, u32[]{:S(2)}, u32[]{:S(2)}) collective-permute-start(f32[48,1024]{1,0:T(8,128)S(1)} %get-tuple-element.33), channel_id=1, source_target_pairs={{0,1},{1,0},{2,3},{3,2},{4,7},{5,6},{6,5},{7,4},{8,9},{9,8},{10,11... | collective-permute-start | bytes 589832 | tf_op jit(solution)/shard_map/ppermute | solution.py:293
  41.9 5.5 %collective-permute-start.11 = (f32[8,256]{1,0:T(8,128)S(1)}, f32[8,256]{1,0:T(8,128)S(1)}, u32[]{:S(2)}, u32[]{:S(2)}) collective-permute-start(f32[8,256]{1,0:T(8,128)S(1)} %get-tuple-element.27.u_ref), channel_id=1, source_target_pairs={{4,0},{8,4},{12,8},{16,12},{20,16},{24,20},{28,24},{32,28},{36,32}... | collective-permute-start | bytes 24584 | tf_op jit(solution)/shard_map/ppermute | solution.py:396
  48.7 16.3 %all-to-all-start = ((f32[32,1,128]{2,1,0:T(1,128)}), f32[32,1,128]{2,1,0:T(1,128)S(1)}, u32[]{:S(2)}, u32[]{:S(2)}) async-start(f32[32,1,128]{2,1,0:T(1,128)} %bitcast.5), calls=%async_computation | async-start | bytes 32768 | tf_op jit(solution)/shard_map/all_to_all | solution.py:412
